TPU v7x, 32 devices: a whole 2x2x4 slice. The times are simulated.
32 devices in a mesh: fsdp: 8 (over z, y), tp: 4 (over x, core).
Axes of the slice: x: 2, y: 2, z: 4, core: 2. Of those that a mesh axis runs over, the one named last changes fastest.
Arguments:
- inputs: bfloat16 [16384, 1024], P(('fsdp', 'tp')), may hold values from -6 to 6
- doc_lengths: int32 [16, 4], P('fsdp'), may hold values from 1 to 512, 1024 in all within a row
- first_gain: float32 [1024], replicated, may hold values from 0.1 to 1.9
- first_bias: float32 [1024], replicated, may hold values from -3 to 3
- w_query: bfloat16 [1024, 1024], P('fsdp', 'tp'), may hold values from -0.25 to 0.25
- b_query: float32 [1024], P('tp'), may hold values from -3 to 3
- w_key: bfloat16 [1024, 1024], P('fsdp', 'tp'), may hold values from -0.25 to 0.25
- w_value: bfloat16 [1024, 1024], P('fsdp', 'tp'), may hold values from -0.1875 to 0.1875
- b_value: float32 [1024], P('tp'), may hold values from -3 to 3
- w_out: bfloat16 [1024, 1024], P('tp', 'fsdp'), may hold values from -0.75 to 0.75
- b_out: float32 [1024], replicated, may hold values from -3 to 3
- second_gain: float32 [1024], replicated, may hold values from 0.1 to 1.9
- second_bias: float32 [1024], replicated, may hold values from -3 to 3
- w_up: bfloat16 [1024, 4096], P('fsdp', 'tp'), may hold values from -0.1875 to 0.1875
- b_up: float32 [4096], P('tp'), may hold values from -3 to 3
- w_down: bfloat16 [4096, 1024], P('tp', 'fsdp'), may hold values from -0.09375 to 0.09375
- b_down: float32 [1024], replicated, may hold values from -3 to 3
- cotangent: float32 [16384, 1024], P(('fsdp', 'tp')), may hold values from -6 to 6
Outputs:
- layer_out: bfloat16 [16384, 1024], P(('fsdp', 'tp'))
- input_grad: float32 [16384, 1024], P(('fsdp', 'tp'))
- grad_first_gain: float32 [1024], replicated
- grad_first_bias: float32 [1024], replicated
- grad_w_query: float32 [1024, 1024], P('fsdp', 'tp')
- grad_b_query: float32 [1024], P('tp')
- grad_w_key: float32 [1024, 1024], P('fsdp', 'tp')
- grad_w_value: float32 [1024, 1024], P('fsdp', 'tp')
- grad_b_value: float32 [1024], P('tp')
- grad_w_out: float32 [1024, 1024], P('tp', 'fsdp')
- grad_b_out: float32 [1024], replicated
- grad_second_gain: float32 [1024], replicated
- grad_second_bias: float32 [1024], replicated
- grad_w_up: float32 [1024, 4096], P('fsdp', 'tp')
- grad_b_up: float32 [4096], P('tp')
- grad_w_down: float32 [4096, 1024], P('tp', 'fsdp')
- grad_b_down: float32 [1024], replicated
Inputs may be any that keep to these rules, and one draw needn't show every extreme that they name: `doc_lengths`: each row holds the lengths of the 4 documents of one sequence, in order, summing to 1024; the longest document of every row has 512 tokens.
All inputs are finite; a program needn't handle non-finite values.
Results may differ from a plain program's by a relative error of at most 0.018.
Values may be sent and summed in bfloat16 or wider, within the bound.
No kernel may reach another device: no remote copies, remote signals or barrier semaphores. Data moves between devices by JAX's collectives and lax.ppermute only.
A program may use at most 192 MiB of HBM per device.

v0:
```python
import jax
import jax.numpy as jnp
from jax import lax
from jax.experimental import pallas as pl
from jax.experimental.pallas import tpu as pltpu
from jax.sharding import Mesh, PartitionSpec as P

HEAD_DIM = 64
LENGTH = 1024
BLOCK = 256
PAIR = 2 * HEAD_DIM
EPSILON = 1e-05
SCALE = HEAD_DIM**-0.5
LOW = jnp.bfloat16
FULL = jnp.float32
SWAP = ((0, 1), (1, 0))
DEEP = 4
LANES = 128
HALF = DEEP * LANES


def swap(values, axis):
    return lax.ppermute(values, axis, SWAP)


def swap_both(values):
    return lax.ppermute(values, ("y", "x"), ((0, 3), (1, 2), (2, 1), (3, 0)))


def all_sum(values, axis):
    size, step = lax.axis_size(axis), 1
    while step < size:
        values = values + lax.ppermute(values, axis, [(i, i ^ step) for i in range(size)])
        step *= 2
    return values


def after(values, *others):
    return lax.optimization_barrier((values, *others))[0]


def like(shape, kind):
    return jax.ShapeDtypeStruct(shape, kind)


ALL = slice(None)


ALL = slice(None)


class Operands:
    def __init__(self):
        self.parts = []

    def add(self, array, *index):
        for at, (one, where) in enumerate(self.parts):
            if one is array and where == index:
                return at
        self.parts.append((array, index))
        return len(self.parts) - 1

    def side(self, blocks):
        return [(self.add(array), index) for array, index in blocks]


class Buffers:
    def __init__(self, buffers, copies):
        self.buffers, self.copies = buffers, dict(enumerate(copies))

    def __getitem__(self, at):
        if at in self.copies:
            self.copies.pop(at).wait()
        return self.buffers[at]


def call(kernel, meta, ops, outs, scratch=(), time=3, limit=60):
    arrays = []
    for array, _ in ops.parts:
        if not any(array is one for one in arrays):
            arrays.append(array)
    source = [next(at for at, one in enumerate(arrays) if one is array) for array, _ in ops.parts]
    blocks = [jax.eval_shape(lambda a, index=index: a[index], like(array.shape, array.dtype)) for array, index in ops.parts]
    count, parts, results = len(arrays), len(ops.parts), len(outs)

    def body(*refs):
        meta_ref, sources, targets = refs[0], refs[1 : 1 + count], refs[1 + count : 1 + count + results]
        rest = refs[1 + count + results :]
        buffers, copies = rest[:parts], rest[parts : parts + results]
        in_sems, out_sems, *extra = rest[parts + results :]
        fetches = []
        for at, (_, index) in enumerate(ops.parts):
            ref = sources[source[at]]
            fetches.append(pltpu.make_async_copy(ref.at[index] if index else ref, buffers[at], in_sems.at[at]))
            fetches[-1].start()
        sent = []

        def put(at, *index):
            one, two = (copies[at].at[index], targets[at].at[index]) if index else (copies[at], targets[at])
            sent.append(pltpu.make_async_copy(one, two, out_sems.at[len(sent)]))
            sent[-1].start()

        kernel(meta_ref, Buffers(buffers, fetches), copies, put, *extra)
        for one in sent:
            one.wait()

    whole = pl.BlockSpec(memory_space=pl.ANY)
    return pl.pallas_call(
        body,
        out_shape=outs,
        in_specs=[pl.BlockSpec(memory_space=pltpu.SMEM)] + [whole] * count,
        out_specs=[whole] * results,
        scratch_shapes=[pltpu.VMEM(one.shape, one.dtype) for one in blocks]
        + [pltpu.VMEM(one.shape, one.dtype) for one in outs]
        + [pltpu.SemaphoreType.DMA((parts,)), pltpu.SemaphoreType.DMA((64,))]
        + list(scratch),
        compiler_params=pltpu.CompilerParams(vmem_limit_bytes=limit << 20),
        cost_estimate=pl.CostEstimate(flops=time << 20, bytes_accessed=1 << 16, transcendentals=0),
    )(meta, *arrays)


def whole_side(array):
    return [(array, (z,)) for z in range(DEEP)]


def stacked_side(array, which):
    return [(array, (z, which)) for z in range(DEEP)]


def split_side(low, high):
    return [((low, high)[z // 2], (z % 2,)) for z in range(DEEP)]


def dot(left, right):
    return jnp.dot(left, right, preferred_element_type=FULL)


def nt(left, right):
    return lax.dot_general(left, right, (((1,), (1,)), ((), ())), preferred_element_type=FULL)


def tn(left, right):
    return lax.dot_general(left, right, (((0,), (0,)), ((), ())), preferred_element_type=FULL)


def tall(refs, side, units=ALL):
    return jnp.concatenate([refs[at][(*index, ALL, units)] for at, index in side], axis=0)


def flat(refs, side, units):
    return jnp.concatenate([refs[at][(*index, units)] for at, index in side], axis=1)


def unfold(block):
    return jnp.concatenate([block[:, :LANES], block[:, LANES:]], axis=0)


def row_slices(count=LENGTH // BLOCK):
    return [slice(at * BLOCK, (at + 1) * BLOCK) for at in range(count)]


def rows_of(refs, pair, columns=ALL):
    for at in pair:
        for first in range(0, refs[at].shape[0], BLOCK):
            yield refs[at][first : first + BLOCK, columns]


def chunk_pairs():
    for first in range(0, 2 * DEEP, 2):
        yield (first, first + 1), slice(first * LANES, (first + 2) * LANES)


def by_tokens(lefts, rights):
    total = None
    for left, right in zip(lefts, rights):
        part = tn(left, right)
        total = part if total is None else total + part
    return total.astype(LOW)


def spread(even, terms, own, far, put, at):
    rows = own.shape[0]
    for z in range(DEEP):
        columns = slice(2 * z * LANES, 2 * (z + 1) * LANES)
        rights = []
        for _, chunks, product in terms:
            one, two = chunks(z)
            pair = [jnp.where(even, one, two), jnp.where(even, two, one)]
            rights.append(jnp.concatenate(pair, axis=0 if product is nt else 1))
        for block, here in enumerate(row_slices()):
            total = None
            for (left, _, product), right in zip(terms, rights):
                part = product(left(block), right)
                total = part if total is None else total + part
            if here.start < rows:
                own[here, columns] = total
            else:
                far[here.start - rows : here.stop - rows, columns] = total.astype(LOW)
        if z % 2:
            done = slice(columns.stop - 4 * LANES, columns.stop)
            put(at, ALL, done)
            put(at + 1, ALL, done)


def pick(refs, low, high, change=lambda block: block):
    return lambda z: [change(refs[at][one]) for at, one in (low[z], high[z])]


def to_local(at_y, target, rows, values):
    for chunk in range(2 * DEEP):
        place = chunk // 2 + DEEP * lax.rem(chunk + at_y, 2)
        columns = pl.ds(pl.multiple_of(place * LANES, LANES), LANES)
        target[rows, columns] = values[:, chunk * LANES : (chunk + 1) * LANES]


def row_ranges():
    for first in range(0, LENGTH, BLOCK):
        yield first, max(0, first - LENGTH // 2), first + BLOCK


def ordered(ref, which, core, columns):
    half = LENGTH // 2
    start = pl.multiple_of(core * half, half)
    rest = pl.multiple_of((1 - core) * half, half)
    return jnp.concatenate([ref[which, pl.ds(start, half), columns], ref[which, pl.ds(rest, half), columns]], axis=0)


def local_row(first, core):
    return pl.multiple_of(lax.rem(first + core * (LENGTH // 2), LENGTH), BLOCK)


def allowed_tile(meta, first, low, high):
    shape = (BLOCK, high - low)
    places = first + lax.broadcasted_iota(jnp.int32, (BLOCK, 1), 0)
    start = jnp.zeros((BLOCK, 1), jnp.int32)
    for at in range(2, meta.shape[0]):
        start = jnp.where(places >= meta[at], meta[at], start)
    keys = low + lax.broadcasted_iota(jnp.int32, shape, 1)
    return (keys <= places) & (keys >= start)


def first_lanes():
    return lax.broadcasted_iota(jnp.int32, (BLOCK, PAIR), 1) < HEAD_DIM


def attend(meta, qkv, context, logs, put):
    core = meta[0]
    first_head = first_lanes()
    for pair in range(context.shape[1] // PAIR):
        columns = slice(pair * PAIR, (pair + 1) * PAIR)
        keys = ordered(qkv, 1, core, columns)
        values = ordered(qkv, 2, core, columns)
        for first, low, high in row_ranges():
            here = local_row(first, core)
            query = qkv[0, pl.ds(here, BLOCK), columns] * SCALE
            allowed = allowed_tile(meta, first, low, high)
            outs = []
            sums = []
            for head in range(2):
                picked = jnp.where(first_head if head == 0 else ~first_head, query, jnp.zeros_like(query))
                scores = jnp.where(allowed, nt(picked, keys[low:high]), -1e30)
                highest = jnp.max(scores, axis=-1, keepdims=True)
                expos = jnp.exp(scores - highest)
                totals = jnp.sum(expos, axis=-1, keepdims=True)
                outs.append(dot(expos.astype(LOW), values[low:high]) * (1.0 / totals))
                sums.append(highest + jnp.log(totals))
            context[pl.ds(here, BLOCK), columns] = jnp.where(first_head, outs[0], outs[1]).astype(LOW)
            logs[pl.ds(here, BLOCK), columns] = jnp.where(first_head, sums[0], sums[1])
        put(1, ALL, columns)
        put(2, ALL, columns)


def attend_back(meta, qkv, logs, grads, out, sums, key_sum, value_sum):
    core = meta[0]
    first_head = first_lanes()
    half = LENGTH // 2
    for pair in range(grads.shape[1] // PAIR):
        columns = slice(pair * PAIR, (pair + 1) * PAIR)
        keys = ordered(qkv, 1, core, columns)
        values = ordered(qkv, 2, core, columns)
        key_sum[...] = jnp.zeros_like(key_sum)
        value_sum[...] = jnp.zeros_like(value_sum)
        query_total = value_total = jnp.zeros((1, PAIR), FULL)
        for first, low, high in row_ranges():
            here = local_row(first, core)
            query = qkv[0, pl.ds(here, BLOCK), columns] * SCALE
            grad = grads[pl.ds(here, BLOCK), columns]
            log_pair = logs[pl.ds(here, BLOCK), columns]
            allowed = allowed_tile(meta, first, low, high)
            query_flip = query.T
            grad_flip = grad.T
            outs = []
            for head in range(2):
                mask = first_head if head == 0 else ~first_head
                band = slice(head * HEAD_DIM, (head + 1) * HEAD_DIM)
                query_one = jnp.where(mask, query, jnp.zeros_like(query))
                grad_one = jnp.where(mask, grad, jnp.zeros_like(grad))
                log_one = log_pair[:, head * HEAD_DIM : head * HEAD_DIM + 1]
                scores = jnp.where(allowed, nt(query_one, keys[low:high]), -1e30)
                weights = jnp.exp(scores - log_one)
                grad_probs = nt(grad_one, values[low:high])
                inner = jnp.sum(grad_probs * weights, axis=-1, keepdims=True)
                grad_scores = (weights * (grad_probs - inner)).astype(LOW)
                outs.append(dot(grad_scores, keys[low:high]))
                key_sum[band, low:high] += dot(query_flip[band, :], grad_scores)
                value_sum[band, low:high] += dot(grad_flip[band, :], weights.astype(LOW))
            grad_query = (jnp.where(first_head, outs[0], outs[1]) * SCALE).astype(LOW)
            out[0, pl.ds(here, BLOCK), columns] = grad_query
            query_total = query_total + jnp.sum(grad_query.astype(FULL), axis=0, keepdims=True)
        for part in range(2):
            there = pl.multiple_of(lax.rem(part + core, 2) * half, half)
            out[1, pl.ds(there, half), columns] = key_sum[:, part * half : (part + 1) * half].T.astype(LOW)
            grad_value = value_sum[:, part * half : (part + 1) * half].T.astype(LOW)
            out[2, pl.ds(there, half), columns] = grad_value
            value_total = value_total + jnp.sum(grad_value.astype(FULL), axis=0, keepdims=True)
        sums[0:1, columns] = query_total
        sums[1:2, columns] = value_total


def attention_forward(meta, normed, sides, biases, last=None):
    ops = Operands()
    normed_at = [ops.add(normed[0])]
    sides_at = [[ops.side(one) for one in pair] for pair in sides]
    bias_at = ops.add(biases)
    normed_at.append(ops.add(normed[1]))
    width = sides[0][0][0][0].shape[-1]
    rows, wide = normed[0].shape
    outs = [like((3, LENGTH, width), LOW), like((LENGTH, width), LOW), like((LENGTH, width), FULL)]
    if last:
        first_at = ops.add(last[0])
        out_sides = [[ops.side(one) for one in pair] for pair in last[1]]
        outs += [like((rows, wide), FULL), like((rows, wide), LOW)]

    def kernel(meta, refs, results, put):
        qkv, context, logs = results[:3]
        for which, (low, high) in enumerate(sides_at):
            low_w = high_w = None
            for here, block in zip(row_slices(), rows_of(refs, normed_at)):
                if low_w is None:
                    low_w, high_w = tall(refs, low), tall(refs, high)
                total = dot(block[:, :HALF], low_w) + dot(block[:, HALF:], high_w)
                if which != 1:
                    total = total + refs[bias_at][:, which // 2 * width : (which // 2 + 1) * width]
                qkv[which, here, :] = total.astype(LOW)
        put(0)
        attend(meta, qkv, context, logs, put)
        if last:
            terms = [
                (lambda block, left=left: left[row_slices()[block], :], pick(refs, *pair, unfold), dot)
                for left, pair in zip((refs[first_at], context), out_sides)
            ]
            spread(meta[1] == 0, terms, *results[3:], put, 3)

    return call(kernel, meta, ops, outs, time=12 if last else 8)


def attention_backward(meta, grad, side, qkv, logs, context, normed):
    ops = Operands()
    grad_at = [ops.add(grad[0])]
    low, high = [ops.side(one) for one in side]
    grad_at.append(ops.add(grad[1]))
    qkv_at, log_at = [ops.add(one) for one in (qkv, logs)]
    normed_at = [ops.add(one) for one in normed]
    context_at = ops.add(context)
    width = context.shape[1]
    blocks = like((DEEP, 2, LANES, width), LOW)

    def kernel(meta, refs, results, put, grads, key_sum, value_sum):
        out, sums = results[:2]
        low_w = high_w = None
        for here, block in zip(row_slices(), rows_of(refs, grad_at)):
            if low_w is None:
                low_w, high_w = [
                    jnp.concatenate([unfold(refs[at][index]) for at, index in one], axis=1) for one in (low, high)
                ]
            grads[here, :] = (nt(block[:, :HALF], low_w) + nt(block[:, HALF:], high_w)).astype(LOW)
        attend_back(meta, refs[qkv_at], refs[log_at], grads, out, sums, key_sum, value_sum)
        put(0)
        put(1)
        for which in range(3):
            right = [out[which, here, :] for here in row_slices()]
            for places, columns in chunk_pairs():
                block = by_tokens(rows_of(refs, normed_at, columns), right)
                for part, place in enumerate(places):
                    target = results[2 + which // 2 + 2 * (place // DEEP)]
                    target[place % DEEP, which % 2] = block[part * LANES : (part + 1) * LANES, :]
            if which == 1:
                put(2)
                put(4)
        left = [refs[context_at][here, :] for here in row_slices()]
        for places, columns in chunk_pairs():
            block = by_tokens(left, rows_of(refs, grad_at, columns))
            for part, place in enumerate(places):
                target = results[3 + 2 * (place // DEEP)]
                one = block[:, part * LANES : (part + 1) * LANES]
                target[place % DEEP, 1] = jnp.concatenate([one[:LANES], one[LANES:]], axis=1)
        put(3)
        put(5)

    return call(
        kernel,
        meta,
        ops,
        [like((3, LENGTH, width), LOW), like((2, width), FULL)] + [blocks] * 4,
        [pltpu.VMEM((LENGTH, width), LOW)] + [pltpu.VMEM((PAIR, LENGTH), FULL)] * 2,
        time=15,
    )


def unit_tiles(width):
    for first in range(0, width, BLOCK):
        stop = first + BLOCK
        yield slice(first, stop), slice(stop - width // 2, stop) if stop % (width // 2) == 0 else None


def up_kernel(meta, normed, sides, biases, at, cot):
    ops = Operands()
    normed_at = [ops.add(normed[0])]
    sides_at, bias_at = [[ops.side(one) for one in sides[0]]], [ops.add(biases[0])]
    normed_at.append(ops.add(normed[1]))
    cot_at = [ops.add(one) for one in cot]
    sides_at.append([ops.side(one) for one in sides[1]])
    bias_at.append(ops.add(biases[1]))
    width = sides[0][0][0][0].shape[-1]
    blocks = like((DEEP, width, LANES), LOW)

    def kernel(meta, refs, results, put):
        for x in range(2):
            active, slope, *grads = results[4 * x : 4 * x + 4]
            low, high = sides_at[x]
            for units, done in unit_tiles(width):
                low_w = high_w = None
                for here, block in zip(row_slices(), rows_of(refs, normed_at)):
                    if low_w is None:
                        low_w, high_w = tall(refs, low, units), tall(refs, high, units)
                    before = dot(block[:, :HALF], low_w) + dot(block[:, HALF:], high_w)
                    before = before + refs[bias_at[x]][:, at + units.start : at + units.stop]
                    phi = 0.5 * (1.0 + lax.erf(before * (2.0**-0.5)))
                    active[here, units] = (before * phi).astype(LOW)
                    bell = jnp.exp(-0.5 * before * before) * (2.0 * jnp.pi) ** -0.5
                    slope[here, units] = (phi + before * bell).astype(LOW)
                left = [active[here, units] for here in row_slices()]
                for places, chunks in chunk_pairs():
                    block = by_tokens(left, rows_of(refs, cot_at, chunks))
                    for part, place in enumerate(places):
                        grads[place // DEEP][place % DEEP, units, :] = block[:, part * LANES : (part + 1) * LANES]
                if done:
                    for one in range(4 * x, 4 * x + 4):
                        put(one, ALL, done)

    return call(kernel, meta, ops, ([like((LENGTH, width), LOW)] * 2 + [blocks] * 2) * 2, time=18)


def down_kernel(meta, cot, sides, slopes, normed, up_sides, actives):
    ops = Operands()
    rows, wide = normed[0].shape
    width = slopes[0].shape[1]
    cot_at = [ops.add(cot[0])]
    sides_at, slope_at = [[ops.side(one) for one in sides[0]]], [ops.add(slopes[0])]
    cot_at.append(ops.add(cot[1]))
    sides_at.append([ops.side(one) for one in sides[1]])
    slope_at.append(ops.add(slopes[1]))
    up_at = [[ops.side(one) for one in pair] for pair in up_sides]
    normed_at = [ops.add(one) for one in normed]
    active_at = [ops.add(one) for one in actives]
    pair = [like((rows, wide), FULL), like((rows, wide), LOW)]
    outs = [like((1, width), FULL)] * 2 + pair + [like((2, LANES, width), LOW)] * 8 + pair

    def kernel(meta, refs, results, put, *grads):
        for x in range(2):
            low, high = sides_at[x]
            for units, _ in unit_tiles(width):
                total = jnp.zeros((1, BLOCK), FULL)
                low_w = high_w = None
                for here, block in zip(row_slices(), rows_of(refs, cot_at)):
                    if low_w is None:
                        low_w, high_w = flat(refs, low, units), flat(refs, high, units)
                    grad = nt(block[:, :HALF], low_w) + nt(block[:, HALF:], high_w)
                    grad = (grad * refs[slope_at[x]][here, units].astype(FULL)).astype(LOW)
                    grads[x][here, units] = grad
                    total = total + jnp.sum(grad.astype(FULL), axis=0, keepdims=True)
                results[x][:, units] = total
            put(x)

        def terms(lefts, sides, product):
            return [
                (lambda block, left=left: left[row_slices()[block], :], pick(refs, *one), product)
                for left, one in zip(lefts, sides)
            ]

        spread(meta[1] == 0, terms(grads, up_at, nt), *results[2:4], put, 2)
        for x in (1, 0):
            targets = results[4 + 4 * x : 8 + 4 * x]
            for units, done in unit_tiles(width):
                right = [grads[x][here, units] for here in row_slices()]
                for places, chunks in chunk_pairs():
                    block = by_tokens(rows_of(refs, normed_at, chunks), right)
                    for part, place in enumerate(places):
                        targets[place // 2][place % 2, :, units] = block[part * LANES : (part + 1) * LANES, :]
            for one in range(4 + 4 * x, 8 + 4 * x):
                put(one)
        spread(meta[1] == 0, terms([refs[at] for at in active_at], sides_at, dot), *results[12:14], put, 12)

    return call(kernel, meta, ops, outs, [pltpu.VMEM((LENGTH, width), LOW)] * 2, time=20)


def spread_kernel(meta, terms, rows, wide, product):
    ops = Operands()
    places = [(ops.add(left), at, ops.side(low), ops.side(high)) for left, at, low, high in terms]

    def kernel(meta, refs, results, put):
        def left_of(one, at):
            index = () if at is None else (at,)
            return lambda block: refs[one][(*index, row_slices()[block])]

        parts = [(left_of(one, at), pick(refs, low, high), product) for one, at, low, high in places]
        spread(meta[1] == 0, parts, *results, put, 0)

    return call(kernel, meta, ops, [like((rows, wide), FULL), like((rows, wide), LOW)], time=6)


STRIP = 128


def normalize(values):
    center = values - jnp.mean(values, axis=-1, keepdims=True)
    spread_ = jnp.mean(center * center, axis=-1, keepdims=True)
    rate = lax.rsqrt(spread_ + EPSILON)
    return center * rate, rate


def strips(rows):
    return [slice(first, first + STRIP) for first in range(0, rows, STRIP)]


def by_strips(kernel, meta, arrays, vectors, outs, sums=0):
    ops = Operands()
    rows, wide = arrays[0].shape
    halves = [slice(0, rows // 2), slice(rows // 2, rows)]
    first = [ops.add(array, halves[0]) for array in arrays]
    vector_at = [ops.add(one) for one in vectors]
    places = [first, [ops.add(array, halves[1]) for array in arrays]]
    shapes = [like((rows, wide), kind) for kind in outs]
    if sums:
        shapes.append(like((sums, wide), FULL))

    def body(meta, refs, results, put):
        parts = [None] * sums
        for at, half in zip(places, halves):
            for here in strips(rows // 2):
                kernel(
                    meta,
                    [refs[one][here, :] for one in at],
                    [refs[one][...] for one in vector_at],
                    [(result, slice(half.start + here.start, half.start + here.stop)) for result in results[: len(outs)]],
                    parts,
                )
            for one in range(len(outs)):
                put(one, half)
        if sums:
            for at, value in enumerate(parts):
                results[-1][at : at + 1, :] = jnp.sum(value, axis=0, keepdims=True)
            put(len(outs))

    return call(body, meta, ops, shapes, time=4)


def start_kernel(meta, values, vectors, results, sums):
    tokens, cot = values
    gain, shift = vectors
    hat, _ = normalize(tokens.astype(FULL))
    to_local(meta[1], *results[0], (hat * gain + shift).astype(LOW))
    to_local(meta[1], *results[1], cot.astype(LOW))


def join_kernel(meta, values, vectors, results, sums):
    tokens, own, got = values
    bias, gain, shift = vectors
    total = tokens.astype(FULL) + (own + got.astype(FULL)) + bias
    hidden, here = results[0]
    hidden[here, :] = total
    hat, _ = normalize(total)
    to_local(meta[1], *results[1], (hat * gain + shift).astype(LOW))


def add_sums(sums, values):
    for at, value in enumerate(values):
        part = jnp.sum(value.reshape(STRIP // 8, 8, value.shape[1]), axis=0)
        sums[at] = part if sums[at] is None else sums[at] + part


def norm_back(grad, values, gain):
    hat, rate = normalize(values)
    scaled = grad * gain
    row = rate * (
        scaled
        - jnp.mean(scaled, axis=-1, keepdims=True)
        - hat * jnp.mean(scaled * hat, axis=-1, keepdims=True)
    )
    return row, grad * hat


def second_kernel(meta, values, vectors, results, sums):
    own, got, hidden, pulled = values
    grad = own + got.astype(FULL)
    row, gain_part = norm_back(grad, hidden, vectors[0])
    total = pulled + row
    out, here = results[0]
    out[here, :] = total
    to_local(meta[1], *results[1], total.astype(LOW))
    add_sums(sums, [gain_part, grad, total, pulled])


def first_kernel(meta, values, vectors, results, sums):
    own, got, tokens, hidden_grad = values
    grad = own + got.astype(FULL)
    row, gain_part = norm_back(grad, tokens.astype(FULL), vectors[0])
    out, here = results[0]
    out[here, :] = hidden_grad + row
    add_sums(sums, [gain_part, grad])


def end_kernel(meta, values, vectors, results, sums):
    hidden, own, got = values
    out, here = results[0]
    out[here, :] = (hidden + (own + got.astype(FULL)) + vectors[0]).astype(LOW)


def wide_shard(shard, axis):
    return lax.all_gather(shard, "w", axis=axis, tiled=True) if lax.axis_size("w") > 1 else shard


def gather_deep(shard):
    return lax.all_gather(shard, "z", axis=0, tiled=False)


def add(*values):
    total = values[0].astype(FULL)
    for value in values[1:]:
        total = total + value.astype(FULL)
    return total.astype(LOW)


def scatter_deep(total):
    total = lax.psum_scatter(total, "z", scatter_dimension=0, tiled=False)
    if lax.axis_size("w") > 1:
        total = lax.psum_scatter(total, "w", scatter_dimension=total.ndim - 2, tiled=True)
    return total.astype(FULL)


def on_device(
    inputs,
    doc_lengths,
    first_gain,
    first_bias,
    w_query,
    b_query,
    w_key,
    w_value,
    b_value,
    w_out,
    b_out,
    second_gain,
    second_bias,
    w_up,
    b_up,
    w_down,
    b_down,
    cotangent,
):
    rows, wide = inputs.shape
    here = w_query.shape[1]
    core = lax.axis_index("c").astype(jnp.int32)
    at_y = lax.axis_index("y").astype(jnp.int32)
    at_x = lax.axis_index("x")
    lengths = lax.dynamic_index_in_dim(doc_lengths, at_x, 0, keepdims=False)
    ends = [lengths[0]]
    for one in range(1, lengths.shape[0]):
        ends.append(ends[-1] + lengths[one])
    meta = jnp.stack([core, at_y, *ends])

    def line(vector):
        return vector.reshape(1, -1)

    out_shard = wide_shard(w_out, 1)
    out_shard = jnp.concatenate([out_shard[: here // 2], out_shard[here // 2 :]], axis=1)
    attn_shard = jnp.stack([wide_shard(w_query, 0), wide_shard(w_key, 0), wide_shard(w_value, 0), out_shard])
    up_shard = wide_shard(w_up, 0)
    down_shard = wide_shard(w_down, 1)
    biases = line(jnp.concatenate([b_query, b_value, b_up]))
    far = swap(biases, "x")
    down_raw = swap_both(down_shard)
    attn_mine = after(gather_deep(attn_shard), down_raw, far)
    attn_pairs = [attn_mine[:, :2], attn_mine[:, 2:]]
    attn_x = [swap(one, "x") for one in attn_pairs]
    attn_y = [swap(one, "y") for one in attn_pairs]
    attn_far = [swap(attn_y[0], "x"), swap(attn_x[1], "y")]


    normed, cot = by_strips(start_kernel, meta, [inputs, cotangent], [line(first_gain), line(first_bias)], [LOW, LOW])
    normed = (normed, swap(normed, "c"))
    cot = (cot, swap(cot, "c"))

    attn_sides = [
        [(stacked_side(attn_mine, which), stacked_side(attn_y[which // 2], which % 2)) for which in range(4)],
        [(stacked_side(attn_x[which // 2], which % 2), stacked_side(attn_far[which // 2], which % 2)) for which in range(4)],
    ]

    qkv, context, logs = [None] * 2, [None] * 2, [None] * 2
    qkv[0], context[0], logs[0] = attention_forward(meta, normed, attn_sides[0][:3], biases)

    half = DEEP // 2
    up_mine = after(gather_deep(up_shard), context[0], *attn_far)
    up_parts = [up_mine[:half], up_mine[half:]]
    up_x = [swap(one, "x") for one in up_parts]
    up_y = [swap(one, "y") for one in up_parts]

    qkv[1], context[1], logs[1], own, sent = attention_forward(
        meta,
        normed,
        attn_sides[1][:3],
        far,
        (context[0], [attn_sides[0][3], attn_sides[1][3]]),
    )
    sent = after(sent, *up_x, *up_y)
    hidden, normed_two = by_strips(
        join_kernel,
        meta,
        [inputs, own, swap(sent, "c")],
        [line(b_out), line(second_gain), line(second_bias)],
        [FULL, LOW],
    )
    up_far = [swap(up_y[0], "x"), swap(up_x[1], "y")]
    normed_two = (normed_two, swap(after(normed_two, *up_far), "c"))

    up_sides = [
        (whole_side(up_mine), split_side(*up_y)),
        (split_side(*up_x), split_side(*up_far)),
    ]
    down_mine = after(gather_deep(down_shard), *up_far)
    down_x = swap(down_mine, "x")
    down_y = swap(down_mine, "y")
    down_both = gather_deep(down_raw)
    down_sides = [
        (whole_side(down_mine), whole_side(down_y)),
        (whole_side(down_x), whole_side(down_both)),
    ]
    active, slope, down_own, down_far = [None] * 2, [None] * 2, [None] * 2, [None] * 2
    (
        active[0],
        slope[0],
        down_own[0],
        down_far[0],
        active[1],
        slope[1],
        down_own[1],
        down_far[1],
    ) = up_kernel(meta, normed_two, up_sides, (biases, far), 2 * here, cot)

    *sums, own, sent, own_low, own_high, far_low, far_high, other_low, other_high, both_low, both_high, last, last_sent = down_kernel(
        meta, cot, down_sides, slope, normed_two, up_sides, active
    )
    up_own, up_beyond, up_other, up_both = (own_low, own_high), (far_low, far_high), (other_low, other_high), (both_low, both_high)

    down_diagonal = swap_both(lax.psum_scatter(down_far[1], "z", scatter_dimension=0, tiled=False))
    down_total = add(
        down_own[0], swap(after(down_far[0], down_x, down_y), "y"), swap(after(down_own[1], down_x, down_y), "x")
    )
    owner_down = lax.psum_scatter(down_total, "z", scatter_dimension=0, tiled=False)
    owner_down = owner_down.astype(FULL) + down_diagonal.astype(FULL)
    if lax.axis_size("w") > 1:
        owner_down = lax.psum_scatter(owner_down, "w", scatter_dimension=1, tiled=True)

    got_low = swap(up_both[0], "x")
    got_high = swap(up_both[1], "y")
    got_x = [swap(up_other[0], "x"), None]
    got_y = [None, swap(up_beyond[1], "y")]

    hidden_grad, attn_grad, second_sums = by_strips(
        second_kernel, meta, [own, swap(sent, "c"), hidden, cotangent], [line(second_gain)], [FULL, LOW], sums=4
    )
    attn_grad = (attn_grad, swap(attn_grad, "c"))

    got_y[0] = swap(add(up_beyond[0], after(got_low, attn_grad[0])), "y")
    got_x[1] = swap(add(up_other[1], after(got_high, attn_grad[0])), "x")

    back, unit_sums = [None] * 2, [None] * 2
    back[1], unit_sums[1], other_qk, other_vo, both_qk, both_vo = attention_backward(
        meta, attn_grad, attn_sides[1][3], qkv[1], logs[1], context[1], normed
    )
    got_qk = swap(both_qk, "x")
    got_vo = swap(both_vo, "y")
    x_qk = swap(other_qk, "x")
    got_x, got_y = [[after(one, back[1]) for one in parts] for parts in (got_x, got_y)]
    up_total = jnp.concatenate([add(up_own[part], got_x[part], got_y[part]) for part in range(2)])
    owner_up = scatter_deep(up_total)
    back[0], unit_sums[0], own_qk, own_vo, far_qk, far_vo = attention_backward(
        meta, (after(attn_grad[0], back[1]), attn_grad[1]), attn_sides[0][3], qkv[0], logs[0], context[0], normed
    )
    y_vo = swap(far_vo, "y")
    x_vo = swap(add(other_vo, after(got_vo, back[0])), "x")
    y_qk = swap(add(far_qk, after(got_qk, back[0])), "y")
    attn_total = jnp.concatenate([add(own_qk, x_qk, y_qk), add(own_vo, x_vo, y_vo)], axis=1)
    owner_attn = lax.psum_scatter(attn_total, "z", scatter_dimension=0, tiled=False)
    owner_out = owner_attn[3].astype(FULL)
    owner_out = jnp.concatenate([owner_out[:, :LANES], owner_out[:, LANES:]])
    owner_attn = owner_attn[:3].astype(FULL)
    if lax.axis_size("w") > 1:
        owner_attn = lax.psum_scatter(owner_attn, "w", scatter_dimension=1, tiled=True)
        owner_out = lax.psum_scatter(owner_out, "w", scatter_dimension=1, tiled=True)

    own, sent = spread_kernel(
        meta,
        [(back[x], which, *attn_sides[x][which]) for x in range(2) for which in range(3)],
        rows,
        wide,
        nt,
    )
    input_grad, first_sums = by_strips(
        first_kernel, meta, [own, swap(sent, "c"), inputs, hidden_grad], [line(first_gain)], [FULL], sums=2
    )

    [layer_out] = by_strips(
        end_kernel, meta, [hidden, last, swap(last_sent, "c")], [line(b_down)], [LOW]
    )

    replicated = all_sum(jnp.concatenate([first_sums, second_sums]).reshape(-1), "c")
    own_units, far_units = [
        jnp.concatenate([unit_sums[x][0], unit_sums[x][1], sums[x][0]]) for x in range(2)
    ]
    got = swap(jnp.concatenate([replicated, far_units]), "x")
    summed = jnp.concatenate([replicated, own_units]) + got
    for axis in ("y", "z", "w"):
        summed = all_sum(summed, axis)
    vectors = summed[: 6 * wide].reshape(6, wide)
    units = summed[6 * wide :]

    return (
        layer_out,
        input_grad,
        vectors[0],
        vectors[1],
        owner_attn[0],
        units[:here],
        owner_attn[1],
        owner_attn[2],
        units[here : 2 * here],
        owner_out,
        vectors[4],
        vectors[2],
        vectors[3],
        owner_up,
        units[2 * here :],
        owner_down,
        vectors[5],
    )


def solution(mesh):
    groups, lanes = mesh.shape["fsdp"], mesh.shape["tp"]
    inner = Mesh(
        mesh.devices.reshape(DEEP, 2, groups // (2 * DEEP), lanes // 2, 2), ("z", "y", "w", "x", "c")
    )
    f, t = ("z", "y", "w"), ("x", "c")
    tokens, rows, columns, units = P(f + t, None), P(f, t), P(t, f), P(t)
    return jax.shard_map(
        on_device,
        mesh=inner,
        in_specs=(
            tokens,
            P(f, None),
            P(),
            P(),
            rows,
            units,
            rows,
            rows,
            units,
            columns,
            P(),
            P(),
            P(),
            rows,
            units,
            columns,
            P(),
            tokens,
        ),
        out_specs=(
            tokens,
            tokens,
            P(),
            P(),
            rows,
            units,
            rows,
            rows,
            units,
            columns,
            P(),
            P(),
            P(),
            rows,
            units,
            columns,
            P(),
        ),
        check_vma=False,
    )
```

profile of v0, /device:TPU:0, one launch (start us, length us, event | category | flops | bytes accessed | tf_op | source)
XLA Modules:
  0.0 316.4 jit_solution(2951701716303345077)
XLA Ops:
  8.0 1.6 pad_maximum_fusion.2
  10.5 4.0 %collective-permute-start = (bf16[1024,128]{1,0:T(8,128)(2,1)}, bf16[1024,128]{1,0:T(8,128)(2,1)S(1)}, u32[]{:S(2)}, u32[]{:S(2)}) collective-permute-start(bf16[1024,128]{1,0:T(8,128)(2,1)} %param.33), channel_id=1, source_target_pairs={{0,6},{2,4},{4,2},{6,0},{1,7},{3,5},{5,3},{7,1},{8,14},{10,12},{12... | collective-permute-start | bytes 786440 | tf_op jit(solution)/shard_map/ppermute | solution.py:27
  20.3 4.7 %shard_map.305 = (bf16[512,1024]{1,0:T(8,128)(2,1)}, bf16[512,1024]{1,0:T(8,128)(2,1)}) custom-call(s32[6]{0:T(128)} %stack.38.refs_0_, bf16[512,1024]{1,0:T(8,128)(2,1)} %refs_3_.1, f32[512,1024]{1,0:T(8,128)} %refs_4_.1, f32[1,1024]{1,0:T(1,128)} %bitcast.62, f32[1,1024]{1,0:T(1,128)} %bitcast.64), custom_call_target="tpu_custom_call" | custom-call | flops 4194304 | bytes 65536 | tf_op jit(solution)/shard_map/pallas_call | solution.py:108
  25.1 15.8 %all-gather.9.cloned.1.call-done = bf16[16,128,256]{2,1,0:T(8,128)(2,1)} async-done(((bf16[4,128,256]{2,1,0:T(8,128)(2,1)}), bf16[16,128,256]{2,1,0:T(8,128)(2,1)}) %all-gather.9.cloned.1.call-update) | async-done | bytes 1048592 | tf_op jit(solution)/shard_map/all_gather | solution.py:634
  40.9 2.1 fusion.7
  46.5 10.2 %collective-permute-done.5.refs_4_.refs_2_.refs_8_ = bf16[4,2,128,256]{3,2,1,0:T(8,128)(2,1)S(1)} collective-permute-done((bf16[4,2,128,256]{3,2,1,0:T(8,128)(2,1)}, bf16[4,2,128,256]{3,2,1,0:T(8,128)(2,1)S(1)}, u32[]{:S(2)}, u32[]{:S(2)}) %collective-permute-start.5) | collective-permute-done | bytes 524320 | tf_op jit(solution)/shard_map/ppermute | solution.py:23
  61.6 8.9 %collective-permute-done.8.refs_4_.refs_10_.refs_3_ = bf16[4,2,128,256]{3,2,1,0:T(8,128)(2,1)S(1)} collective-permute-done((bf16[4,2,128,256]{3,2,1,0:T(8,128)(2,1)}, bf16[4,2,128,256]{3,2,1,0:T(8,128)(2,1)S(1)}, u32[]{:S(2)}, u32[]{:S(2)}) %collective-permute-start.8) | collective-permute-done | bytes 524320 | tf_op jit(solution)/shard_map/ppermute | solution.py:23
  71.3 12.5 %shard_map.306 = (bf16[3,1024,256]{2,1,0:T(8,128)(2,1)}, bf16[1024,256]{1,0:T(8,128)(2,1)}, f32[1024,256]{1,0:T(8,128)}) custom-call(s32[6]{0:T(128)} %stack.38.refs_0_, bf16[512,1024]{1,0:T(8,128)(2,1)} %get-tuple-element.86.refs_1_.refs_7_, bf16[4,4,128,256]{3,2,1,0:T(8,128)(2,1)} %bitcast.46, bf16[4,2,128,256]{3,2,1,0:T(8,128)(2,1)} %copy-done.14, ...), custom_call_target="tpu_custom_call" | custom-call | flops 8388608 | bytes 65536 | tf_op jit(solution)/shard_map/pallas_call | solution.py:108
  83.9 2.5 fusion.6
  90.4 14.0 %shard_map.307 = (bf16[3,1024,256]{2,1,0:T(8,128)(2,1)}, bf16[1024,256]{1,0:T(8,128)(2,1)}, f32[1024,256]{1,0:T(8,128)}, f32[512,1024]{1,0:T(8,128)}, bf16[512,1024]{1,0:T(8,128)(2,1)}) custom-call(s32[6]{0:T(128)} %stack.38.refs_0_, bf16[512,1024]{1,0:T(8,128)(2,1)} %get-tuple-element.86.refs_1_.refs_7_, ...), custom_call_target="tpu_custom_call" | custom-call | flops 12582912 | bytes 65536 | tf_op jit(solution)/shard_map/pallas_call | solution.py:108
  104.5 4.4 %collective-permute-done.12.refs_4_.refs_11_ = bf16[2,128,1024]{2,1,0:T(8,128)(2,1)S(1)} collective-permute-done((bf16[2,128,1024]{2,1,0:T(8,128)(2,1)}, bf16[2,128,1024]{2,1,0:T(8,128)(2,1)S(1)}, u32[]{:S(2)}, u32[]{:S(2)}) %collective-permute-start.12) | collective-permute-done | bytes 524320 | tf_op jit(solution)/shard_map/ppermute | solution.py:23
  112.8 5.1 %shard_map.308 = (f32[512,1024]{1,0:T(8,128)}, bf16[512,1024]{1,0:T(8,128)(2,1)}) custom-call(s32[6]{0:T(128)} %stack.38.refs_0_, bf16[512,1024]{1,0:T(8,128)(2,1)} %refs_3_.1, f32[512,1024]{1,0:T(8,128)} %get-tuple-element.89.refs_2_, bf16[512,1024]{1,0:T(8,128)(2,1)} %collective-permute-done.13.refs_3_, f32[1,1024]{1,0:T(1,128)} %bitcast.65, ...), custom_call_target="tpu_custom_call" | custom-call | flops 4194304 | bytes 65536 | tf_op jit(solution)/shard_map/pallas_call | solution.py:108
  117.9 5.6 %collective-permute-done.14.refs_11_.refs_14_ = bf16[2,128,1024]{2,1,0:T(8,128)(2,1)S(1)} collective-permute-done((bf16[2,128,1024]{2,1,0:T(8,128)(2,1)}, bf16[2,128,1024]{2,1,0:T(8,128)(2,1)S(1)}, u32[]{:S(2)}, u32[]{:S(2)}) %collective-permute-start.14) | collective-permute-done | bytes 524320 | tf_op jit(solution)/shard_map/ppermute | solution.py:23
  129.2 17.8 %shard_map.309 = (bf16[1024,1024]{1,0:T(8,128)(2,1)}, bf16[1024,1024]{1,0:T(8,128)(2,1)}, bf16[4,1024,128]{2,1,0:T(8,128)(2,1)}, bf16[4,1024,128]{2,1,0:T(8,128)...) custom-call(s32[6]{0:T(128)} %stack.38.refs_0_, ...), custom_call_target="tpu_custom_call" | custom-call | flops 18874368 | bytes 65536 | tf_op jit(solution)/shard_map/pallas_call | solution.py:108
  147.1 3.3 %collective-permute-done.16.refs_3_ = bf16[4,1024,128]{2,1,0:T(8,128)(2,1)} collective-permute-done((bf16[4,1024,128]{2,1,0:T(8,128)(2,1)}, bf16[4,1024,128]{2,1,0:T(8,128)(2,1)}, u32[]{:S(2)}, u32[]{:S(2)}) %collective-permute-start.16) | collective-permute-done | bytes 1048608 | tf_op jit(solution)/shard_map/ppermute | solution.py:23
  153.4 25.2 %shard_map.310 = (f32[1,1024]{1,0:T(1,128)}, f32[1,1024]{1,0:T(1,128)}, f32[512,1024]{1,0:T(8,128)}, bf16[512,1024]{1,0:T(8,128)(2,1)}, bf16[2,128,1024]{2,1,0:T...) custom-call(s32[6]{0:T(128)} %stack.38.refs_0_, ...), custom_call_target="tpu_custom_call" | custom-call | flops 20971520 | bytes 65536 | tf_op jit(solution)/shard_map/pallas_call | solution.py:108
  179.6 2.8 add_convert_fusion
  186.1 6.9 %shard_map.312 = (f32[512,1024]{1,0:T(8,128)}, bf16[512,1024]{1,0:T(8,128)(2,1)}, f32[4,1024]{1,0:T(4,128)}) custom-call(s32[6]{0:T(128)} %stack.38.refs_0_, f32[512,1024]{1,0:T(8,128)} %get-tuple-element.104.refs_1_, bf16[512,1024]{1,0:T(8,128)(2,1)} %copy-done.15, f32[512,1024]{1,0:T(8,128)} %get-tuple-element.93.refs_1_.refs_3_, f32[512,1024]{1,0:T(8,128)} %refs_4_.1, ...), custom_call_target="tpu_custom_call" | custom-call | flops 4194304 | bytes 65536 | tf_op jit(solution)/shard_map/pallas_call | solution.py:108
  200.7 17.6 %shard_map.313 = (bf16[3,1024,256]{2,1,0:T(8,128)(2,1)}, f32[2,256]{1,0:T(2,128)}, bf16[4,2,128,256]{3,2,1,0:T(8,128)(2,1)}, bf16[4,2,128,256]{3,2,1,0:T(8,128)(...) custom-call(s32[6]{0:T(128)} %stack.38.refs_0_, bf16[512,1024]{1,0:T(8,128)(2,1)} %get-tuple-element.111.refs_1_, ...), custom_call_target="tpu_custom_call" | custom-call | flops 15728640 | bytes 65536 | tf_op jit(solution)/shard_map/pallas_call | solution.py:108
  218.4 1.7 collective-permute-done.40
  227.1 17.7 %shard_map.314 = (bf16[3,1024,256]{2,1,0:T(8,128)(2,1)}, f32[2,256]{1,0:T(2,128)}, bf16[4,2,128,256]{3,2,1,0:T(8,128)(2,1)}, bf16[4,2,128,256]{3,2,1,0:T(8,128)(...) custom-call(s32[6]{0:T(128)} %stack.38.refs_0_, bf16[512,1024]{1,0:T(8,128)(2,1)} %get-tuple-element.111.refs_1_, ...), custom_call_target="tpu_custom_call" | custom-call | flops 15728640 | bytes 65536 | tf_op jit(solution)/shard_map/pallas_call | solution.py:108
  249.5 8.9 %shard_map.315 = (f32[512,1024]{1,0:T(8,128)}, bf16[512,1024]{1,0:T(8,128)(2,1)}) custom-call(s32[6]{0:T(128)} %stack.38.refs_0_, bf16[3,1024,256]{2,1,0:T(8,128)(2,1)} %get-tuple-element.114.refs_1_, bf16[4,4,128,256]{3,2,1,0:T(8,128)(2,1)} %bitcast.49, bf16[4,2,128,256]{3,2,1,0:T(8,128)(2,1)} %copy-done.14, bf16[4,2,128,256]{3,2,1,0:T(8,128)(2,1)} %copy-done.3, ...), custom_call_target="tpu_custom_call" | custom-call | flops 6291456 | bytes 65536 | tf_op jit(solution)/shard_map/pallas_call | solution.py:108
  258.5 2.5 collective-permute-done.31
  262.3 6.2 %collective-permute-done.34 = bf16[4,2,128,256]{3,2,1,0:T(8,128)(2,1)S(1)} collective-permute-done((bf16[4,2,128,256]{3,2,1,0:T(8,128)(2,1)}, bf16[4,2,128,256]{3,2,1,0:T(8,128)(2,1)S(1)}, u32[]{:S(2)}, u32[]{:S(2)}) %collective-permute-start.34) | collective-permute-done | bytes 524320 | tf_op jit(solution)/shard_map/ppermute | solution.py:23
  271.4 2.0 collective-permute-start.43
  274.4 6.3 %shard_map.316 = (f32[512,1024]{1,0:T(8,128)}, f32[2,1024]{1,0:T(2,128)}) custom-call(s32[6]{0:T(128)} %stack.38.refs_0_, f32[512,1024]{1,0:T(8,128)} %get-tuple-element.115.refs_1_, bf16[512,1024]{1,0:T(8,128)(2,1)} %copy-done.18, bf16[512,1024]{1,0:T(8,128)(2,1)} %refs_3_.1, f32[512,1024]{1,0:T(8,128)} %get-tuple-element.117.refs_4_, f32[1,1024]{1,0:T(1,128)} %bitcast.63), custom_call_target="tpu_custom_call" | custom-call | flops 4194304 | bytes 65536 | tf_op jit(solution)/shard_map/pallas_call | solution.py:108
  283.9 2.8 collective-permute-done.25
  287.1 3.6 %collective-permute-done.26 = f32[7680]{0:T(1024)S(1)} collective-permute-done((f32[7680]{0:T(1024)S(1)}, f32[7680]{0:T(1024)S(1)}, u32[]{:S(2)}, u32[]{:S(2)}) %collective-permute-start.26) | collective-permute-done | bytes 30752 | tf_op jit(solution)/shard_map/ppermute | solution.py:33
  293.0 4.9 %shard_map.311 = bf16[512,1024]{1,0:T(8,128)(2,1)} custom-call(s32[6]{0:T(128)} %stack.38.refs_0_, f32[512,1024]{1,0:T(8,128)} %get-tuple-element.93.refs_1_.refs_3_, f32[512,1024]{1,0:T(8,128)} %get-tuple-element.102.refs_2_, bf16[512,1024]{1,0:T(8,128)(2,1)} %copy-done.16, f32[1,1024]{1,0:T(1,128)} %bitcast.73), custom_call_target="tpu_custom_call" | custom-call | flops 4194304 | bytes 65536 | tf_op jit(solution)/shard_map/pallas_call | solution.py:108
  299.3 1.8 convert_add_fusion
  301.1 2.0 collective-permute-done.28
  304.3 1.8 bitcast_convert_fusion
  (206 shorter events, 71.5 us)
Async XLA Ops:
  7.2 33.7 %all-gather.9.cloned.1.call-start = ((), (), s32[]{:S(2)}) async-start(), calls=%async_computation.8 | async-start | bytes 1310720 | tf_op jit(solution)/shard_map/all_gather | solution.py:634
  9.7 74.1 %all-gather.11.cloned.1.call-start = ((), (), s32[]{:S(2)}) async-start(), calls=%async_computation.9 | async-start | bytes 1310720 | tf_op jit(solution)/shard_map/all_gather | solution.py:634
  10.5 114.1 %all-gather.13.cloned.1.call-start = ((), (), s32[]{:S(2)}) async-start(), calls=%async_computation.10 | async-start | bytes 1310720 | tf_op jit(solution)/shard_map/all_gather | solution.py:634
  24.9 36.7 %collective-permute-start.7 = (bf16[512,1024]{1,0:T(8,128)(2,1)}, bf16[512,1024]{1,0:T(8,128)(2,1)S(1)}, u32[]{:S(2)}, u32[]{:S(2)}) collective-permute-start(bf16[512,1024]{1,0:T(8,128)(2,1)} %get-tuple-element.86.refs_1_.refs_7_), channel_id=1, source_target_pairs={{0,1},{1,0},{2,3},{3,2},{4,5},{5,4},{6,7},{7,6},{8,9},{9,8},{10,11... | collective-permute-start | bytes 3145736 | tf_op jit(solution)/shard_map/ppermute | solution.py:23
  45.9 24.6 %collective-permute-start.8 = (bf16[4,2,128,256]{3,2,1,0:T(8,128)(2,1)}, bf16[4,2,128,256]{3,2,1,0:T(8,128)(2,1)S(1)}, u32[]{:S(2)}, u32[]{:S(2)}) collective-permute-start(bf16[4,2,128,256]{3,2,1,0:T(8,128)(2,1)} %get-tuple-element.157), channel_id=1, source_target_pairs={{0,4},{4,0},{1,5},{5,1},{2,6},{6,2},{3,7},{7,3},{8,12},{12,8},{9,1... | collective-permute-start | bytes 1572872 | tf_op jit(solution)/shard_map/ppermute | solution.py:23
  56.7 27.2 %collective-permute-start.6 = (bf16[4,2,128,256]{3,2,1,0:T(8,128)(2,1)S(1)}, bf16[4,2,128,256]{3,2,1,0:T(8,128)(2,1)S(1)}, u32[]{:S(2)}, u32[]{:S(2)}) collective-permute-start(bf16[4,2,128,256]{3,2,1,0:T(8,128)(2,1)S(1)} %collective-permute-done.5.refs_4_.refs_2_.refs_8_), channel_id=1, source_target_pairs={{0,4},{4,0},{1,5},{5,1},{2,6},{6,2},{3,7},{7,3},{8,12},{12,8},{9,1... | collective-permute-start | bytes 1572872 | tf_op jit(solution)/shard_map/ppermute | solution.py:23
  59.3 24.6 %collective-permute-start.4 = (bf16[4,2,128,256]{3,2,1,0:T(8,128)(2,1)S(1)}, bf16[4,2,128,256]{3,2,1,0:T(8,128)(2,1)}, u32[]{:S(2)}, u32[]{:S(2)}) collective-permute-start(bf16[4,2,128,256]{3,2,1,0:T(8,128)(2,1)S(1)} %collective-permute-done.3.refs_3_), channel_id=1, source_target_pairs={{0,2},{2,0},{1,3},{3,1},{4,6},{6,4},{5,7},{7,5},{8,10},{10,8},{9,1... | collective-permute-start | bytes 1572872 | tf_op jit(solution)/shard_map/ppermute | solution.py:23
  59.9 93.5 %all-gather.15.cloned.1.call-start = ((), (), s32[]{:S(2)}) async-start(), calls=%async_computation.11 | async-start | bytes 1310720 | tf_op jit(solution)/shard_map/all_gather | solution.py:634
  60.1 30.3 %collective-permute-start.2 = (bf16[4,2,128,256]{3,2,1,0:T(8,128)(2,1)}, bf16[4,2,128,256]{3,2,1,0:T(8,128)(2,1)}, u32[]{:S(2)}, u32[]{:S(2)}) collective-permute-start(bf16[4,2,128,256]{3,2,1,0:T(8,128)(2,1)} %copy-done.24), channel_id=1, source_target_pairs={{0,2},{2,0},{1,3},{3,1},{4,6},{6,4},{5,7},{7,5},{8,10},{10,8},{9,1... | collective-permute-start | bytes 1572872 | tf_op jit(solution)/shard_map/ppermute | solution.py:23
  86.3 18.1 %collective-permute-start.10 = (bf16[2,128,1024]{2,1,0:T(8,128)(2,1)}, bf16[2,128,1024]{2,1,0:T(8,128)(2,1)S(1)}, u32[]{:S(2)}, u32[]{:S(2)}) collective-permute-start(bf16[2,128,1024]{2,1,0:T(8,128)(2,1)} %get-tuple-element.155), channel_id=1, source_target_pairs={{0,2},{2,0},{1,3},{3,1},{4,6},{6,4},{5,7},{7,5},{8,10},{10,8},{9,1... | collective-permute-start | bytes 1572872 | tf_op jit(solution)/shard_map/ppermute | solution.py:23
  86.9 17.6 %collective-permute-start.11 = (bf16[2,128,1024]{2,1,0:T(8,128)(2,1)}, bf16[2,128,1024]{2,1,0:T(8,128)(2,1)}, u32[]{:S(2)}, u32[]{:S(2)}) collective-permute-start(bf16[2,128,1024]{2,1,0:T(8,128)(2,1)} %get-tuple-element.156), channel_id=1, source_target_pairs={{0,4},{4,0},{1,5},{5,1},{2,6},{6,2},{3,7},{7,3},{8,12},{12,8},{9,1... | collective-permute-start | bytes 1572872 | tf_op jit(solution)/shard_map/ppermute | solution.py:23
  88.3 20.5 %collective-permute-start.12 = (bf16[2,128,1024]{2,1,0:T(8,128)(2,1)}, bf16[2,128,1024]{2,1,0:T(8,128)(2,1)S(1)}, u32[]{:S(2)}, u32[]{:S(2)}) collective-permute-start(bf16[2,128,1024]{2,1,0:T(8,128)(2,1)} %get-tuple-element.155), channel_id=1, source_target_pairs={{0,4},{4,0},{1,5},{5,1},{2,6},{6,2},{3,7},{7,3},{8,12},{12,8},{9,1... | collective-permute-start | bytes 1572872 | tf_op jit(solution)/shard_map/ppermute | solution.py:23
  88.9 20.0 %collective-permute-start.9 = (bf16[2,128,1024]{2,1,0:T(8,128)(2,1)}, bf16[2,128,1024]{2,1,0:T(8,128)(2,1)S(1)}, u32[]{:S(2)}, u32[]{:S(2)}) collective-permute-start(bf16[2,128,1024]{2,1,0:T(8,128)(2,1)} %get-tuple-element.156), channel_id=1, source_target_pairs={{0,2},{2,0},{1,3},{3,1},{4,6},{6,4},{5,7},{7,5},{8,10},{10,8},{9,1... | collective-permute-start | bytes 1572872 | tf_op jit(solution)/shard_map/ppermute | solution.py:23
  112.7 158.7 %reduce-scatter.11.cloned.1.call-start = ((), (), s32[]{:S(2)}) async-start(), calls=%async_computation.7 | async-start | bytes 1310720 | tf_op jit(solution)/shard_map/reduce_scatter | solution.py:765
  124.5 25.9 %collective-permute-start.16 = (bf16[4,1024,128]{2,1,0:T(8,128)(2,1)}, bf16[4,1024,128]{2,1,0:T(8,128)(2,1)}, u32[]{:S(2)}, u32[]{:S(2)}) collective-permute-start(bf16[4,1024,128]{2,1,0:T(8,128)(2,1)} %bitcast.53), channel_id=1, source_target_pairs={{0,4},{4,0},{1,5},{5,1},{2,6},{6,2},{3,7},{7,3},{8,12},{12,8},{9,1... | collective-permute-start | bytes 3145736 | tf_op jit(solution)/shard_map/ppermute | solution.py:23
  126.1 25.5 %collective-permute-start.19 = (bf16[4,1024,128]{2,1,0:T(8,128)(2,1)}, bf16[4,1024,128]{2,1,0:T(8,128)(2,1)}, u32[]{:S(2)}, u32[]{:S(2)}) collective-permute-start(bf16[4,1024,128]{2,1,0:T(8,128)(2,1)} %bitcast.54), channel_id=1, source_target_pairs={{0,2},{2,0},{1,3},{3,1},{4,6},{6,4},{5,7},{7,5},{8,10},{10,8},{9,1... | collective-permute-start | bytes 3145736 | tf_op jit(solution)/shard_map/ppermute | solution.py:23
  147.0 152.3 %reduce-scatter.9.cloned.1.call-start = ((), (), s32[]{:S(2)}) async-start(), calls=%async_computation.6 | async-start | bytes 1310720 | tf_op jit(solution)/shard_map/reduce_scatter | solution.py:769
  151.7 27.9 %collective-permute-start.41 = (bf16[4,1024,128]{2,1,0:T(8,128)(2,1)}, bf16[4,1024,128]{2,1,0:T(8,128)(2,1)S(1)}, u32[]{:S(2)}, u32[]{:S(2)}) collective-permute-start(bf16[4,1024,128]{2,1,0:T(8,128)(2,1)} %get-tuple-element.151), channel_id=1, source_target_pairs={{0,4},{4,0},{1,5},{5,1},{2,6},{6,2},{3,7},{7,3},{8,12},{12,8},{9,1... | collective-permute-start | bytes 3145736 | tf_op jit(solution)/shard_map/ppermute | solution.py:23
  152.2 27.4 %collective-permute-start.42 = (bf16[4,1024,128]{2,1,0:T(8,128)(2,1)}, bf16[4,1024,128]{2,1,0:T(8,128)(2,1)}, u32[]{:S(2)}, u32[]{:S(2)}) collective-permute-start(bf16[4,1024,128]{2,1,0:T(8,128)(2,1)} %get-tuple-element.153), channel_id=1, source_target_pairs={{0,2},{2,0},{1,3},{3,1},{4,6},{6,4},{5,7},{7,5},{8,10},{10,8},{9,1... | collective-permute-start | bytes 3145736 | tf_op jit(solution)/shard_map/ppermute | solution.py:23
  182.4 121.9 %reduce-scatter.7.cloned.1.call-start = ((), (), s32[]{:S(2)}) async-start(), calls=%async_computation.5 | async-start | bytes 1310720 | tf_op jit(solution)/shard_map/reduce_scatter | solution.py:645
  184.0 34.4 %collective-permute-start.35 = (bf16[2,128,1024]{2,1,0:T(8,128)(2,1)}, bf16[2,128,1024]{2,1,0:T(8,128)(2,1)S(1)}, u32[]{:S(2)}, u32[]{:S(2)}) collective-permute-start(bf16[2,128,1024]{2,1,0:T(8,128)(2,1)} %get-tuple-element.136), channel_id=1, source_target_pairs={{0,2},{2,0},{1,3},{3,1},{4,6},{6,4},{5,7},{7,5},{8,10},{10,8},{9,1... | collective-permute-start | bytes 1572872 | tf_op jit(solution)/shard_map/ppermute | solution.py:23
  195.0 23.3 %collective-permute-start.37 = (bf16[2,128,1024]{2,1,0:T(8,128)(2,1)S(1)}, bf16[2,128,1024]{2,1,0:T(8,128)(2,1)}, u32[]{:S(2)}, u32[]{:S(2)}) collective-permute-start(bf16[2,128,1024]{2,1,0:T(8,128)(2,1)S(1)} %add_convert_fusion.4), channel_id=1, source_target_pairs={{0,4},{4,0},{1,5},{5,1},{2,6},{6,2},{3,7},{7,3},{8,12},{12,8},{9,1... | collective-permute-start | bytes 1572872 | tf_op jit(solution)/shard_map/ppermute | solution.py:23
  196.9 21.5 %collective-permute-start.39 = (bf16[2,128,1024]{2,1,0:T(8,128)(2,1)S(1)}, bf16[2,128,1024]{2,1,0:T(8,128)(2,1)}, u32[]{:S(2)}, u32[]{:S(2)}) collective-permute-start(bf16[2,128,1024]{2,1,0:T(8,128)(2,1)S(1)} %add_convert_fusion.2), channel_id=1, source_target_pairs={{0,2},{2,0},{1,3},{3,1},{4,6},{6,4},{5,7},{7,5},{8,10},{10,8},{9,1... | collective-permute-start | bytes 1572872 | tf_op jit(solution)/shard_map/ppermute | solution.py:23
  198.1 22.0 %collective-permute-start.40 = (bf16[2,128,1024]{2,1,0:T(8,128)(2,1)}, bf16[2,128,1024]{2,1,0:T(8,128)(2,1)}, u32[]{:S(2)}, u32[]{:S(2)}) collective-permute-start(bf16[2,128,1024]{2,1,0:T(8,128)(2,1)} %get-tuple-element.147), channel_id=1, source_target_pairs={{0,4},{4,0},{1,5},{5,1},{2,6},{6,2},{3,7},{7,3},{8,12},{12,8},{9,1... | collective-permute-start | bytes 1572872 | tf_op jit(solution)/shard_map/ppermute | solution.py:23
  224.1 82.0 %reduce-scatter.5.cloned.1.call-start = ((), (), s32[]{:S(2)}) async-start(), calls=%async_computation.4 | async-start | bytes 1310720 | tf_op jit(solution)/shard_map/reduce_scatter | solution.py:804
  224.1 20.7 %collective-permute-start.30 = (bf16[4,2,128,256]{3,2,1,0:T(8,128)(2,1)S(1)}, bf16[4,2,128,256]{3,2,1,0:T(8,128)(2,1)S(1)}, u32[]{:S(2)}, u32[]{:S(2)}) collective-permute-start(bf16[4,2,128,256]{3,2,1,0:T(8,128)(2,1)S(1)} %copy-done.36), channel_id=1, source_target_pairs={{0,2},{2,0},{1,3},{3,1},{4,6},{6,4},{5,7},{7,5},{8,10},{10,8},{9,1... | collective-permute-start | bytes 1572872 | tf_op jit(solution)/shard_map/ppermute | solution.py:23
  225.0 23.1 %collective-permute-start.32 = (bf16[4,2,128,256]{3,2,1,0:T(8,128)(2,1)}, bf16[4,2,128,256]{3,2,1,0:T(8,128)(2,1)S(1)}, u32[]{:S(2)}, u32[]{:S(2)}) collective-permute-start(bf16[4,2,128,256]{3,2,1,0:T(8,128)(2,1)} %get-tuple-element.132), channel_id=1, source_target_pairs={{0,4},{4,0},{1,5},{5,1},{2,6},{6,2},{3,7},{7,3},{8,12},{12,8},{9,1... | collective-permute-start | bytes 1572872 | tf_op jit(solution)/shard_map/ppermute | solution.py:23
  226.0 32.5 %collective-permute-start.29 = (bf16[4,2,128,256]{3,2,1,0:T(8,128)(2,1)}, bf16[4,2,128,256]{3,2,1,0:T(8,128)(2,1)S(1)}, u32[]{:S(2)}, u32[]{:S(2)}) collective-permute-start(bf16[4,2,128,256]{3,2,1,0:T(8,128)(2,1)} %get-tuple-element.126), channel_id=1, source_target_pairs={{0,2},{2,0},{1,3},{3,1},{4,6},{6,4},{5,7},{7,5},{8,10},{10,8},{9,1... | collective-permute-start | bytes 1572872 | tf_op jit(solution)/shard_map/ppermute | solution.py:23
  247.2 21.3 %collective-permute-start.34 = (bf16[4,2,128,256]{3,2,1,0:T(8,128)(2,1)}, bf16[4,2,128,256]{3,2,1,0:T(8,128)(2,1)S(1)}, u32[]{:S(2)}, u32[]{:S(2)}) collective-permute-start(bf16[4,2,128,256]{3,2,1,0:T(8,128)(2,1)} %get-tuple-element.134), channel_id=1, source_target_pairs={{0,4},{4,0},{1,5},{5,1},{2,6},{6,2},{3,7},{7,3},{8,12},{12,8},{9,1... | collective-permute-start | bytes 1572872 | tf_op jit(solution)/shard_map/ppermute | solution.py:23
  248.5 20.0 %collective-permute-start.33 = (bf16[4,2,128,256]{3,2,1,0:T(8,128)(2,1)S(1)}, bf16[4,2,128,256]{3,2,1,0:T(8,128)(2,1)}, u32[]{:S(2)}, u32[]{:S(2)}) collective-permute-start(bf16[4,2,128,256]{3,2,1,0:T(8,128)(2,1)S(1)} %add_convert_fusion.6), channel_id=1, source_target_pairs={{0,2},{2,0},{1,3},{3,1},{4,6},{6,4},{5,7},{7,5},{8,10},{10,8},{9,1... | collective-permute-start | bytes 1572872 | tf_op jit(solution)/shard_map/ppermute | solution.py:23
  271.4 20.6 %collective-permute-start.20 = (bf16[512,1024]{1,0:T(8,128)(2,1)S(1)}, bf16[512,1024]{1,0:T(8,128)(2,1)S(1)}, u32[]{:S(2)}, u32[]{:S(2)}) collective-permute-start(bf16[512,1024]{1,0:T(8,128)(2,1)S(1)} %copy-done.35), channel_id=1, source_target_pairs={{0,1},{1,0},{2,3},{3,2},{4,5},{5,4},{6,7},{7,6},{8,9},{9,8},{10,11... | collective-permute-start | bytes 3145736 | tf_op jit(solution)/shard_map/ppermute | solution.py:23
  271.4 27.9 %collective-permute-start.43 = (bf16[1024,128]{1,0:T(8,128)(2,1)}, bf16[1024,128]{1,0:T(8,128)(2,1)S(1)}, u32[]{:S(2)}, u32[]{:S(2)}) collective-permute-start(bf16[1024,128]{1,0:T(8,128)(2,1)} %bitcast.74), channel_id=1, source_target_pairs={{0,6},{2,4},{4,2},{6,0},{1,7},{3,5},{5,3},{7,1},{8,14},{10,12},{12... | collective-permute-start | bytes 786440 | tf_op jit(solution)/shard_map/ppermute | solution.py:27
  (57 other events, 651.9 us)
Sparse Core Ops, SparseCore 0:
  10.2 30.6 all-gather.8
  42.4 27.3 all-gather.10
  71.4 27.4 all-gather.12
  112.8 26.2 all-gather.14
  147.2 26.2 reduce-scatter.10
  182.5 27.0 reduce-scatter.8
  224.2 26.1 reduce-scatter.6
  271.0 27.3 reduce-scatter.4
where the time goes:
time: 320 us; the launch traced here: 316 us
  Pallas kernels  142 us (44%)
  waiting for transfers between devices  73.2 us (23%)
  starting transfers between devices  44.6 us (14%)
  other arithmetic  22.2 us (7%)
  between operations  17.8 us (6%)
  local copies, waits for them, and re-layouts  17.1 us (5%)
    pallas_call x12, Pallas kernels, call(): pl.pallas_call(body, out_shape=outs, in_specs=[pl.BlockSpec(memory_space=...  142 us
    ppermute x38, waiting for transfers between devices, swap(): return lax.ppermute(values, axis, SWAP)  50 us
    ppermute x38, starting transfers between devices, swap(): return lax.ppermute(values, axis, SWAP)  34.8 us
    all_gather x4, waiting for transfers between devices, gather_deep(): return lax.all_gather(shard, 'z', axis=0, tiled=False)  15.8 us
    convert_element_type x9, other arithmetic, add(): return total.astype(LOW)  10.8 us
    unnamed x74, local copies, waits for them, and re-layouts  7.96 us
    ppermute x4, waiting for transfers between devices, all_sum(): lax.ppermute(values, axis, [(i, i ^ step) for i in range(size)])  6.58 us
  transfers between devices with their start and end apart: 52, of which 19 were waited for; matrix products, arithmetic and copies ran while one was open for 8% of the time, Pallas kernels for 45%

commit v1 on v0

--- a/solution.py
+++ b/solution.py
@@ -27,9 +27,11 @@
     return lax.ppermute(values, ("y", "x"), ((0, 3), (1, 2), (2, 1), (3, 0)))
 
 
-def all_sum(values, axis):
+def all_sum(values, axis, *cover):
     size, step = lax.axis_size(axis), 1
     while step < size:
+        if cover:
+            values, cover = after(values, *cover[0]), cover[1:]
         values = values + lax.ppermute(values, axis, [(i, i ^ step) for i in range(size)])
         step *= 2
     return values
@@ -250,6 +252,7 @@
         columns = slice(pair * PAIR, (pair + 1) * PAIR)
         keys = ordered(qkv, 1, core, columns)
         values = ordered(qkv, 2, core, columns)
+        values = jnp.concatenate([values, jnp.ones_like(values)], axis=1)
         for first, low, high in row_ranges():
             here = local_row(first, core)
             query = qkv[0, pl.ds(here, BLOCK), columns] * SCALE
@@ -260,9 +263,9 @@
                 picked = jnp.where(first_head if head == 0 else ~first_head, query, jnp.zeros_like(query))
                 scores = jnp.where(allowed, nt(picked, keys[low:high]), -1e30)
                 highest = jnp.max(scores, axis=-1, keepdims=True)
-                expos = jnp.exp(scores - highest)
-                totals = jnp.sum(expos, axis=-1, keepdims=True)
-                outs.append(dot(expos.astype(LOW), values[low:high]) * (1.0 / totals))
+                mixed = dot(jnp.exp(scores - highest).astype(LOW), values[low:high])
+                totals = mixed[:, PAIR:]
+                outs.append(mixed[:, :PAIR] / totals)
                 sums.append(highest + jnp.log(totals))
             context[pl.ds(here, BLOCK), columns] = jnp.where(first_head, outs[0], outs[1]).astype(LOW)
             logs[pl.ds(here, BLOCK), columns] = jnp.where(first_head, sums[0], sums[1])
@@ -363,7 +366,7 @@
     normed_at = [ops.add(one) for one in normed]
     context_at = ops.add(context)
     width = context.shape[1]
-    blocks = like((DEEP, 2, LANES, width), LOW)
+    blocks = like((DEEP, 4, LANES, width), LOW)
 
     def kernel(meta, refs, results, put, grads, key_sum, value_sum):
         out, sums = results[:2]
@@ -382,26 +385,21 @@
             for places, columns in chunk_pairs():
                 block = by_tokens(rows_of(refs, normed_at, columns), right)
                 for part, place in enumerate(places):
-                    target = results[2 + which // 2 + 2 * (place // DEEP)]
-                    target[place % DEEP, which % 2] = block[part * LANES : (part + 1) * LANES, :]
-            if which == 1:
-                put(2)
-                put(4)
+                    results[2 + place // DEEP][place % DEEP, which] = block[part * LANES : (part + 1) * LANES, :]
         left = [refs[context_at][here, :] for here in row_slices()]
         for places, columns in chunk_pairs():
             block = by_tokens(left, rows_of(refs, grad_at, columns))
             for part, place in enumerate(places):
-                target = results[3 + 2 * (place // DEEP)]
                 one = block[:, part * LANES : (part + 1) * LANES]
-                target[place % DEEP, 1] = jnp.concatenate([one[:LANES], one[LANES:]], axis=1)
+                results[2 + place // DEEP][place % DEEP, 3] = jnp.concatenate([one[:LANES], one[LANES:]], axis=1)
+        put(2)
         put(3)
-        put(5)
 
     return call(
         kernel,
         meta,
         ops,
-        [like((3, LENGTH, width), LOW), like((2, width), FULL)] + [blocks] * 4,
+        [like((3, LENGTH, width), LOW), like((2, width), FULL)] + [blocks] * 2,
         [pltpu.VMEM((LENGTH, width), LOW)] + [pltpu.VMEM((PAIR, LENGTH), FULL)] * 2,
         time=15,
     )
@@ -451,7 +449,7 @@
     return call(kernel, meta, ops, ([like((LENGTH, width), LOW)] * 2 + [blocks] * 2) * 2, time=18)
 
 
-def down_kernel(meta, cot, sides, slopes, normed, up_sides, actives):
+def down_kernel(meta, cot, sides, slopes, normed, up_sides):
     ops = Operands()
     rows, wide = normed[0].shape
     width = slopes[0].shape[1]
@@ -462,9 +460,9 @@
     slope_at.append(ops.add(slopes[1]))
     up_at = [[ops.side(one) for one in pair] for pair in up_sides]
     normed_at = [ops.add(one) for one in normed]
-    active_at = [ops.add(one) for one in actives]
     pair = [like((rows, wide), FULL), like((rows, wide), LOW)]
-    outs = [like((1, width), FULL)] * 2 + pair + [like((2, LANES, width), LOW)] * 8 + pair
+    block, half = like((DEEP, LANES, width), LOW), like((DEEP // 2, LANES, width), LOW)
+    outs = [like((1, width), FULL)] * 2 + pair + [block] * 3 + [half] * 2
 
     def kernel(meta, refs, results, put, *grads):
         for x in range(2):
@@ -482,24 +480,28 @@
                 results[x][:, units] = total
             put(x)
 
-        def terms(lefts, sides, product):
-            return [
-                (lambda block, left=left: left[row_slices()[block], :], pick(refs, *one), product)
-                for left, one in zip(lefts, sides)
-            ]
-
-        spread(meta[1] == 0, terms(grads, up_at, nt), *results[2:4], put, 2)
+        terms = [
+            (lambda block, left=left: left[row_slices()[block], :], pick(refs, *one), nt)
+            for left, one in zip(grads, up_at)
+        ]
+        spread(meta[1] == 0, terms, *results[2:4], put, 2)
         for x in (1, 0):
-            targets = results[4 + 4 * x : 8 + 4 * x]
+            own, low, high = (results[6], *results[7:9]) if x else (results[4], None, None)
+
+            def target(place, own=own, low=low, high=high):
+                if place < DEEP:
+                    return own.at[place]
+                place -= DEEP
+                return (low, high)[place // 2].at[place % 2] if low is not None else results[5].at[place]
+
             for units, done in unit_tiles(width):
                 right = [grads[x][here, units] for here in row_slices()]
                 for places, chunks in chunk_pairs():
                     block = by_tokens(rows_of(refs, normed_at, chunks), right)
                     for part, place in enumerate(places):
-                        targets[place // 2][place % 2, :, units] = block[part * LANES : (part + 1) * LANES, :]
-            for one in range(4 + 4 * x, 8 + 4 * x):
+                        target(place)[:, units] = block[part * LANES : (part + 1) * LANES, :]
+            for one in (6, 7, 8) if x else (4, 5):
                 put(one)
-        spread(meta[1] == 0, terms([refs[at] for at in active_at], sides_at, dot), *results[12:14], put, 12)
 
     return call(kernel, meta, ops, outs, [pltpu.VMEM((LENGTH, width), LOW)] * 2, time=20)
 
@@ -694,7 +696,10 @@
     attn_pairs = [attn_mine[:, :2], attn_mine[:, 2:]]
     attn_x = [swap(one, "x") for one in attn_pairs]
     attn_y = [swap(one, "y") for one in attn_pairs]
-    attn_far = [swap(attn_y[0], "x"), swap(attn_x[1], "y")]
+    attn_far = [
+        swap(after(attn_y[0], attn_y[1], *attn_x), "x"),
+        swap(after(attn_x[1], attn_x[0], *attn_y), "y"),
+    ]
 
 
     normed, cot = by_strips(start_kernel, meta, [inputs, cotangent], [line(first_gain), line(first_bias)], [LOW, LOW])
@@ -757,10 +762,9 @@
         down_far[1],
     ) = up_kernel(meta, normed_two, up_sides, (biases, far), 2 * here, cot)
 
-    *sums, own, sent, own_low, own_high, far_low, far_high, other_low, other_high, both_low, both_high, last, last_sent = down_kernel(
-        meta, cot, down_sides, slope, normed_two, up_sides, active
-    )
-    up_own, up_beyond, up_other, up_both = (own_low, own_high), (far_low, far_high), (other_low, other_high), (both_low, both_high)
+    *sums, own, sent, up_own, up_beyond, up_other, up_both_low, up_both_high = down_kernel(
+        meta, cot, down_sides, slope, normed_two, up_sides
+    )
 
     down_diagonal = swap_both(lax.psum_scatter(down_far[1], "z", scatter_dimension=0, tiled=False))
     down_total = add(
@@ -771,36 +775,38 @@
     if lax.axis_size("w") > 1:
         owner_down = lax.psum_scatter(owner_down, "w", scatter_dimension=1, tiled=True)
 
-    got_low = swap(up_both[0], "x")
-    got_high = swap(up_both[1], "y")
-    got_x = [swap(up_other[0], "x"), None]
-    got_y = [None, swap(up_beyond[1], "y")]
+    got_low = swap(up_both_low, "x")
+    got_high = swap(up_both_high, "y")
 
     hidden_grad, attn_grad, second_sums = by_strips(
         second_kernel, meta, [own, swap(sent, "c"), hidden, cotangent], [line(second_gain)], [FULL, LOW], sums=4
     )
     attn_grad = (attn_grad, swap(attn_grad, "c"))
 
-    got_y[0] = swap(add(up_beyond[0], after(got_low, attn_grad[0])), "y")
-    got_x[1] = swap(add(up_other[1], after(got_high, attn_grad[0])), "x")
+    got_low, got_high = [after(one, attn_grad[0]).astype(FULL) for one in (got_low, got_high)]
+    half = ((DEEP // 2, 0, 0), (0, 0, 0), (0, 0, 0))
+    got_y = swap(add(up_beyond, lax.pad(got_low, FULL(0), ((0, DEEP // 2, 0), *half[1:]))), "y")
+    got_x = swap(add(up_other, lax.pad(got_high, FULL(0), half)), "x")
 
     back, unit_sums = [None] * 2, [None] * 2
-    back[1], unit_sums[1], other_qk, other_vo, both_qk, both_vo = attention_backward(
+    back[1], unit_sums[1], attn_other_x, attn_both = attention_backward(
         meta, attn_grad, attn_sides[1][3], qkv[1], logs[1], context[1], normed
     )
-    got_qk = swap(both_qk, "x")
-    got_vo = swap(both_vo, "y")
-    x_qk = swap(other_qk, "x")
-    got_x, got_y = [[after(one, back[1]) for one in parts] for parts in (got_x, got_y)]
-    up_total = jnp.concatenate([add(up_own[part], got_x[part], got_y[part]) for part in range(2)])
-    owner_up = scatter_deep(up_total)
-    back[0], unit_sums[0], own_qk, own_vo, far_qk, far_vo = attention_backward(
+    got_both = swap(attn_both, "x")
+    attn_got_x = swap(attn_other_x, "x")
+    back[0], unit_sums[0], attn_own, attn_beyond = attention_backward(
         meta, (after(attn_grad[0], back[1]), attn_grad[1]), attn_sides[0][3], qkv[0], logs[0], context[0], normed
     )
-    y_vo = swap(far_vo, "y")
-    x_vo = swap(add(other_vo, after(got_vo, back[0])), "x")
-    y_qk = swap(add(far_qk, after(got_qk, back[0])), "y")
-    attn_total = jnp.concatenate([add(own_qk, x_qk, y_qk), add(own_vo, x_vo, y_vo)], axis=1)
+    attn_got_y = swap(add(attn_beyond, after(got_both, back[0])), "y")
+    owner_up = scatter_deep(add(up_own, *[after(one, back[0]) for one in (got_x, got_y)]))
+    last, last_sent = spread_kernel(
+        meta,
+        [(after(active[0], back[0]), None, *down_sides[0]), (active[1], None, *down_sides[1])],
+        rows,
+        wide,
+        dot,
+    )
+    attn_total = add(attn_own, after(attn_got_x, last_sent), attn_got_y)
     owner_attn = lax.psum_scatter(attn_total, "z", scatter_dimension=0, tiled=False)
     owner_out = owner_attn[3].astype(FULL)
     owner_out = jnp.concatenate([owner_out[:, :LANES], owner_out[:, LANES:]])
@@ -821,7 +827,7 @@
     )
 
     [layer_out] = by_strips(
-        end_kernel, meta, [hidden, last, swap(last_sent, "c")], [line(b_down)], [LOW]
+        end_kernel, meta, [hidden, after(last, attn_total), swap(last_sent, "c")], [line(b_down)], [LOW]
     )
 
     replicated = all_sum(jnp.concatenate([first_sums, second_sums]).reshape(-1), "c")
@@ -830,8 +836,9 @@
     ]
     got = swap(jnp.concatenate([replicated, far_units]), "x")
     summed = jnp.concatenate([replicated, own_units]) + got
-    for axis in ("y", "z", "w"):
-        summed = all_sum(summed, axis)
+    summed = all_sum(summed, "y")
+    summed = all_sum(summed, "z", (layer_out,), (owner_up, owner_down))
+    summed = all_sum(summed, "w")
     vectors = summed[: 6 * wide].reshape(6, wide)
     units = summed[6 * wide :]
 

time: 320 us -> 317 us (level)
  starting transfers between devices: 44.6 us -> 38.9 us
    ppermute x38 -> x33, starting transfers between devices: 34.8 us -> 27.6 us  [swap(): return lax.ppermute(values, axis, SWAP)]
    pallas_call x12 -> x13, Pallas kernels: 142 us -> 145 us  [call(): pl.pallas_call(body, out_shape=outs, in_specs=[pl.BlockSpec(memory_space=...]
    convert_element_type x9 -> x6, other arithmetic: 10.8 us -> 12.9 us  [add(): return total.astype(LOW)]
    ppermute x38 -> x33, waiting for transfers between devices: 50 us -> 52.1 us  [swap(): return lax.ppermute(values, axis, SWAP)]
    unnamed x74 -> x68, local copies, waits for them, and re-layouts: 7.96 us -> 8.29 us
  transfers between devices with their start and end apart: 52 -> 47, of which waited for: 19 -> 20; matrix products, arithmetic and copies ran while one was open for 8% -> 8% of each run, Pallas kernels for 45% -> 46%
where the time goes in v1:
time: 317 us; the launch traced here: 314 us
  Pallas kernels  145 us (46%)
  waiting for transfers between devices  74 us (23%)
  starting transfers between devices  38.9 us (12%)
  other arithmetic  22.1 us (7%)
  between operations  17.6 us (6%)
  local copies, waits for them, and re-layouts  16.6 us (5%)
    pallas_call x13, Pallas kernels, call(): pl.pallas_call(body, out_shape=outs, in_specs=[pl.BlockSpec(memory_space=...  145 us
    ppermute x33, waiting for transfers between devices, swap(): return lax.ppermute(values, axis, SWAP)  52.1 us
    ppermute x33, starting transfers between devices, swap(): return lax.ppermute(values, axis, SWAP)  27.6 us
    all_gather x4, waiting for transfers between devices, gather_deep(): return lax.all_gather(shard, 'z', axis=0, tiled=False)  15.9 us
    convert_element_type x6, other arithmetic, add(): return total.astype(LOW)  12.9 us
    unnamed x68, local copies, waits for them, and re-layouts  8.29 us
  transfers between devices with their start and end apart: 47, of which 20 were waited for; matrix products, arithmetic and copies ran while one was open for 8% of the time, Pallas kernels for 46%

profile of v1, /device:TPU:0, one launch (start us, length us, event | category | flops | bytes accessed | tf_op | source)
XLA Modules:
  0.0 313.6 jit_solution(2086046180048922519)
XLA Ops:
  8.0 1.6 pad_maximum_fusion
  10.5 4.0 %collective-permute-start = (bf16[1024,128]{1,0:T(8,128)(2,1)}, bf16[1024,128]{1,0:T(8,128)(2,1)S(1)}, u32[]{:S(2)}, u32[]{:S(2)}) collective-permute-start(bf16[1024,128]{1,0:T(8,128)(2,1)} %param.33), channel_id=1, source_target_pairs={{0,6},{2,4},{4,2},{6,0},{1,7},{3,5},{5,3},{7,1},{8,14},{10,12},{12... | collective-permute-start | bytes 786440 | tf_op jit(solution)/shard_map/ppermute | solution.py:27
  20.3 4.6 %shard_map.305 = (bf16[512,1024]{1,0:T(8,128)(2,1)}, bf16[512,1024]{1,0:T(8,128)(2,1)}) custom-call(s32[6]{0:T(128)} %stack.38.refs_0_, bf16[512,1024]{1,0:T(8,128)(2,1)} %refs_3_.1, f32[512,1024]{1,0:T(8,128)} %refs_4_.1, f32[1,1024]{1,0:T(1,128)} %bitcast.64, f32[1,1024]{1,0:T(1,128)} %bitcast.66), custom_call_target="tpu_custom_call" | custom-call | flops 4194304 | bytes 65536 | tf_op jit(solution)/shard_map/pallas_call | solution.py:110
  25.0 15.8 %all-gather.9.cloned.1.call-done = bf16[16,128,256]{2,1,0:T(8,128)(2,1)} async-done(((bf16[4,128,256]{2,1,0:T(8,128)(2,1)}), bf16[16,128,256]{2,1,0:T(8,128)(2,1)}) %all-gather.9.cloned.1.call-update) | async-done | bytes 1048592 | tf_op jit(solution)/shard_map/all_gather | solution.py:636
  46.3 10.8 %collective-permute-done.5.refs_4_.refs_2_.refs_8_ = bf16[4,2,128,256]{3,2,1,0:T(8,128)(2,1)S(1)} collective-permute-done((bf16[4,2,128,256]{3,2,1,0:T(8,128)(2,1)S(1)}, bf16[4,2,128,256]{3,2,1,0:T(8,128)(2,1)S(1)}, u32[]{:S(2)}, u32[]{:S(2)}) %collective-permute-start.5) | collective-permute-done | bytes 524320 | tf_op jit(solution)/shard_map/ppermute | solution.py:23
  58.5 9.6 %collective-permute-done.3.refs_3_ = bf16[4,2,128,256]{3,2,1,0:T(8,128)(2,1)S(1)} collective-permute-done((bf16[4,2,128,256]{3,2,1,0:T(8,128)(2,1)S(1)}, bf16[4,2,128,256]{3,2,1,0:T(8,128)(2,1)S(1)}, u32[]{:S(2)}, u32[]{:S(2)}) %collective-permute-start.3) | collective-permute-done | bytes 524320 | tf_op jit(solution)/shard_map/ppermute | solution.py:23
  72.3 10.8 %shard_map.306 = (bf16[3,1024,256]{2,1,0:T(8,128)(2,1)}, bf16[1024,256]{1,0:T(8,128)(2,1)}, f32[1024,256]{1,0:T(8,128)}) custom-call(s32[6]{0:T(128)} %stack.38.refs_0_, bf16[512,1024]{1,0:T(8,128)(2,1)} %get-tuple-element.83.refs_1_.refs_7_, bf16[4,4,128,256]{3,2,1,0:T(8,128)(2,1)} %bitcast.46, bf16[4,2,128,256]{3,2,1,0:T(8,128)(2,1)} %copy-done.15, ...), custom_call_target="tpu_custom_call" | custom-call | flops 8388608 | bytes 65536 | tf_op jit(solution)/shard_map/pallas_call | solution.py:110
  83.2 2.4 fusion.6
  89.7 12.7 %shard_map.307 = (bf16[3,1024,256]{2,1,0:T(8,128)(2,1)}, bf16[1024,256]{1,0:T(8,128)(2,1)}, f32[1024,256]{1,0:T(8,128)}, f32[512,1024]{1,0:T(8,128)}, bf16[512,1024]{1,0:T(8,128)(2,1)}) custom-call(s32[6]{0:T(128)} %stack.38.refs_0_, bf16[512,1024]{1,0:T(8,128)(2,1)} %get-tuple-element.83.refs_1_.refs_7_, bf16[4,2,128,256]{3,2,1,0:T(8,128)(2,1)} %copy-done.16, ...), custom_call_target="tpu_custom_call" | custom-call | flops 12582912 | bytes 65536 | tf_op jit(solution)/shard_map/pallas_call | solution.py:110
  102.4 6.7 %collective-permute-done.11.refs_3_.refs_10_ = bf16[2,128,1024]{2,1,0:T(8,128)(2,1)} collective-permute-done((bf16[2,128,1024]{2,1,0:T(8,128)(2,1)}, bf16[2,128,1024]{2,1,0:T(8,128)(2,1)}, u32[]{:S(2)}, u32[]{:S(2)}) %collective-permute-start.11) | collective-permute-done | bytes 524320 | tf_op jit(solution)/shard_map/ppermute | solution.py:23
  113.2 5.1 %shard_map.308 = (f32[512,1024]{1,0:T(8,128)}, bf16[512,1024]{1,0:T(8,128)(2,1)}) custom-call(s32[6]{0:T(128)} %stack.38.refs_0_, bf16[512,1024]{1,0:T(8,128)(2,1)} %refs_3_.1, f32[512,1024]{1,0:T(8,128)} %get-tuple-element.88.refs_2_, bf16[512,1024]{1,0:T(8,128)(2,1)} %collective-permute-done.13.refs_3_, f32[1,1024]{1,0:T(1,128)} %bitcast.67, ...), custom_call_target="tpu_custom_call" | custom-call | flops 4194304 | bytes 65536 | tf_op jit(solution)/shard_map/pallas_call | solution.py:110
  118.3 6.1 %collective-permute-done.15.refs_12_.refs_15_ = bf16[2,128,1024]{2,1,0:T(8,128)(2,1)S(1)} collective-permute-done((bf16[2,128,1024]{2,1,0:T(8,128)(2,1)S(1)}, bf16[2,128,1024]{2,1,0:T(8,128)(2,1)S(1)}, u32[]{:S(2)}, u32[]{:S(2)}) %collective-permute-start.15) | collective-permute-done | bytes 524320 | tf_op jit(solution)/shard_map/ppermute | solution.py:23
  128.8 18.0 %shard_map.309 = (bf16[1024,1024]{1,0:T(8,128)(2,1)}, bf16[1024,1024]{1,0:T(8,128)(2,1)}, bf16[4,1024,128]{2,1,0:T(8,128)(2,1)}, bf16[4,1024,128]{2,1,0:T(8,128)...) custom-call(s32[6]{0:T(128)} %stack.38.refs_0_, ...), custom_call_target="tpu_custom_call" | custom-call | flops 18874368 | bytes 65536 | tf_op jit(solution)/shard_map/pallas_call | solution.py:110
  146.9 4.7 %collective-permute-done.19.refs_6_.refs_5_ = bf16[4,1024,128]{2,1,0:T(8,128)(2,1)S(1)} collective-permute-done((bf16[4,1024,128]{2,1,0:T(8,128)(2,1)}, bf16[4,1024,128]{2,1,0:T(8,128)(2,1)S(1)}, u32[]{:S(2)}, u32[]{:S(2)}) %collective-permute-start.19) | collective-permute-done | bytes 1048608 | tf_op jit(solution)/shard_map/ppermute | solution.py:23
  153.9 20.7 %shard_map.310 = (f32[1,1024]{1,0:T(1,128)}, f32[1,1024]{1,0:T(1,128)}, f32[512,1024]{1,0:T(8,128)}, bf16[512,1024]{1,0:T(8,128)(2,1)}, bf16[4,128,1024]{2,1,0:T...) custom-call(s32[6]{0:T(128)} %stack.38.refs_0_, ...), custom_call_target="tpu_custom_call" | custom-call | flops 20971520 | bytes 65536 | tf_op jit(solution)/shard_map/pallas_call | solution.py:110
  177.7 3.3 %add_convert_fusion = bf16[4,1024,128]{2,1,0:T(8,128)(2,1)} fusion(bf16[4,1024,128]{2,1,0:T(8,128)(2,1)} %collective-permute-done.36, bf16[4,1024,128]{2,1,0:T(8,128)(2,1)} %collective-permute-done.35, bf16[4,1024,128]{2,1,0:T(8,128)(2,1)} %get-tuple-element.142), kind=kLoop, calls=%fused_computation | loop fusion | flops 3145728 | bytes 4194304 | tf_op jit(solution)/shard_map/convert_element_type | solution.py:643
  182.1 6.8 %shard_map.311 = (f32[512,1024]{1,0:T(8,128)}, bf16[512,1024]{1,0:T(8,128)(2,1)}, f32[4,1024]{1,0:T(4,128)}) custom-call(s32[6]{0:T(128)} %stack.38.refs_0_, f32[512,1024]{1,0:T(8,128)} %get-tuple-element.100.refs_1_, bf16[512,1024]{1,0:T(8,128)(2,1)} %copy-done.18, f32[512,1024]{1,0:T(8,128)} %get-tuple-element.92.refs_3_.refs_1_, f32[512,1024]{1,0:T(8,128)} %refs_4_.1, ...), custom_call_target="tpu_custom_call" | custom-call | flops 4194304 | bytes 65536 | tf_op jit(solution)/shard_map/pallas_call | solution.py:110
  196.6 17.7 %shard_map.312 = (bf16[3,1024,256]{2,1,0:T(8,128)(2,1)}, f32[2,256]{1,0:T(2,128)}, bf16[4,4,128,256]{3,2,1,0:T(8,128)(2,1)}, bf16[4,4,128,256]{3,2,1,0:T(8,128)(2,1)}) custom-call(s32[6]{0:T(128)} %stack.38.refs_0_, bf16[512,1024]{1,0:T(8,128)(2,1)} %get-tuple-element.107.refs_1_, bf16[4,2,128,256]{3,2,1,0:T(8,128)(2,1)} %copy-done.4, ...), custom_call_target="tpu_custom_call" | custom-call | flops 15728640 | bytes 65536 | tf_op jit(solution)/shard_map/pallas_call | solution.py:110
  215.1 17.7 %shard_map.313 = (bf16[3,1024,256]{2,1,0:T(8,128)(2,1)}, f32[2,256]{1,0:T(2,128)}, bf16[4,4,128,256]{3,2,1,0:T(8,128)(2,1)}, bf16[4,4,128,256]{3,2,1,0:T(8,128)(2,1)}) custom-call(s32[6]{0:T(128)} %stack.38.refs_0_, bf16[512,1024]{1,0:T(8,128)(2,1)} %get-tuple-element.107.refs_1_, bf16[4,4,128,256]{3,2,1,0:T(8,128)(2,1)} %bitcast.48, ...), custom_call_target="tpu_custom_call" | custom-call | flops 15728640 | bytes 65536 | tf_op jit(solution)/shard_map/pallas_call | solution.py:110
  232.8 3.6 %add_convert_fusion.1 = bf16[4,128,1024]{2,1,0:T(8,128)(2,1)} fusion(bf16[4,128,1024]{2,1,0:T(8,128)(2,1)} %collective-permute-done.34, bf16[4,128,1024]{2,1,0:T(8,128)(2,1)} %collective-permute-done.32, bf16[4,128,1024]{2,1,0:T(8,128)(2,1)} %get-tuple-element.133), kind=kLoop, calls=%fused_computation.1 | loop fusion | flops 3145728 | bytes 4194304 | tf_op jit(solution)/shard_map/convert_element_type | solution.py:643
  238.1 4.7 %collective-permute-done.23 = bf16[4,4,128,256]{3,2,1,0:T(8,128)(2,1)S(1)} collective-permute-done((bf16[4,4,128,256]{3,2,1,0:T(8,128)(2,1)}, bf16[4,4,128,256]{3,2,1,0:T(8,128)(2,1)S(1)}, u32[]{:S(2)}, u32[]{:S(2)}) %collective-permute-start.23) | collective-permute-done | bytes 1048608 | tf_op jit(solution)/shard_map/ppermute | solution.py:23
  243.6 8.9 %shard_map.316 = (f32[512,1024]{1,0:T(8,128)}, bf16[512,1024]{1,0:T(8,128)(2,1)}) custom-call(s32[6]{0:T(128)} %stack.38.refs_0_, bf16[3,1024,256]{2,1,0:T(8,128)(2,1)} %get-tuple-element.110.refs_1_, bf16[4,4,128,256]{3,2,1,0:T(8,128)(2,1)} %bitcast.49, bf16[4,2,128,256]{3,2,1,0:T(8,128)(2,1)} %copy-done.15, bf16[4,2,128,256]{3,2,1,0:T(8,128)(2,1)} %copy-done.3, ...), custom_call_target="tpu_custom_call" | custom-call | flops 6291456 | bytes 65536 | tf_op jit(solution)/shard_map/pallas_call | solution.py:110
  252.7 10.3 %shard_map.314 = (f32[512,1024]{1,0:T(8,128)}, bf16[512,1024]{1,0:T(8,128)(2,1)}) custom-call(s32[6]{0:T(128)} %stack.38.refs_0_, bf16[1024,1024]{1,0:T(8,128)(2,1)} %get-tuple-element.111.refs_1_, bf16[4,1024,128]{2,1,0:T(8,128)(2,1)} %bitcast.56, bf16[4,1024,128]{2,1,0:T(8,128)(2,1)} %copy-done.8, bf16[1024,1024]{1,0:T(8,128)(2,1)} %get-tuple-element.112.refs_4_, ...), custom_call_target="tpu_custom_call" | custom-call | flops 6291456 | bytes 65536 | tf_op jit(solution)/shard_map/pallas_call | solution.py:110
  265.4 3.1 add_convert_fusion.4
  271.1 6.3 %shard_map.317 = (f32[512,1024]{1,0:T(8,128)}, f32[2,1024]{1,0:T(2,128)}) custom-call(s32[6]{0:T(128)} %stack.38.refs_0_, f32[512,1024]{1,0:T(8,128)} %get-tuple-element.122.refs_1_, bf16[512,1024]{1,0:T(8,128)(2,1)} %copy-done.23, bf16[512,1024]{1,0:T(8,128)(2,1)} %refs_3_.1, f32[512,1024]{1,0:T(8,128)} %get-tuple-element.124.refs_4_, f32[1,1024]{1,0:T(1,128)} %bitcast.65), custom_call_target="tpu_custom_call" | custom-call | flops 4194304 | bytes 65536 | tf_op jit(solution)/shard_map/pallas_call | solution.py:110
  279.4 1.7 collective-permute-start.28
  281.0 2.3 collective-permute-done.28
  284.9 1.8 convert_add_fusion
  288.4 4.9 %shard_map.315 = bf16[512,1024]{1,0:T(8,128)(2,1)} custom-call(s32[6]{0:T(128)} %stack.38.refs_0_, f32[512,1024]{1,0:T(8,128)} %get-tuple-element.92.refs_3_.refs_1_, f32[512,1024]{1,0:T(8,128)} %get-tuple-element.121.refs_2_, bf16[512,1024]{1,0:T(8,128)(2,1)} %copy-done.21, f32[1,1024]{1,0:T(1,128)} %bitcast.75), custom_call_target="tpu_custom_call" | custom-call | flops 4194304 | bytes 65536 | tf_op jit(solution)/shard_map/pallas_call | solution.py:110
  294.6 1.8 bitcast_convert_fusion
  297.3 2.1 collective-permute-start.38
  299.5 2.7 collective-permute-done.38
  (186 shorter events, 62.7 us)
Async XLA Ops:
  7.2 33.7 %all-gather.9.cloned.1.call-start = ((), (), s32[]{:S(2)}) async-start(), calls=%async_computation.8 | async-start | bytes 1310720 | tf_op jit(solution)/shard_map/all_gather | solution.py:636
  9.7 73.5 %all-gather.11.cloned.1.call-start = ((), (), s32[]{:S(2)}) async-start(), calls=%async_computation.9 | async-start | bytes 1310720 | tf_op jit(solution)/shard_map/all_gather | solution.py:636
  10.5 115.4 %all-gather.13.cloned.1.call-start = ((), (), s32[]{:S(2)}) async-start(), calls=%async_computation.10 | async-start | bytes 1310720 | tf_op jit(solution)/shard_map/all_gather | solution.py:636
  24.9 46.4 %collective-permute-start.8 = (bf16[512,1024]{1,0:T(8,128)(2,1)}, bf16[512,1024]{1,0:T(8,128)(2,1)S(1)}, u32[]{:S(2)}, u32[]{:S(2)}) collective-permute-start(bf16[512,1024]{1,0:T(8,128)(2,1)} %get-tuple-element.83.refs_1_.refs_7_), channel_id=1, source_target_pairs={{0,1},{1,0},{2,3},{3,2},{4,5},{5,4},{6,7},{7,6},{8,9},{9,8},{10,11... | collective-permute-start | bytes 3145736 | tf_op jit(solution)/shard_map/ppermute | solution.py:23
  42.1 14.9 %collective-permute-start.5 = (bf16[4,2,128,256]{3,2,1,0:T(8,128)(2,1)S(1)}, bf16[4,2,128,256]{3,2,1,0:T(8,128)(2,1)S(1)}, u32[]{:S(2)}, u32[]{:S(2)}) collective-permute-start(bf16[4,2,128,256]{3,2,1,0:T(8,128)(2,1)S(1)} %get-tuple-element.151), channel_id=1, source_target_pairs={{0,2},{2,0},{1,3},{3,1},{4,6},{6,4},{5,7},{7,5},{8,10},{10,8},{9,1... | collective-permute-start | bytes 1572872 | tf_op jit(solution)/shard_map/ppermute | solution.py:23
  43.7 14.9 %collective-permute-start.4 = (bf16[4,2,128,256]{3,2,1,0:T(8,128)(2,1)S(1)}, bf16[4,2,128,256]{3,2,1,0:T(8,128)(2,1)S(1)}, u32[]{:S(2)}, u32[]{:S(2)}) collective-permute-start(bf16[4,2,128,256]{3,2,1,0:T(8,128)(2,1)S(1)} %get-tuple-element.151), channel_id=1, source_target_pairs={{0,4},{4,0},{1,5},{5,1},{2,6},{6,2},{3,7},{7,3},{8,12},{12,8},{9,1... | collective-permute-start | bytes 1572872 | tf_op jit(solution)/shard_map/ppermute | solution.py:23
  45.1 23.0 %collective-permute-start.3 = (bf16[4,2,128,256]{3,2,1,0:T(8,128)(2,1)S(1)}, bf16[4,2,128,256]{3,2,1,0:T(8,128)(2,1)S(1)}, u32[]{:S(2)}, u32[]{:S(2)}) collective-permute-start(bf16[4,2,128,256]{3,2,1,0:T(8,128)(2,1)S(1)} %get-tuple-element.152), channel_id=1, source_target_pairs={{0,4},{4,0},{1,5},{5,1},{2,6},{6,2},{3,7},{7,3},{8,12},{12,8},{9,1... | collective-permute-start | bytes 1572872 | tf_op jit(solution)/shard_map/ppermute | solution.py:23
  45.7 22.4 %collective-permute-start.2 = (bf16[4,2,128,256]{3,2,1,0:T(8,128)(2,1)S(1)}, bf16[4,2,128,256]{3,2,1,0:T(8,128)(2,1)S(1)}, u32[]{:S(2)}, u32[]{:S(2)}) collective-permute-start(bf16[4,2,128,256]{3,2,1,0:T(8,128)(2,1)S(1)} %get-tuple-element.152), channel_id=1, source_target_pairs={{0,2},{2,0},{1,3},{3,1},{4,6},{6,4},{5,7},{7,5},{8,10},{10,8},{9,1... | collective-permute-start | bytes 1572872 | tf_op jit(solution)/shard_map/ppermute | solution.py:23
  71.0 82.9 %all-gather.15.cloned.1.call-start = ((), (), s32[]{:S(2)}) async-start(), calls=%async_computation.11 | async-start | bytes 1310720 | tf_op jit(solution)/shard_map/all_gather | solution.py:636
  85.6 16.8 %collective-permute-start.12 = (bf16[2,128,1024]{2,1,0:T(8,128)(2,1)}, bf16[2,128,1024]{2,1,0:T(8,128)(2,1)S(1)}, u32[]{:S(2)}, u32[]{:S(2)}) collective-permute-start(bf16[2,128,1024]{2,1,0:T(8,128)(2,1)} %get-tuple-element.149), channel_id=1, source_target_pairs={{0,4},{4,0},{1,5},{5,1},{2,6},{6,2},{3,7},{7,3},{8,12},{12,8},{9,1... | collective-permute-start | bytes 1572872 | tf_op jit(solution)/shard_map/ppermute | solution.py:23
  86.2 16.2 %collective-permute-start.10 = (bf16[2,128,1024]{2,1,0:T(8,128)(2,1)}, bf16[2,128,1024]{2,1,0:T(8,128)(2,1)S(1)}, u32[]{:S(2)}, u32[]{:S(2)}) collective-permute-start(bf16[2,128,1024]{2,1,0:T(8,128)(2,1)} %get-tuple-element.149), channel_id=1, source_target_pairs={{0,2},{2,0},{1,3},{3,1},{4,6},{6,4},{5,7},{7,5},{8,10},{10,8},{9,1... | collective-permute-start | bytes 1572872 | tf_op jit(solution)/shard_map/ppermute | solution.py:23
  87.7 21.4 %collective-permute-start.11 = (bf16[2,128,1024]{2,1,0:T(8,128)(2,1)}, bf16[2,128,1024]{2,1,0:T(8,128)(2,1)}, u32[]{:S(2)}, u32[]{:S(2)}) collective-permute-start(bf16[2,128,1024]{2,1,0:T(8,128)(2,1)} %get-tuple-element.150), channel_id=1, source_target_pairs={{0,4},{4,0},{1,5},{5,1},{2,6},{6,2},{3,7},{7,3},{8,12},{12,8},{9,1... | collective-permute-start | bytes 1572872 | tf_op jit(solution)/shard_map/ppermute | solution.py:23
  89.1 20.1 %collective-permute-start.9 = (bf16[2,128,1024]{2,1,0:T(8,128)(2,1)}, bf16[2,128,1024]{2,1,0:T(8,128)(2,1)S(1)}, u32[]{:S(2)}, u32[]{:S(2)}) collective-permute-start(bf16[2,128,1024]{2,1,0:T(8,128)(2,1)} %get-tuple-element.150), channel_id=1, source_target_pairs={{0,2},{2,0},{1,3},{3,1},{4,6},{6,4},{5,7},{7,5},{8,10},{10,8},{9,1... | collective-permute-start | bytes 1572872 | tf_op jit(solution)/shard_map/ppermute | solution.py:23
  113.0 155.6 %reduce-scatter.9.cloned.1.call-start = ((), (), s32[]{:S(2)}) async-start(), calls=%async_computation.6 | async-start | bytes 1310720 | tf_op jit(solution)/shard_map/reduce_scatter | solution.py:769
  113.1 15.5 %collective-permute-start.17 = (bf16[512,1024]{1,0:T(8,128)(2,1)S(1)}, bf16[512,1024]{1,0:T(8,128)(2,1)}, u32[]{:S(2)}, u32[]{:S(2)}) collective-permute-start(bf16[512,1024]{1,0:T(8,128)(2,1)S(1)} %copy-done.6), channel_id=1, source_target_pairs={{0,1},{1,0},{2,3},{3,2},{4,5},{5,4},{6,7},{7,6},{8,9},{9,8},{10,11... | collective-permute-start | bytes 3145736 | tf_op jit(solution)/shard_map/ppermute | solution.py:23
  126.6 25.0 %collective-permute-start.19 = (bf16[4,1024,128]{2,1,0:T(8,128)(2,1)}, bf16[4,1024,128]{2,1,0:T(8,128)(2,1)S(1)}, u32[]{:S(2)}, u32[]{:S(2)}) collective-permute-start(bf16[4,1024,128]{2,1,0:T(8,128)(2,1)} %bitcast.53), channel_id=1, source_target_pairs={{0,2},{2,0},{1,3},{3,1},{4,6},{6,4},{5,7},{7,5},{8,10},{10,8},{9,1... | collective-permute-start | bytes 3145736 | tf_op jit(solution)/shard_map/ppermute | solution.py:23
  128.0 24.7 %collective-permute-start.18 = (bf16[4,1024,128]{2,1,0:T(8,128)(2,1)}, bf16[4,1024,128]{2,1,0:T(8,128)(2,1)S(1)}, u32[]{:S(2)}, u32[]{:S(2)}) collective-permute-start(bf16[4,1024,128]{2,1,0:T(8,128)(2,1)} %bitcast.54), channel_id=1, source_target_pairs={{0,4},{4,0},{1,5},{5,1},{2,6},{6,2},{3,7},{7,3},{8,12},{12,8},{9,1... | collective-permute-start | bytes 3145736 | tf_op jit(solution)/shard_map/ppermute | solution.py:23
  146.9 138.1 %reduce-scatter.7.cloned.1.call-start = ((), (), s32[]{:S(2)}) async-start(), calls=%async_computation.5 | async-start | bytes 1310720 | tf_op jit(solution)/shard_map/reduce_scatter | solution.py:773
  152.8 24.9 %collective-permute-start.36 = (bf16[4,1024,128]{2,1,0:T(8,128)(2,1)}, bf16[4,1024,128]{2,1,0:T(8,128)(2,1)}, u32[]{:S(2)}, u32[]{:S(2)}) collective-permute-start(bf16[4,1024,128]{2,1,0:T(8,128)(2,1)} %get-tuple-element.146), channel_id=1, source_target_pairs={{0,2},{2,0},{1,3},{3,1},{4,6},{6,4},{5,7},{7,5},{8,10},{10,8},{9,1... | collective-permute-start | bytes 3145736 | tf_op jit(solution)/shard_map/ppermute | solution.py:23
  153.4 24.3 %collective-permute-start.35 = (bf16[4,1024,128]{2,1,0:T(8,128)(2,1)}, bf16[4,1024,128]{2,1,0:T(8,128)(2,1)}, u32[]{:S(2)}, u32[]{:S(2)}) collective-permute-start(bf16[4,1024,128]{2,1,0:T(8,128)(2,1)} %get-tuple-element.144), channel_id=1, source_target_pairs={{0,4},{4,0},{1,5},{5,1},{2,6},{6,2},{3,7},{7,3},{8,12},{12,8},{9,1... | collective-permute-start | bytes 3145736 | tf_op jit(solution)/shard_map/ppermute | solution.py:23
  174.7 14.6 %collective-permute-start.33 = (bf16[2,128,1024]{2,1,0:T(8,128)(2,1)}, bf16[2,128,1024]{2,1,0:T(8,128)(2,1)S(1)}, u32[]{:S(2)}, u32[]{:S(2)}) collective-permute-start(bf16[2,128,1024]{2,1,0:T(8,128)(2,1)} %get-tuple-element.139), channel_id=1, source_target_pairs={{0,2},{2,0},{1,3},{3,1},{4,6},{6,4},{5,7},{7,5},{8,10},{10,8},{9,1... | collective-permute-start | bytes 1572872 | tf_op jit(solution)/shard_map/ppermute | solution.py:23
  176.2 15.1 %collective-permute-start.31 = (bf16[2,128,1024]{2,1,0:T(8,128)(2,1)}, bf16[2,128,1024]{2,1,0:T(8,128)(2,1)}, u32[]{:S(2)}, u32[]{:S(2)}) collective-permute-start(bf16[2,128,1024]{2,1,0:T(8,128)(2,1)} %get-tuple-element.135), channel_id=1, source_target_pairs={{0,4},{4,0},{1,5},{5,1},{2,6},{6,2},{3,7},{7,3},{8,12},{12,8},{9,1... | collective-permute-start | bytes 1572872 | tf_op jit(solution)/shard_map/ppermute | solution.py:23
  181.0 113.6 %reduce-scatter.5.cloned.1.call-start = ((), (), s32[]{:S(2)}) async-start(), calls=%async_computation.4 | async-start | bytes 1310720 | tf_op jit(solution)/shard_map/reduce_scatter | solution.py:647
  191.3 41.4 %collective-permute-start.34 = (bf16[4,128,1024]{2,1,0:T(8,128)(2,1)S(1)}, bf16[4,128,1024]{2,1,0:T(8,128)(2,1)}, u32[]{:S(2)}, u32[]{:S(2)}) collective-permute-start(bf16[4,128,1024]{2,1,0:T(8,128)(2,1)S(1)} %add_convert_fusion.2), channel_id=1, source_target_pairs={{0,4},{4,0},{1,5},{5,1},{2,6},{6,2},{3,7},{7,3},{8,12},{12,8},{9,1... | collective-permute-start | bytes 3145736 | tf_op jit(solution)/shard_map/ppermute | solution.py:23
  194.2 38.6 %collective-permute-start.32 = (bf16[4,128,1024]{2,1,0:T(8,128)(2,1)S(1)}, bf16[4,128,1024]{2,1,0:T(8,128)(2,1)}, u32[]{:S(2)}, u32[]{:S(2)}) collective-permute-start(bf16[4,128,1024]{2,1,0:T(8,128)(2,1)S(1)} %add_convert_fusion.3), channel_id=1, source_target_pairs={{0,2},{2,0},{1,3},{3,1},{4,6},{6,4},{5,7},{7,5},{8,10},{10,8},{9,1... | collective-permute-start | bytes 3145736 | tf_op jit(solution)/shard_map/ppermute | solution.py:23
  214.4 28.4 %collective-permute-start.23 = (bf16[4,4,128,256]{3,2,1,0:T(8,128)(2,1)}, bf16[4,4,128,256]{3,2,1,0:T(8,128)(2,1)S(1)}, u32[]{:S(2)}, u32[]{:S(2)}) collective-permute-start(bf16[4,4,128,256]{3,2,1,0:T(8,128)(2,1)} %get-tuple-element.119), channel_id=1, source_target_pairs={{0,2},{2,0},{1,3},{3,1},{4,6},{6,4},{5,7},{7,5},{8,10},{10,8},{9,1... | collective-permute-start | bytes 3145736 | tf_op jit(solution)/shard_map/ppermute | solution.py:23
  236.4 66.9 %reduce-scatter.11.cloned.1.call-start = ((), (), s32[]{:S(2)}) async-start(), calls=%async_computation.7 | async-start | bytes 1310720 | tf_op jit(solution)/shard_map/reduce_scatter | solution.py:810
  236.7 27.2 %collective-permute-start.22 = (bf16[4,4,128,256]{3,2,1,0:T(8,128)(2,1)}, bf16[4,4,128,256]{3,2,1,0:T(8,128)(2,1)}, u32[]{:S(2)}, u32[]{:S(2)}) collective-permute-start(bf16[4,4,128,256]{3,2,1,0:T(8,128)(2,1)} %get-tuple-element.115), channel_id=1, source_target_pairs={{0,2},{2,0},{1,3},{3,1},{4,6},{6,4},{5,7},{7,5},{8,10},{10,8},{9,1... | collective-permute-start | bytes 3145736 | tf_op jit(solution)/shard_map/ppermute | solution.py:23
  243.1 22.3 %collective-permute-start.24 = (bf16[4,4,128,256]{3,2,1,0:T(8,128)(2,1)S(1)}, bf16[4,4,128,256]{3,2,1,0:T(8,128)(2,1)}, u32[]{:S(2)}, u32[]{:S(2)}) collective-permute-start(bf16[4,4,128,256]{3,2,1,0:T(8,128)(2,1)S(1)} %add_convert_fusion.5), channel_id=1, source_target_pairs={{0,4},{4,0},{1,5},{5,1},{2,6},{6,2},{3,7},{7,3},{8,12},{12,8},{9,1... | collective-permute-start | bytes 3145736 | tf_op jit(solution)/shard_map/ppermute | solution.py:23
  252.6 17.5 %collective-permute-start.26 = (bf16[512,1024]{1,0:T(8,128)(2,1)}, bf16[512,1024]{1,0:T(8,128)(2,1)S(1)}, u32[]{:S(2)}, u32[]{:S(2)}) collective-permute-start(bf16[512,1024]{1,0:T(8,128)(2,1)} %get-tuple-element.123), channel_id=1, source_target_pairs={{0,1},{1,0},{2,3},{3,2},{4,5},{5,4},{6,7},{7,6},{8,9},{9,8},{10,11... | collective-permute-start | bytes 3145736 | tf_op jit(solution)/shard_map/ppermute | solution.py:23
  268.5 18.8 %collective-permute-start.25 = (bf16[512,1024]{1,0:T(8,128)(2,1)S(1)}, bf16[512,1024]{1,0:T(8,128)(2,1)S(1)}, u32[]{:S(2)}, u32[]{:S(2)}) collective-permute-start(bf16[512,1024]{1,0:T(8,128)(2,1)S(1)} %copy-done.33), channel_id=1, source_target_pairs={{0,1},{1,0},{2,3},{3,2},{4,5},{5,4},{6,7},{7,6},{8,9},{9,8},{10,11... | collective-permute-start | bytes 3145736 | tf_op jit(solution)/shard_map/ppermute | solution.py:23
  268.6 16.3 %collective-permute-start.37 = (bf16[1024,128]{1,0:T(8,128)(2,1)}, bf16[1024,128]{1,0:T(8,128)(2,1)S(1)}, u32[]{:S(2)}, u32[]{:S(2)}) collective-permute-start(bf16[1024,128]{1,0:T(8,128)(2,1)} %bitcast.76), channel_id=1, source_target_pairs={{0,6},{2,4},{4,2},{6,0},{1,7},{3,5},{5,3},{7,1},{8,14},{10,12},{12... | collective-permute-start | bytes 786440 | tf_op jit(solution)/shard_map/ppermute | solution.py:27
  (49 other events, 495.3 us)
Sparse Core Ops, SparseCore 0:
  10.2 30.6 all-gather.8
  42.4 27.3 all-gather.10
  71.4 27.4 all-gather.12
  113.1 26.3 all-gather.14
  147.0 26.3 reduce-scatter.8
  181.2 25.6 reduce-scatter.6
  236.5 26.3 reduce-scatter.4
  268.6 26.3 reduce-scatter.10

commit v2 on v1

--- a/solution.py
+++ b/solution.py
@@ -195,7 +195,7 @@
                 part = product(left(block), right)
                 total = part if total is None else total + part
             if here.start < rows:
-                own[here, columns] = total
+                own[here, columns] = total.astype(LOW)
             else:
                 far[here.start - rows : here.stop - rows, columns] = total.astype(LOW)
         if z % 2:
@@ -332,7 +332,7 @@
     if last:
         first_at = ops.add(last[0])
         out_sides = [[ops.side(one) for one in pair] for pair in last[1]]
-        outs += [like((rows, wide), FULL), like((rows, wide), LOW)]
+        outs += [like((rows, wide), LOW), like((rows, wide), LOW)]
 
     def kernel(meta, refs, results, put):
         qkv, context, logs = results[:3]
@@ -357,19 +357,26 @@
     return call(kernel, meta, ops, outs, time=12 if last else 8)
 
 
-def attention_backward(meta, grad, side, qkv, logs, context, normed):
+def attention_backward(meta, grad, side, qkv, logs, context, normed, split):
     ops = Operands()
     grad_at = [ops.add(grad[0])]
-    low, high = [ops.side(one) for one in side]
+    low, high = [[(ops.add(array, ALL, index[1]), (z,)) for z, (array, index) in enumerate(one)] for one in side]
     grad_at.append(ops.add(grad[1]))
     qkv_at, log_at = [ops.add(one) for one in (qkv, logs)]
     normed_at = [ops.add(one) for one in normed]
     context_at = ops.add(context)
     width = context.shape[1]
-    blocks = like((DEEP, 4, LANES, width), LOW)
+    blocks, half = like((DEEP, 4, LANES, width), LOW), like((DEEP // 2, 4, LANES, width), LOW)
+    far = [half, half] if split else [blocks]
 
     def kernel(meta, refs, results, put, grads, key_sum, value_sum):
         out, sums = results[:2]
+
+        def target(place):
+            if place < DEEP or not split:
+                return results[2 + place // DEEP].at[place % DEEP]
+            return results[3 + place // 2 - DEEP // 2].at[place % 2]
+
         low_w = high_w = None
         for here, block in zip(row_slices(), rows_of(refs, grad_at)):
             if low_w is None:
@@ -385,21 +392,23 @@
             for places, columns in chunk_pairs():
                 block = by_tokens(rows_of(refs, normed_at, columns), right)
                 for part, place in enumerate(places):
-                    results[2 + place // DEEP][place % DEEP, which] = block[part * LANES : (part + 1) * LANES, :]
+                    target(place)[which] = block[part * LANES : (part + 1) * LANES, :]
+            for one in range(2, 3 + len(far)):
+                put(one, ALL, which)
         left = [refs[context_at][here, :] for here in row_slices()]
         for places, columns in chunk_pairs():
             block = by_tokens(left, rows_of(refs, grad_at, columns))
             for part, place in enumerate(places):
                 one = block[:, part * LANES : (part + 1) * LANES]
-                results[2 + place // DEEP][place % DEEP, 3] = jnp.concatenate([one[:LANES], one[LANES:]], axis=1)
-        put(2)
-        put(3)
+                target(place)[3] = jnp.concatenate([one[:LANES], one[LANES:]], axis=1)
+        for one in range(2, 3 + len(far)):
+            put(one, ALL, 3)
 
     return call(
         kernel,
         meta,
         ops,
-        [like((3, LENGTH, width), LOW), like((2, width), FULL)] + [blocks] * 2,
+        [like((3, LENGTH, width), LOW), like((2, width), FULL), blocks] + far,
         [pltpu.VMEM((LENGTH, width), LOW)] + [pltpu.VMEM((PAIR, LENGTH), FULL)] * 2,
         time=15,
     )
@@ -460,7 +469,7 @@
     slope_at.append(ops.add(slopes[1]))
     up_at = [[ops.side(one) for one in pair] for pair in up_sides]
     normed_at = [ops.add(one) for one in normed]
-    pair = [like((rows, wide), FULL), like((rows, wide), LOW)]
+    pair = [like((rows, wide), LOW), like((rows, wide), LOW)]
     block, half = like((DEEP, LANES, width), LOW), like((DEEP // 2, LANES, width), LOW)
     outs = [like((1, width), FULL)] * 2 + pair + [block] * 3 + [half] * 2
 
@@ -500,8 +509,9 @@
                     block = by_tokens(rows_of(refs, normed_at, chunks), right)
                     for part, place in enumerate(places):
                         target(place)[:, units] = block[part * LANES : (part + 1) * LANES, :]
-            for one in (6, 7, 8) if x else (4, 5):
-                put(one)
+                if done:
+                    for one in (6, 7, 8) if x else (4, 5):
+                        put(one, ALL, ALL, done)
 
     return call(kernel, meta, ops, outs, [pltpu.VMEM((LENGTH, width), LOW)] * 2, time=20)
 
@@ -518,7 +528,7 @@
         parts = [(left_of(one, at), pick(refs, low, high), product) for one, at, low, high in places]
         spread(meta[1] == 0, parts, *results, put, 0)
 
-    return call(kernel, meta, ops, [like((rows, wide), FULL), like((rows, wide), LOW)], time=6)
+    return call(kernel, meta, ops, [like((rows, wide), LOW), like((rows, wide), LOW)], time=6)
 
 
 STRIP = 128
@@ -578,7 +588,7 @@
 def join_kernel(meta, values, vectors, results, sums):
     tokens, own, got = values
     bias, gain, shift = vectors
-    total = tokens.astype(FULL) + (own + got.astype(FULL)) + bias
+    total = tokens.astype(FULL) + (own.astype(FULL) + got.astype(FULL)) + bias
     hidden, here = results[0]
     hidden[here, :] = total
     hat, _ = normalize(total)
@@ -604,7 +614,7 @@
 
 def second_kernel(meta, values, vectors, results, sums):
     own, got, hidden, pulled = values
-    grad = own + got.astype(FULL)
+    grad = own.astype(FULL) + got.astype(FULL)
     row, gain_part = norm_back(grad, hidden, vectors[0])
     total = pulled + row
     out, here = results[0]
@@ -615,7 +625,7 @@
 
 def first_kernel(meta, values, vectors, results, sums):
     own, got, tokens, hidden_grad = values
-    grad = own + got.astype(FULL)
+    grad = own.astype(FULL) + got.astype(FULL)
     row, gain_part = norm_back(grad, tokens.astype(FULL), vectors[0])
     out, here = results[0]
     out[here, :] = hidden_grad + row
@@ -625,7 +635,7 @@
 def end_kernel(meta, values, vectors, results, sums):
     hidden, own, got = values
     out, here = results[0]
-    out[here, :] = (hidden + (own + got.astype(FULL)) + vectors[0]).astype(LOW)
+    out[here, :] = (hidden + (own.astype(FULL) + got.astype(FULL)) + vectors[0]).astype(LOW)
 
 
 def wide_shard(shard, axis):
@@ -641,6 +651,12 @@
     for value in values[1:]:
         total = total + value.astype(FULL)
     return total.astype(LOW)
+
+
+def add_half(whole, part, which):
+    size = part.shape[0]
+    edges = [(size * which, size * (1 - which), 0)] + [(0, 0, 0)] * (part.ndim - 1)
+    return add(whole, lax.pad(part.astype(FULL), FULL(0), edges))
 
 
 def scatter_deep(total):
@@ -789,15 +805,17 @@
     got_x = swap(add(up_other, lax.pad(got_high, FULL(0), half)), "x")
 
     back, unit_sums = [None] * 2, [None] * 2
-    back[1], unit_sums[1], attn_other_x, attn_both = attention_backward(
-        meta, attn_grad, attn_sides[1][3], qkv[1], logs[1], context[1], normed
-    )
-    got_both = swap(attn_both, "x")
-    attn_got_x = swap(attn_other_x, "x")
+    back[1], unit_sums[1], attn_other, attn_both_low, attn_both_high = attention_backward(
+        meta, attn_grad, attn_sides[1][3], qkv[1], logs[1], context[1], normed, True
+    )
+    attn_low = swap(attn_both_low, "x")
+    attn_high = swap(attn_both_high, "y")
     back[0], unit_sums[0], attn_own, attn_beyond = attention_backward(
-        meta, (after(attn_grad[0], back[1]), attn_grad[1]), attn_sides[0][3], qkv[0], logs[0], context[0], normed
-    )
-    attn_got_y = swap(add(attn_beyond, after(got_both, back[0])), "y")
+        meta, (after(attn_grad[0], back[1]), attn_grad[1]), attn_sides[0][3], qkv[0], logs[0], context[0], normed, False
+    )
+    send_y = add_half(attn_beyond, after(attn_low, back[0]), 0)
+    send_x = add_half(attn_other, after(attn_high, back[0]), 1)
+    attn_got_y, attn_got_x = swap(send_y, "y"), swap(send_x, "x")
     owner_up = scatter_deep(add(up_own, *[after(one, back[0]) for one in (got_x, got_y)]))
     last, last_sent = spread_kernel(
         meta,
@@ -836,8 +854,8 @@
     ]
     got = swap(jnp.concatenate([replicated, far_units]), "x")
     summed = jnp.concatenate([replicated, own_units]) + got
-    summed = all_sum(summed, "y")
-    summed = all_sum(summed, "z", (layer_out,), (owner_up, owner_down))
+    summed = all_sum(summed, "y", (layer_out,))
+    summed = all_sum(summed, "z", (owner_down,), (owner_up,))
     summed = all_sum(summed, "w")
     vectors = summed[: 6 * wide].reshape(6, wide)
     units = summed[6 * wide :]

time: 317 us -> 313 us (0.987)
    ppermute x33 -> x34, waiting for transfers between devices: 52.1 us -> 50.5 us  [swap(): return lax.ppermute(values, axis, SWAP)]
    unnamed x68 -> x74, local copies, waits for them, and re-layouts: 8.29 us -> 6.94 us
    convert_element_type x6 -> x7, other arithmetic: 12.9 us -> 12.6 us  [add(): return total.astype(LOW)]
    ppermute x33 -> x34, starting transfers between devices: 27.6 us -> 27.9 us  [swap(): return lax.ppermute(values, axis, SWAP)]
  transfers between devices with their start and end apart: 47 -> 48, of which waited for: 20 -> 21; matrix products, arithmetic and copies ran while one was open for 8% -> 8% of each run, Pallas kernels for 46% -> 46%
where the time goes in v2:
time: 313 us; the launch traced here: 309 us
  Pallas kernels  142 us (45%)
  waiting for transfers between devices  75 us (24%)
  starting transfers between devices  39.2 us (13%)
  other arithmetic  21.8 us (7%)
  between operations  17.6 us (6%)
  local copies, waits for them, and re-layouts  14.3 us (5%)
    pallas_call x13, Pallas kernels, call(): pl.pallas_call(body, out_shape=outs, in_specs=[pl.BlockSpec(memory_space=...  142 us
    ppermute x34, waiting for transfers between devices, swap(): return lax.ppermute(values, axis, SWAP)  50.5 us
    ppermute x34, starting transfers between devices, swap(): return lax.ppermute(values, axis, SWAP)  27.9 us
    all_gather x4, waiting for transfers between devices, gather_deep(): return lax.all_gather(shard, 'z', axis=0, tiled=False)  15.8 us
    convert_element_type x7, other arithmetic, add(): return total.astype(LOW)  12.6 us
    ppermute x4, waiting for transfers between devices, all_sum(): lax.ppermute(values, axis, [(i, i ^ step) for i in range(size)])  7.82 us
    unnamed x74, local copies, waits for them, and re-layouts  6.94 us
    ppermute x2, starting transfers between devices, swap_both(): return lax.ppermute(values, ('y', 'x'), ((0, 3), (1, 2), (2, 1), (3, 0)))  6.3 us
  transfers between devices with their start and end apart: 48, of which 21 were waited for; matrix products, arithmetic and copies ran while one was open for 8% of the time, Pallas kernels for 46%

profile of v2, /device:TPU:0, one launch (start us, length us, event | category | flops | bytes accessed | tf_op | source)
XLA Modules:
  0.0 309.5 jit_solution(8520805239154870529)
XLA Ops:
  8.0 1.6 pad_maximum_fusion
  10.5 4.0 %collective-permute-start = (bf16[1024,128]{1,0:T(8,128)(2,1)}, bf16[1024,128]{1,0:T(8,128)(2,1)S(1)}, u32[]{:S(2)}, u32[]{:S(2)}) collective-permute-start(bf16[1024,128]{1,0:T(8,128)(2,1)} %param.33), channel_id=1, source_target_pairs={{0,6},{2,4},{4,2},{6,0},{1,7},{3,5},{5,3},{7,1},{8,14},{10,12},{12... | collective-permute-start | bytes 786440 | tf_op jit(solution)/shard_map/ppermute | solution.py:27
  20.3 4.7 %shard_map.305 = (bf16[512,1024]{1,0:T(8,128)(2,1)}, bf16[512,1024]{1,0:T(8,128)(2,1)}) custom-call(s32[6]{0:T(128)} %stack.38.refs_0_, bf16[512,1024]{1,0:T(8,128)(2,1)} %refs_3_.1, f32[512,1024]{1,0:T(8,128)} %refs_4_.1, f32[1,1024]{1,0:T(1,128)} %bitcast.62, f32[1,1024]{1,0:T(1,128)} %bitcast.66), custom_call_target="tpu_custom_call" | custom-call | flops 4194304 | bytes 65536 | tf_op jit(solution)/shard_map/pallas_call | solution.py:110
  25.1 15.8 %all-gather.9.cloned.1.call-done = bf16[16,128,256]{2,1,0:T(8,128)(2,1)} async-done(((bf16[4,128,256]{2,1,0:T(8,128)(2,1)}), bf16[16,128,256]{2,1,0:T(8,128)(2,1)}) %all-gather.9.cloned.1.call-update) | async-done | bytes 1048592 | tf_op jit(solution)/shard_map/all_gather | solution.py:646
  46.3 10.8 %collective-permute-done.5.refs_4_.refs_2_.refs_8_ = bf16[4,2,128,256]{3,2,1,0:T(8,128)(2,1)S(1)} collective-permute-done((bf16[4,2,128,256]{3,2,1,0:T(8,128)(2,1)S(1)}, bf16[4,2,128,256]{3,2,1,0:T(8,128)(2,1)S(1)}, u32[]{:S(2)}, u32[]{:S(2)}) %collective-permute-start.5) | collective-permute-done | bytes 524320 | tf_op jit(solution)/shard_map/ppermute | solution.py:23
  58.5 9.6 %collective-permute-done.3.refs_3_ = bf16[4,2,128,256]{3,2,1,0:T(8,128)(2,1)S(1)} collective-permute-done((bf16[4,2,128,256]{3,2,1,0:T(8,128)(2,1)S(1)}, bf16[4,2,128,256]{3,2,1,0:T(8,128)(2,1)S(1)}, u32[]{:S(2)}, u32[]{:S(2)}) %collective-permute-start.3) | collective-permute-done | bytes 524320 | tf_op jit(solution)/shard_map/ppermute | solution.py:23
  72.3 10.9 %shard_map.306 = (bf16[3,1024,256]{2,1,0:T(8,128)(2,1)}, bf16[1024,256]{1,0:T(8,128)(2,1)}, f32[1024,256]{1,0:T(8,128)}) custom-call(s32[6]{0:T(128)} %stack.38.refs_0_, bf16[512,1024]{1,0:T(8,128)(2,1)} %get-tuple-element.86.refs_1_.refs_7_, bf16[4,4,128,256]{3,2,1,0:T(8,128)(2,1)} %bitcast.46, bf16[4,2,128,256]{3,2,1,0:T(8,128)(2,1)} %copy-done.14, ...), custom_call_target="tpu_custom_call" | custom-call | flops 8388608 | bytes 65536 | tf_op jit(solution)/shard_map/pallas_call | solution.py:110
  88.8 12.5 %shard_map.307 = (bf16[3,1024,256]{2,1,0:T(8,128)(2,1)}, bf16[1024,256]{1,0:T(8,128)(2,1)}, f32[1024,256]{1,0:T(8,128)}, bf16[512,1024]{1,0:T(8,128)(2,1)}, bf16[512,1024]{1,0:T(8,128)(2,1)}) custom-call(s32[6]{0:T(128)} %stack.38.refs_0_, bf16[512,1024]{1,0:T(8,128)(2,1)} %get-tuple-element.86.refs_1_.refs_7_, bf16[4,2,128,256]{3,2,1,0:T(8,128)(2,1)} %copy-done.15, ...), custom_call_target="tpu_custom_call" | custom-call | flops 12582912 | bytes 65536 | tf_op jit(solution)/shard_map/pallas_call | solution.py:110
  101.3 6.6 %collective-permute-done.11.refs_3_.refs_10_ = bf16[2,128,1024]{2,1,0:T(8,128)(2,1)S(1)} collective-permute-done((bf16[2,128,1024]{2,1,0:T(8,128)(2,1)S(1)}, bf16[2,128,1024]{2,1,0:T(8,128)(2,1)S(1)}, u32[]{:S(2)}, u32[]{:S(2)}) %collective-permute-start.11) | collective-permute-done | bytes 524320 | tf_op jit(solution)/shard_map/ppermute | solution.py:23
  111.2 4.9 %shard_map.308 = (f32[512,1024]{1,0:T(8,128)}, bf16[512,1024]{1,0:T(8,128)(2,1)}) custom-call(s32[6]{0:T(128)} %stack.38.refs_0_, bf16[512,1024]{1,0:T(8,128)(2,1)} %refs_3_.1, bf16[512,1024]{1,0:T(8,128)(2,1)} %get-tuple-element.91.refs_2_, bf16[512,1024]{1,0:T(8,128)(2,1)} %collective-permute-done.13.refs_3_, f32[1,1024]{1,0:T(1,128)} %bitcast.67, ...), custom_call_target="tpu_custom_call" | custom-call | flops 4194304 | bytes 65536 | tf_op jit(solution)/shard_map/pallas_call | solution.py:110
  116.2 6.3 %collective-permute-done.15.refs_12_.refs_15_ = bf16[2,128,1024]{2,1,0:T(8,128)(2,1)S(1)} collective-permute-done((bf16[2,128,1024]{2,1,0:T(8,128)(2,1)S(1)}, bf16[2,128,1024]{2,1,0:T(8,128)(2,1)S(1)}, u32[]{:S(2)}, u32[]{:S(2)}) %collective-permute-start.15) | collective-permute-done | bytes 524320 | tf_op jit(solution)/shard_map/ppermute | solution.py:23
  127.2 17.9 %shard_map.309 = (bf16[1024,1024]{1,0:T(8,128)(2,1)}, bf16[1024,1024]{1,0:T(8,128)(2,1)}, bf16[4,1024,128]{2,1,0:T(8,128)(2,1)}, bf16[4,1024,128]{2,1,0:T(8,128)...) custom-call(s32[6]{0:T(128)} %stack.38.refs_0_, ...), custom_call_target="tpu_custom_call" | custom-call | flops 18874368 | bytes 65536 | tf_op jit(solution)/shard_map/pallas_call | solution.py:110
  145.2 4.5 %collective-permute-done.19.refs_6_.refs_5_ = bf16[4,1024,128]{2,1,0:T(8,128)(2,1)S(1)} collective-permute-done((bf16[4,1024,128]{2,1,0:T(8,128)(2,1)}, bf16[4,1024,128]{2,1,0:T(8,128)(2,1)S(1)}, u32[]{:S(2)}, u32[]{:S(2)}) %collective-permute-start.19) | collective-permute-done | bytes 1048608 | tf_op jit(solution)/shard_map/ppermute | solution.py:23
  152.0 20.6 %shard_map.310 = (f32[1,1024]{1,0:T(1,128)}, f32[1,1024]{1,0:T(1,128)}, bf16[512,1024]{1,0:T(8,128)(2,1)}, bf16[512,1024]{1,0:T(8,128)(2,1)}, bf16[4,128,1024]{2...) custom-call(s32[6]{0:T(128)} %stack.38.refs_0_, ...), custom_call_target="tpu_custom_call" | custom-call | flops 20971520 | bytes 65536 | tf_op jit(solution)/shard_map/pallas_call | solution.py:110
  176.0 2.9 add_convert_fusion.3
  180.1 6.4 %shard_map.311 = (f32[512,1024]{1,0:T(8,128)}, bf16[512,1024]{1,0:T(8,128)(2,1)}, f32[4,1024]{1,0:T(4,128)}) custom-call(s32[6]{0:T(128)} %stack.38.refs_0_, bf16[512,1024]{1,0:T(8,128)(2,1)} %get-tuple-element.103.refs_1_, bf16[512,1024]{1,0:T(8,128)(2,1)} %copy-done.23, f32[512,1024]{1,0:T(8,128)} %get-tuple-element.95.refs_3_.refs_1_, ...), custom_call_target="tpu_custom_call" | custom-call | flops 4194304 | bytes 65536 | tf_op jit(solution)/shard_map/pallas_call | solution.py:110
  194.0 17.2 %shard_map.312 = (bf16[3,1024,256]{2,1,0:T(8,128)(2,1)}, f32[2,256]{1,0:T(2,128)}, bf16[4,4,128,256]{3,2,1,0:T(8,128)(2,1)}, bf16[2,4,128,256]{3,2,1,0:T(8,128)(2,1)}, bf16[2,4,128,256]{3,2,1,0:T(8,128)(2,1)}) custom-call(s32[6]{0:T(128)} %stack.38.refs_0_, bf16[512,1024]{1,0:T(8,128)(2,1)} %get-tuple-element.110.refs_1_, ...), custom_call_target="tpu_custom_call" | custom-call | flops 15728640 | bytes 65536 | tf_op jit(solution)/shard_map/pallas_call | solution.py:110
  213.2 16.9 %shard_map.313 = (bf16[3,1024,256]{2,1,0:T(8,128)(2,1)}, f32[2,256]{1,0:T(2,128)}, bf16[4,4,128,256]{3,2,1,0:T(8,128)(2,1)}, bf16[4,4,128,256]{3,2,1,0:T(8,128)(2,1)}) custom-call(s32[6]{0:T(128)} %stack.38.refs_0_, bf16[512,1024]{1,0:T(8,128)(2,1)} %get-tuple-element.110.refs_1_, bf16[4,4,128,256]{3,2,1,0:T(8,128)(2,1)} %bitcast.48, ...), custom_call_target="tpu_custom_call" | custom-call | flops 15728640 | bytes 65536 | tf_op jit(solution)/shard_map/pallas_call | solution.py:110
  230.1 3.6 %add_convert_fusion = bf16[4,128,1024]{2,1,0:T(8,128)(2,1)} fusion(bf16[4,128,1024]{2,1,0:T(8,128)(2,1)} %collective-permute-done.38, bf16[4,128,1024]{2,1,0:T(8,128)(2,1)} %collective-permute-done.36, bf16[4,128,1024]{2,1,0:T(8,128)(2,1)} %get-tuple-element.145), kind=kLoop, calls=%fused_computation | loop fusion | flops 3145728 | bytes 4194304 | tf_op jit(solution)/shard_map/convert_element_type | solution.py:653
  238.4 8.9 %shard_map.316 = (bf16[512,1024]{1,0:T(8,128)(2,1)}, bf16[512,1024]{1,0:T(8,128)(2,1)}) custom-call(s32[6]{0:T(128)} %stack.38.refs_0_, bf16[3,1024,256]{2,1,0:T(8,128)(2,1)} %get-tuple-element.113.refs_1_, bf16[4,4,128,256]{3,2,1,0:T(8,128)(2,1)} %bitcast.49, bf16[4,2,128,256]{3,2,1,0:T(8,128)(2,1)} %copy-done.14, bf16[4,2,128,256]{3,2,1,0:T(8,128)(2,1)} %copy-done.3, ...), custom_call_target="tpu_custom_call" | custom-call | flops 6291456 | bytes 65536 | tf_op jit(solution)/shard_map/pallas_call | solution.py:110
  247.5 10.3 %shard_map.314 = (bf16[512,1024]{1,0:T(8,128)(2,1)}, bf16[512,1024]{1,0:T(8,128)(2,1)}) custom-call(s32[6]{0:T(128)} %stack.38.refs_0_, bf16[1024,1024]{1,0:T(8,128)(2,1)} %get-tuple-element.114.refs_1_, bf16[4,1024,128]{2,1,0:T(8,128)(2,1)} %bitcast.56, bf16[4,1024,128]{2,1,0:T(8,128)(2,1)} %copy-done.7, bf16[1024,1024]{1,0:T(8,128)(2,1)} %get-tuple-element.115.refs_4_, ...), custom_call_target="tpu_custom_call" | custom-call | flops 6291456 | bytes 65536 | tf_op jit(solution)/shard_map/pallas_call | solution.py:110
  257.8 1.8 collective-permute-done.23
  260.2 3.1 %add_convert_fusion.4 = bf16[4,4,128,256]{3,2,1,0:T(8,128)(2,1)} fusion(bf16[4,4,128,256]{3,2,1,0:T(8,128)(2,1)} %collective-permute-done.25, bf16[4,4,128,256]{3,2,1,0:T(8,128)(2,1)} %collective-permute-done.23, bf16[4,4,128,256]{3,2,1,0:T(8,128)(2,1)S(1)} %copy-done.20), kind=kLoop, calls=%fused_computation.4 | loop fusion | flops 3145728 | bytes 4194304 | tf_op jit(solution)/shard_map/convert_element_type | solution.py:653
  263.5 2.3 collective-permute-start.33
  265.9 5.9 %shard_map.317 = (f32[512,1024]{1,0:T(8,128)}, f32[2,1024]{1,0:T(2,128)}) custom-call(s32[6]{0:T(128)} %stack.38.refs_0_, bf16[512,1024]{1,0:T(8,128)(2,1)} %get-tuple-element.127.refs_1_, bf16[512,1024]{1,0:T(8,128)(2,1)} %collective-permute-done.27.refs_2_, bf16[512,1024]{1,0:T(8,128)(2,1)} %refs_3_.1, f32[512,1024]{1,0:T(8,128)} %get-tuple-element.129.refs_4_, ...), custom_call_target="tpu_custom_call" | custom-call | flops 4194304 | bytes 65536 | tf_op jit(solution)/shard_map/pallas_call | solution.py:110
  274.5 3.3 %collective-permute-done.29 = f32[7680]{0:T(1024)S(1)} collective-permute-done((f32[7680]{0:T(1024)S(1)}, f32[7680]{0:T(1024)S(1)}, u32[]{:S(2)}, u32[]{:S(2)}) %collective-permute-start.29) | collective-permute-done | bytes 30752 | tf_op jit(solution)/shard_map/ppermute | solution.py:23
  278.8 4.6 %shard_map.315 = bf16[512,1024]{1,0:T(8,128)(2,1)} custom-call(s32[6]{0:T(128)} %stack.38.refs_0_, f32[512,1024]{1,0:T(8,128)} %get-tuple-element.95.refs_3_.refs_1_, bf16[512,1024]{1,0:T(8,128)(2,1)} %get-tuple-element.126.refs_2_, bf16[512,1024]{1,0:T(8,128)(2,1)} %copy-done.22, f32[1,1024]{1,0:T(1,128)} %bitcast.69), custom_call_target="tpu_custom_call" | custom-call | flops 4194304 | bytes 65536 | tf_op jit(solution)/shard_map/pallas_call | solution.py:110
  284.1 1.8 convert_add_fusion
  288.7 2.6 collective-permute-done.34
  291.4 1.8 bitcast_convert_fusion
  293.2 2.2 collective-permute-start.39
  295.3 2.6 collective-permute-done.39
  (195 shorter events, 63.0 us)
Async XLA Ops:
  7.2 33.7 %all-gather.9.cloned.1.call-start = ((), (), s32[]{:S(2)}) async-start(), calls=%async_computation.8 | async-start | bytes 1310720 | tf_op jit(solution)/shard_map/all_gather | solution.py:646
  9.7 73.4 %all-gather.11.cloned.1.call-start = ((), (), s32[]{:S(2)}) async-start(), calls=%async_computation.9 | async-start | bytes 1310720 | tf_op jit(solution)/shard_map/all_gather | solution.py:646
  10.5 113.3 %all-gather.13.cloned.1.call-start = ((), (), s32[]{:S(2)}) async-start(), calls=%async_computation.10 | async-start | bytes 1310720 | tf_op jit(solution)/shard_map/all_gather | solution.py:646
  10.5 14.5 %collective-permute-start = (bf16[1024,128]{1,0:T(8,128)(2,1)}, bf16[1024,128]{1,0:T(8,128)(2,1)S(1)}, u32[]{:S(2)}, u32[]{:S(2)}) collective-permute-start(bf16[1024,128]{1,0:T(8,128)(2,1)} %param.33), channel_id=1, source_target_pairs={{0,6},{2,4},{4,2},{6,0},{1,7},{3,5},{5,3},{7,1},{8,14},{10,12},{12... | collective-permute-start | bytes 786440 | tf_op jit(solution)/shard_map/ppermute | solution.py:27
  24.9 46.3 %collective-permute-start.8 = (bf16[512,1024]{1,0:T(8,128)(2,1)}, bf16[512,1024]{1,0:T(8,128)(2,1)S(1)}, u32[]{:S(2)}, u32[]{:S(2)}) collective-permute-start(bf16[512,1024]{1,0:T(8,128)(2,1)} %get-tuple-element.86.refs_1_.refs_7_), channel_id=1, source_target_pairs={{0,1},{1,0},{2,3},{3,2},{4,5},{5,4},{6,7},{7,6},{8,9},{9,8},{10,11... | collective-permute-start | bytes 3145736 | tf_op jit(solution)/shard_map/ppermute | solution.py:23
  42.1 14.9 %collective-permute-start.5 = (bf16[4,2,128,256]{3,2,1,0:T(8,128)(2,1)S(1)}, bf16[4,2,128,256]{3,2,1,0:T(8,128)(2,1)S(1)}, u32[]{:S(2)}, u32[]{:S(2)}) collective-permute-start(bf16[4,2,128,256]{3,2,1,0:T(8,128)(2,1)S(1)} %get-tuple-element.157), channel_id=1, source_target_pairs={{0,2},{2,0},{1,3},{3,1},{4,6},{6,4},{5,7},{7,5},{8,10},{10,8},{9,1... | collective-permute-start | bytes 1572872 | tf_op jit(solution)/shard_map/ppermute | solution.py:23
  43.7 14.9 %collective-permute-start.4 = (bf16[4,2,128,256]{3,2,1,0:T(8,128)(2,1)S(1)}, bf16[4,2,128,256]{3,2,1,0:T(8,128)(2,1)S(1)}, u32[]{:S(2)}, u32[]{:S(2)}) collective-permute-start(bf16[4,2,128,256]{3,2,1,0:T(8,128)(2,1)S(1)} %get-tuple-element.157), channel_id=1, source_target_pairs={{0,4},{4,0},{1,5},{5,1},{2,6},{6,2},{3,7},{7,3},{8,12},{12,8},{9,1... | collective-permute-start | bytes 1572872 | tf_op jit(solution)/shard_map/ppermute | solution.py:23
  45.1 23.0 %collective-permute-start.3 = (bf16[4,2,128,256]{3,2,1,0:T(8,128)(2,1)S(1)}, bf16[4,2,128,256]{3,2,1,0:T(8,128)(2,1)S(1)}, u32[]{:S(2)}, u32[]{:S(2)}) collective-permute-start(bf16[4,2,128,256]{3,2,1,0:T(8,128)(2,1)S(1)} %get-tuple-element.158), channel_id=1, source_target_pairs={{0,4},{4,0},{1,5},{5,1},{2,6},{6,2},{3,7},{7,3},{8,12},{12,8},{9,1... | collective-permute-start | bytes 1572872 | tf_op jit(solution)/shard_map/ppermute | solution.py:23
  45.7 22.4 %collective-permute-start.2 = (bf16[4,2,128,256]{3,2,1,0:T(8,128)(2,1)S(1)}, bf16[4,2,128,256]{3,2,1,0:T(8,128)(2,1)S(1)}, u32[]{:S(2)}, u32[]{:S(2)}) collective-permute-start(bf16[4,2,128,256]{3,2,1,0:T(8,128)(2,1)S(1)} %get-tuple-element.158), channel_id=1, source_target_pairs={{0,2},{2,0},{1,3},{3,1},{4,6},{6,4},{5,7},{7,5},{8,10},{10,8},{9,1... | collective-permute-start | bytes 1572872 | tf_op jit(solution)/shard_map/ppermute | solution.py:23
  71.0 80.9 %all-gather.15.cloned.1.call-start = ((), (), s32[]{:S(2)}) async-start(), calls=%async_computation.11 | async-start | bytes 1310720 | tf_op jit(solution)/shard_map/all_gather | solution.py:646
  84.7 16.6 %collective-permute-start.12 = (bf16[2,128,1024]{2,1,0:T(8,128)(2,1)S(1)}, bf16[2,128,1024]{2,1,0:T(8,128)(2,1)}, u32[]{:S(2)}, u32[]{:S(2)}) collective-permute-start(bf16[2,128,1024]{2,1,0:T(8,128)(2,1)S(1)} %get-tuple-element.155), channel_id=1, source_target_pairs={{0,4},{4,0},{1,5},{5,1},{2,6},{6,2},{3,7},{7,3},{8,12},{12,8},{9,1... | collective-permute-start | bytes 1572872 | tf_op jit(solution)/shard_map/ppermute | solution.py:23
  85.3 16.0 %collective-permute-start.10 = (bf16[2,128,1024]{2,1,0:T(8,128)(2,1)S(1)}, bf16[2,128,1024]{2,1,0:T(8,128)(2,1)S(1)}, u32[]{:S(2)}, u32[]{:S(2)}) collective-permute-start(bf16[2,128,1024]{2,1,0:T(8,128)(2,1)S(1)} %get-tuple-element.155), channel_id=1, source_target_pairs={{0,2},{2,0},{1,3},{3,1},{4,6},{6,4},{5,7},{7,5},{8,10},{10,8},{9,1... | collective-permute-start | bytes 1572872 | tf_op jit(solution)/shard_map/ppermute | solution.py:23
  86.8 21.1 %collective-permute-start.11 = (bf16[2,128,1024]{2,1,0:T(8,128)(2,1)S(1)}, bf16[2,128,1024]{2,1,0:T(8,128)(2,1)S(1)}, u32[]{:S(2)}, u32[]{:S(2)}) collective-permute-start(bf16[2,128,1024]{2,1,0:T(8,128)(2,1)S(1)} %get-tuple-element.156), channel_id=1, source_target_pairs={{0,4},{4,0},{1,5},{5,1},{2,6},{6,2},{3,7},{7,3},{8,12},{12,8},{9,1... | collective-permute-start | bytes 1572872 | tf_op jit(solution)/shard_map/ppermute | solution.py:23
  88.3 19.9 %collective-permute-start.9 = (bf16[2,128,1024]{2,1,0:T(8,128)(2,1)S(1)}, bf16[2,128,1024]{2,1,0:T(8,128)(2,1)S(1)}, u32[]{:S(2)}, u32[]{:S(2)}) collective-permute-start(bf16[2,128,1024]{2,1,0:T(8,128)(2,1)S(1)} %get-tuple-element.156), channel_id=1, source_target_pairs={{0,2},{2,0},{1,3},{3,1},{4,6},{6,4},{5,7},{7,5},{8,10},{10,8},{9,1... | collective-permute-start | bytes 1572872 | tf_op jit(solution)/shard_map/ppermute | solution.py:23
  111.1 152.4 %reduce-scatter.7.cloned.1.call-start = ((), (), s32[]{:S(2)}) async-start(), calls=%async_computation.5 | async-start | bytes 1310720 | tf_op jit(solution)/shard_map/reduce_scatter | solution.py:785
  111.2 15.1 %collective-permute-start.17 = (bf16[512,1024]{1,0:T(8,128)(2,1)}, bf16[512,1024]{1,0:T(8,128)(2,1)S(1)}, u32[]{:S(2)}, u32[]{:S(2)}) collective-permute-start(bf16[512,1024]{1,0:T(8,128)(2,1)} %get-tuple-element.98.refs_7_.refs_1_), channel_id=1, source_target_pairs={{0,1},{1,0},{2,3},{3,2},{4,5},{5,4},{6,7},{7,6},{8,9},{9,8},{10,11... | collective-permute-start | bytes 3145736 | tf_op jit(solution)/shard_map/ppermute | solution.py:23
  123.8 25.8 %collective-permute-start.19 = (bf16[4,1024,128]{2,1,0:T(8,128)(2,1)}, bf16[4,1024,128]{2,1,0:T(8,128)(2,1)S(1)}, u32[]{:S(2)}, u32[]{:S(2)}) collective-permute-start(bf16[4,1024,128]{2,1,0:T(8,128)(2,1)} %bitcast.53), channel_id=1, source_target_pairs={{0,2},{2,0},{1,3},{3,1},{4,6},{6,4},{5,7},{7,5},{8,10},{10,8},{9,1... | collective-permute-start | bytes 3145736 | tf_op jit(solution)/shard_map/ppermute | solution.py:23
  125.3 25.5 %collective-permute-start.18 = (bf16[4,1024,128]{2,1,0:T(8,128)(2,1)}, bf16[4,1024,128]{2,1,0:T(8,128)(2,1)S(1)}, u32[]{:S(2)}, u32[]{:S(2)}) collective-permute-start(bf16[4,1024,128]{2,1,0:T(8,128)(2,1)} %bitcast.54), channel_id=1, source_target_pairs={{0,4},{4,0},{1,5},{5,1},{2,6},{6,2},{3,7},{7,3},{8,12},{12,8},{9,1... | collective-permute-start | bytes 3145736 | tf_op jit(solution)/shard_map/ppermute | solution.py:23
  145.1 138.9 %reduce-scatter.5.cloned.1.call-start = ((), (), s32[]{:S(2)}) async-start(), calls=%async_computation.4 | async-start | bytes 1310720 | tf_op jit(solution)/shard_map/reduce_scatter | solution.py:789
  150.8 24.8 %collective-permute-start.32 = (bf16[4,1024,128]{2,1,0:T(8,128)(2,1)}, bf16[4,1024,128]{2,1,0:T(8,128)(2,1)}, u32[]{:S(2)}, u32[]{:S(2)}) collective-permute-start(bf16[4,1024,128]{2,1,0:T(8,128)(2,1)} %get-tuple-element.142), channel_id=1, source_target_pairs={{0,2},{2,0},{1,3},{3,1},{4,6},{6,4},{5,7},{7,5},{8,10},{10,8},{9,1... | collective-permute-start | bytes 3145736 | tf_op jit(solution)/shard_map/ppermute | solution.py:23
  151.4 24.6 %collective-permute-start.31 = (bf16[4,1024,128]{2,1,0:T(8,128)(2,1)}, bf16[4,1024,128]{2,1,0:T(8,128)(2,1)}, u32[]{:S(2)}, u32[]{:S(2)}) collective-permute-start(bf16[4,1024,128]{2,1,0:T(8,128)(2,1)} %get-tuple-element.140), channel_id=1, source_target_pairs={{0,4},{4,0},{1,5},{5,1},{2,6},{6,2},{3,7},{7,3},{8,12},{12,8},{9,1... | collective-permute-start | bytes 3145736 | tf_op jit(solution)/shard_map/ppermute | solution.py:23
  172.6 14.7 %collective-permute-start.37 = (bf16[2,128,1024]{2,1,0:T(8,128)(2,1)}, bf16[2,128,1024]{2,1,0:T(8,128)(2,1)}, u32[]{:S(2)}, u32[]{:S(2)}) collective-permute-start(bf16[2,128,1024]{2,1,0:T(8,128)(2,1)} %get-tuple-element.151), channel_id=1, source_target_pairs={{0,2},{2,0},{1,3},{3,1},{4,6},{6,4},{5,7},{7,5},{8,10},{10,8},{9,1... | collective-permute-start | bytes 1572872 | tf_op jit(solution)/shard_map/ppermute | solution.py:23
  179.0 112.4 %reduce-scatter.9.cloned.1.call-start = ((), (), s32[]{:S(2)}) async-start(), calls=%async_computation.6 | async-start | bytes 1310720 | tf_op jit(solution)/shard_map/reduce_scatter | solution.py:663
  190.5 39.6 %collective-permute-start.38 = (bf16[4,128,1024]{2,1,0:T(8,128)(2,1)S(1)}, bf16[4,128,1024]{2,1,0:T(8,128)(2,1)}, u32[]{:S(2)}, u32[]{:S(2)}) collective-permute-start(bf16[4,128,1024]{2,1,0:T(8,128)(2,1)S(1)} %add_convert_fusion.1), channel_id=1, source_target_pairs={{0,4},{4,0},{1,5},{5,1},{2,6},{6,2},{3,7},{7,3},{8,12},{12,8},{9,1... | collective-permute-start | bytes 3145736 | tf_op jit(solution)/shard_map/ppermute | solution.py:23
  192.3 37.8 %collective-permute-start.36 = (bf16[4,128,1024]{2,1,0:T(8,128)(2,1)S(1)}, bf16[4,128,1024]{2,1,0:T(8,128)(2,1)}, u32[]{:S(2)}, u32[]{:S(2)}) collective-permute-start(bf16[4,128,1024]{2,1,0:T(8,128)(2,1)S(1)} %add_convert_fusion.2), channel_id=1, source_target_pairs={{0,2},{2,0},{1,3},{3,1},{4,6},{6,4},{5,7},{7,5},{8,10},{10,8},{9,1... | collective-permute-start | bytes 3145736 | tf_op jit(solution)/shard_map/ppermute | solution.py:23
  211.1 22.8 %collective-permute-start.22 = (bf16[2,4,128,256]{3,2,1,0:T(8,128)(2,1)}, bf16[2,4,128,256]{3,2,1,0:T(8,128)(2,1)}, u32[]{:S(2)}, u32[]{:S(2)}) collective-permute-start(bf16[2,4,128,256]{3,2,1,0:T(8,128)(2,1)} %get-tuple-element.119), channel_id=1, source_target_pairs={{0,4},{4,0},{1,5},{5,1},{2,6},{6,2},{3,7},{7,3},{8,12},{12,8},{9,1... | collective-permute-start | bytes 1572872 | tf_op jit(solution)/shard_map/ppermute | solution.py:23
  211.7 22.3 %collective-permute-start.24 = (bf16[2,4,128,256]{3,2,1,0:T(8,128)(2,1)}, bf16[2,4,128,256]{3,2,1,0:T(8,128)(2,1)S(1)}, u32[]{:S(2)}, u32[]{:S(2)}) collective-permute-start(bf16[2,4,128,256]{3,2,1,0:T(8,128)(2,1)} %get-tuple-element.124), channel_id=1, source_target_pairs={{0,2},{2,0},{1,3},{3,1},{4,6},{6,4},{5,7},{7,5},{8,10},{10,8},{9,1... | collective-permute-start | bytes 1572872 | tf_op jit(solution)/shard_map/ppermute | solution.py:23
  233.7 65.4 %reduce-scatter.11.cloned.1.call-start = ((), (), s32[]{:S(2)}) async-start(), calls=%async_computation.7 | async-start | bytes 1310720 | tf_op jit(solution)/shard_map/reduce_scatter | solution.py:828
  236.0 23.6 %collective-permute-start.23 = (bf16[4,4,128,256]{3,2,1,0:T(8,128)(2,1)S(1)}, bf16[4,4,128,256]{3,2,1,0:T(8,128)(2,1)}, u32[]{:S(2)}, u32[]{:S(2)}) collective-permute-start(bf16[4,4,128,256]{3,2,1,0:T(8,128)(2,1)S(1)} %add_convert_fusion.6), channel_id=1, source_target_pairs={{0,2},{2,0},{1,3},{3,1},{4,6},{6,4},{5,7},{7,5},{8,10},{10,8},{9,1... | collective-permute-start | bytes 3145736 | tf_op jit(solution)/shard_map/ppermute | solution.py:23
  236.9 23.4 %collective-permute-start.25 = (bf16[4,4,128,256]{3,2,1,0:T(8,128)(2,1)S(1)}, bf16[4,4,128,256]{3,2,1,0:T(8,128)(2,1)}, u32[]{:S(2)}, u32[]{:S(2)}) collective-permute-start(bf16[4,4,128,256]{3,2,1,0:T(8,128)(2,1)S(1)} %add_convert_fusion.5), channel_id=1, source_target_pairs={{0,4},{4,0},{1,5},{5,1},{2,6},{6,2},{3,7},{7,3},{8,12},{12,8},{9,1... | collective-permute-start | bytes 3145736 | tf_op jit(solution)/shard_map/ppermute | solution.py:23
  247.4 18.5 %collective-permute-start.27 = (bf16[512,1024]{1,0:T(8,128)(2,1)}, bf16[512,1024]{1,0:T(8,128)(2,1)}, u32[]{:S(2)}, u32[]{:S(2)}) collective-permute-start(bf16[512,1024]{1,0:T(8,128)(2,1)} %get-tuple-element.128), channel_id=1, source_target_pairs={{0,1},{1,0},{2,3},{3,2},{4,5},{5,4},{6,7},{7,6},{8,9},{9,8},{10,11... | collective-permute-start | bytes 3145736 | tf_op jit(solution)/shard_map/ppermute | solution.py:23
  263.5 20.5 %collective-permute-start.33 = (bf16[1024,128]{1,0:T(8,128)(2,1)}, bf16[1024,128]{1,0:T(8,128)(2,1)S(1)}, u32[]{:S(2)}, u32[]{:S(2)}) collective-permute-start(bf16[1024,128]{1,0:T(8,128)(2,1)} %bitcast.76), channel_id=1, source_target_pairs={{0,6},{2,4},{4,2},{6,0},{1,7},{3,5},{5,3},{7,1},{8,14},{10,12},{12... | collective-permute-start | bytes 786440 | tf_op jit(solution)/shard_map/ppermute | solution.py:27
  (53 other events, 535.3 us)
Sparse Core Ops, SparseCore 0:
  10.2 30.6 all-gather.8
  42.4 27.3 all-gather.10
  71.4 27.4 all-gather.12
  111.2 26.3 all-gather.14
  145.3 26.1 reduce-scatter.6
  179.1 26.2 reduce-scatter.4
  233.8 26.4 reduce-scatter.8
  263.5 27.1 reduce-scatter.10

commit v3 on v2

--- a/solution.py
+++ b/solution.py
@@ -548,27 +548,27 @@
 def by_strips(kernel, meta, arrays, vectors, outs, sums=0):
     ops = Operands()
     rows, wide = arrays[0].shape
-    halves = [slice(0, rows // 2), slice(rows // 2, rows)]
-    first = [ops.add(array, halves[0]) for array in arrays]
+    pieces = [slice(0, STRIP), slice(STRIP, rows - STRIP), slice(rows - STRIP, rows)]
+    first = [ops.add(array, pieces[0]) for array in arrays]
     vector_at = [ops.add(one) for one in vectors]
-    places = [first, [ops.add(array, halves[1]) for array in arrays]]
+    places = [first] + [[ops.add(array, piece) for array in arrays] for piece in pieces[1:]]
     shapes = [like((rows, wide), kind) for kind in outs]
     if sums:
         shapes.append(like((sums, wide), FULL))
 
     def body(meta, refs, results, put):
         parts = [None] * sums
-        for at, half in zip(places, halves):
-            for here in strips(rows // 2):
+        for at, piece in zip(places, pieces):
+            for here in strips(piece.stop - piece.start):
                 kernel(
                     meta,
                     [refs[one][here, :] for one in at],
                     [refs[one][...] for one in vector_at],
-                    [(result, slice(half.start + here.start, half.start + here.stop)) for result in results[: len(outs)]],
+                    [(result, slice(piece.start + here.start, piece.start + here.stop)) for result in results[: len(outs)]],
                     parts,
                 )
             for one in range(len(outs)):
-                put(one, half)
+                put(one, piece)
         if sums:
             for at, value in enumerate(parts):
                 results[-1][at : at + 1, :] = jnp.sum(value, axis=0, keepdims=True)

time: 313 us -> 313 us (level)
  no operation moved by 1% of the time
where the time goes in v3:
time: 313 us; the launch traced here: 309 us
  Pallas kernels  141 us (45%)
  waiting for transfers between devices  75.2 us (24%)
  starting transfers between devices  39.3 us (13%)
  other arithmetic  21.8 us (7%)
  between operations  17.6 us (6%)
  local copies, waits for them, and re-layouts  14.3 us (5%)
    pallas_call x13, Pallas kernels, call(): pl.pallas_call(body, out_shape=outs, in_specs=[pl.BlockSpec(memory_space=...  141 us
    ppermute x34, waiting for transfers between devices, swap(): return lax.ppermute(values, axis, SWAP)  50.6 us
    ppermute x34, starting transfers between devices, swap(): return lax.ppermute(values, axis, SWAP)  27.9 us
    all_gather x4, waiting for transfers between devices, gather_deep(): return lax.all_gather(shard, 'z', axis=0, tiled=False)  15.9 us
    convert_element_type x7, other arithmetic, add(): return total.astype(LOW)  12.6 us
    ppermute x4, waiting for transfers between devices, all_sum(): lax.ppermute(values, axis, [(i, i ^ step) for i in range(size)])  7.83 us
    unnamed x74, local copies, waits for them, and re-layouts  6.96 us
    ppermute x2, starting transfers between devices, swap_both(): return lax.ppermute(values, ('y', 'x'), ((0, 3), (1, 2), (2, 1), (3, 0)))  6.4 us
  transfers between devices with their start and end apart: 48, of which 21 were waited for; matrix products, arithmetic and copies ran while one was open for 8% of the time, Pallas kernels for 46%

profile of v3, /device:TPU:0, one launch (start us, length us, event | category | flops | bytes accessed | tf_op | source)
XLA Modules:
  0.0 309.2 jit_solution(5961039312867956165)
XLA Ops:
  8.0 1.6 pad_maximum_fusion
  10.5 4.0 %collective-permute-start = (bf16[1024,128]{1,0:T(8,128)(2,1)}, bf16[1024,128]{1,0:T(8,128)(2,1)S(1)}, u32[]{:S(2)}, u32[]{:S(2)}) collective-permute-start(bf16[1024,128]{1,0:T(8,128)(2,1)} %param.33), channel_id=1, source_target_pairs={{0,6},{2,4},{4,2},{6,0},{1,7},{3,5},{5,3},{7,1},{8,14},{10,12},{12... | collective-permute-start | bytes 786440 | tf_op jit(solution)/shard_map/ppermute | solution.py:27
  20.3 4.6 %shard_map.305 = (bf16[512,1024]{1,0:T(8,128)(2,1)}, bf16[512,1024]{1,0:T(8,128)(2,1)}) custom-call(s32[6]{0:T(128)} %stack.38.refs_0_, bf16[512,1024]{1,0:T(8,128)(2,1)} %refs_3_.1, f32[512,1024]{1,0:T(8,128)} %refs_4_.1, f32[1,1024]{1,0:T(1,128)} %bitcast.62, f32[1,1024]{1,0:T(1,128)} %bitcast.66), custom_call_target="tpu_custom_call" | custom-call | flops 4194304 | bytes 65536 | tf_op jit(solution)/shard_map/pallas_call | solution.py:110
  25.0 15.9 %all-gather.9.cloned.1.call-done = bf16[16,128,256]{2,1,0:T(8,128)(2,1)} async-done(((bf16[4,128,256]{2,1,0:T(8,128)(2,1)}), bf16[16,128,256]{2,1,0:T(8,128)(2,1)}) %all-gather.9.cloned.1.call-update) | async-done | bytes 1048592 | tf_op jit(solution)/shard_map/all_gather | solution.py:646
  46.3 10.8 %collective-permute-done.5.refs_4_.refs_2_.refs_8_ = bf16[4,2,128,256]{3,2,1,0:T(8,128)(2,1)S(1)} collective-permute-done((bf16[4,2,128,256]{3,2,1,0:T(8,128)(2,1)S(1)}, bf16[4,2,128,256]{3,2,1,0:T(8,128)(2,1)S(1)}, u32[]{:S(2)}, u32[]{:S(2)}) %collective-permute-start.5) | collective-permute-done | bytes 524320 | tf_op jit(solution)/shard_map/ppermute | solution.py:23
  58.5 9.6 %collective-permute-done.3.refs_3_ = bf16[4,2,128,256]{3,2,1,0:T(8,128)(2,1)S(1)} collective-permute-done((bf16[4,2,128,256]{3,2,1,0:T(8,128)(2,1)S(1)}, bf16[4,2,128,256]{3,2,1,0:T(8,128)(2,1)S(1)}, u32[]{:S(2)}, u32[]{:S(2)}) %collective-permute-start.3) | collective-permute-done | bytes 524320 | tf_op jit(solution)/shard_map/ppermute | solution.py:23
  72.3 10.9 %shard_map.306 = (bf16[3,1024,256]{2,1,0:T(8,128)(2,1)}, bf16[1024,256]{1,0:T(8,128)(2,1)}, f32[1024,256]{1,0:T(8,128)}) custom-call(s32[6]{0:T(128)} %stack.38.refs_0_, bf16[512,1024]{1,0:T(8,128)(2,1)} %get-tuple-element.86.refs_1_.refs_7_, bf16[4,4,128,256]{3,2,1,0:T(8,128)(2,1)} %bitcast.46, bf16[4,2,128,256]{3,2,1,0:T(8,128)(2,1)} %copy-done.14, ...), custom_call_target="tpu_custom_call" | custom-call | flops 8388608 | bytes 65536 | tf_op jit(solution)/shard_map/pallas_call | solution.py:110
  88.8 12.5 %shard_map.307 = (bf16[3,1024,256]{2,1,0:T(8,128)(2,1)}, bf16[1024,256]{1,0:T(8,128)(2,1)}, f32[1024,256]{1,0:T(8,128)}, bf16[512,1024]{1,0:T(8,128)(2,1)}, bf16[512,1024]{1,0:T(8,128)(2,1)}) custom-call(s32[6]{0:T(128)} %stack.38.refs_0_, bf16[512,1024]{1,0:T(8,128)(2,1)} %get-tuple-element.86.refs_1_.refs_7_, bf16[4,2,128,256]{3,2,1,0:T(8,128)(2,1)} %copy-done.15, ...), custom_call_target="tpu_custom_call" | custom-call | flops 12582912 | bytes 65536 | tf_op jit(solution)/shard_map/pallas_call | solution.py:110
  101.3 6.6 %collective-permute-done.11.refs_3_.refs_10_ = bf16[2,128,1024]{2,1,0:T(8,128)(2,1)S(1)} collective-permute-done((bf16[2,128,1024]{2,1,0:T(8,128)(2,1)S(1)}, bf16[2,128,1024]{2,1,0:T(8,128)(2,1)S(1)}, u32[]{:S(2)}, u32[]{:S(2)}) %collective-permute-start.11) | collective-permute-done | bytes 524320 | tf_op jit(solution)/shard_map/ppermute | solution.py:23
  111.3 4.8 %shard_map.308 = (f32[512,1024]{1,0:T(8,128)}, bf16[512,1024]{1,0:T(8,128)(2,1)}) custom-call(s32[6]{0:T(128)} %stack.38.refs_0_, bf16[512,1024]{1,0:T(8,128)(2,1)} %refs_3_.1, bf16[512,1024]{1,0:T(8,128)(2,1)} %get-tuple-element.91.refs_2_, bf16[512,1024]{1,0:T(8,128)(2,1)} %collective-permute-done.13.refs_3_, f32[1,1024]{1,0:T(1,128)} %bitcast.67, ...), custom_call_target="tpu_custom_call" | custom-call | flops 4194304 | bytes 65536 | tf_op jit(solution)/shard_map/pallas_call | solution.py:110
  116.1 6.4 %collective-permute-done.15.refs_12_.refs_15_ = bf16[2,128,1024]{2,1,0:T(8,128)(2,1)S(1)} collective-permute-done((bf16[2,128,1024]{2,1,0:T(8,128)(2,1)S(1)}, bf16[2,128,1024]{2,1,0:T(8,128)(2,1)S(1)}, u32[]{:S(2)}, u32[]{:S(2)}) %collective-permute-start.15) | collective-permute-done | bytes 524320 | tf_op jit(solution)/shard_map/ppermute | solution.py:23
  127.3 17.9 %shard_map.309 = (bf16[1024,1024]{1,0:T(8,128)(2,1)}, bf16[1024,1024]{1,0:T(8,128)(2,1)}, bf16[4,1024,128]{2,1,0:T(8,128)(2,1)}, bf16[4,1024,128]{2,1,0:T(8,128)...) custom-call(s32[6]{0:T(128)} %stack.38.refs_0_, ...), custom_call_target="tpu_custom_call" | custom-call | flops 18874368 | bytes 65536 | tf_op jit(solution)/shard_map/pallas_call | solution.py:110
  145.2 4.5 %collective-permute-done.19.refs_6_.refs_5_ = bf16[4,1024,128]{2,1,0:T(8,128)(2,1)S(1)} collective-permute-done((bf16[4,1024,128]{2,1,0:T(8,128)(2,1)}, bf16[4,1024,128]{2,1,0:T(8,128)(2,1)S(1)}, u32[]{:S(2)}, u32[]{:S(2)}) %collective-permute-start.19) | collective-permute-done | bytes 1048608 | tf_op jit(solution)/shard_map/ppermute | solution.py:23
  152.0 20.6 %shard_map.310 = (f32[1,1024]{1,0:T(1,128)}, f32[1,1024]{1,0:T(1,128)}, bf16[512,1024]{1,0:T(8,128)(2,1)}, bf16[512,1024]{1,0:T(8,128)(2,1)}, bf16[4,128,1024]{2...) custom-call(s32[6]{0:T(128)} %stack.38.refs_0_, ...), custom_call_target="tpu_custom_call" | custom-call | flops 20971520 | bytes 65536 | tf_op jit(solution)/shard_map/pallas_call | solution.py:110
  176.0 2.9 add_convert_fusion.3
  180.1 6.2 %shard_map.311 = (f32[512,1024]{1,0:T(8,128)}, bf16[512,1024]{1,0:T(8,128)(2,1)}, f32[4,1024]{1,0:T(4,128)}) custom-call(s32[6]{0:T(128)} %stack.38.refs_0_, bf16[512,1024]{1,0:T(8,128)(2,1)} %get-tuple-element.103.refs_1_, bf16[512,1024]{1,0:T(8,128)(2,1)} %copy-done.23, f32[512,1024]{1,0:T(8,128)} %get-tuple-element.95.refs_3_.refs_1_, ...), custom_call_target="tpu_custom_call" | custom-call | flops 4194304 | bytes 65536 | tf_op jit(solution)/shard_map/pallas_call | solution.py:110
  194.0 17.2 %shard_map.312 = (bf16[3,1024,256]{2,1,0:T(8,128)(2,1)}, f32[2,256]{1,0:T(2,128)}, bf16[4,4,128,256]{3,2,1,0:T(8,128)(2,1)}, bf16[2,4,128,256]{3,2,1,0:T(8,128)(2,1)}, bf16[2,4,128,256]{3,2,1,0:T(8,128)(2,1)}) custom-call(s32[6]{0:T(128)} %stack.38.refs_0_, bf16[512,1024]{1,0:T(8,128)(2,1)} %get-tuple-element.110.refs_1_, ...), custom_call_target="tpu_custom_call" | custom-call | flops 15728640 | bytes 65536 | tf_op jit(solution)/shard_map/pallas_call | solution.py:110
  213.2 16.9 %shard_map.313 = (bf16[3,1024,256]{2,1,0:T(8,128)(2,1)}, f32[2,256]{1,0:T(2,128)}, bf16[4,4,128,256]{3,2,1,0:T(8,128)(2,1)}, bf16[4,4,128,256]{3,2,1,0:T(8,128)(2,1)}) custom-call(s32[6]{0:T(128)} %stack.38.refs_0_, bf16[512,1024]{1,0:T(8,128)(2,1)} %get-tuple-element.110.refs_1_, bf16[4,4,128,256]{3,2,1,0:T(8,128)(2,1)} %bitcast.48, ...), custom_call_target="tpu_custom_call" | custom-call | flops 15728640 | bytes 65536 | tf_op jit(solution)/shard_map/pallas_call | solution.py:110
  230.1 3.6 %add_convert_fusion = bf16[4,128,1024]{2,1,0:T(8,128)(2,1)} fusion(bf16[4,128,1024]{2,1,0:T(8,128)(2,1)} %collective-permute-done.38, bf16[4,128,1024]{2,1,0:T(8,128)(2,1)} %collective-permute-done.36, bf16[4,128,1024]{2,1,0:T(8,128)(2,1)} %get-tuple-element.145), kind=kLoop, calls=%fused_computation | loop fusion | flops 3145728 | bytes 4194304 | tf_op jit(solution)/shard_map/convert_element_type | solution.py:653
  238.4 8.9 %shard_map.316 = (bf16[512,1024]{1,0:T(8,128)(2,1)}, bf16[512,1024]{1,0:T(8,128)(2,1)}) custom-call(s32[6]{0:T(128)} %stack.38.refs_0_, bf16[3,1024,256]{2,1,0:T(8,128)(2,1)} %get-tuple-element.113.refs_1_, bf16[4,4,128,256]{3,2,1,0:T(8,128)(2,1)} %bitcast.49, bf16[4,2,128,256]{3,2,1,0:T(8,128)(2,1)} %copy-done.14, bf16[4,2,128,256]{3,2,1,0:T(8,128)(2,1)} %copy-done.3, ...), custom_call_target="tpu_custom_call" | custom-call | flops 6291456 | bytes 65536 | tf_op jit(solution)/shard_map/pallas_call | solution.py:110
  247.5 10.3 %shard_map.314 = (bf16[512,1024]{1,0:T(8,128)(2,1)}, bf16[512,1024]{1,0:T(8,128)(2,1)}) custom-call(s32[6]{0:T(128)} %stack.38.refs_0_, bf16[1024,1024]{1,0:T(8,128)(2,1)} %get-tuple-element.114.refs_1_, bf16[4,1024,128]{2,1,0:T(8,128)(2,1)} %bitcast.56, bf16[4,1024,128]{2,1,0:T(8,128)(2,1)} %copy-done.7, bf16[1024,1024]{1,0:T(8,128)(2,1)} %get-tuple-element.115.refs_4_, ...), custom_call_target="tpu_custom_call" | custom-call | flops 6291456 | bytes 65536 | tf_op jit(solution)/shard_map/pallas_call | solution.py:110
  257.8 1.8 collective-permute-done.23
  260.2 3.1 %add_convert_fusion.4 = bf16[4,4,128,256]{3,2,1,0:T(8,128)(2,1)} fusion(bf16[4,4,128,256]{3,2,1,0:T(8,128)(2,1)} %collective-permute-done.25, bf16[4,4,128,256]{3,2,1,0:T(8,128)(2,1)} %collective-permute-done.23, bf16[4,4,128,256]{3,2,1,0:T(8,128)(2,1)S(1)} %copy-done.20), kind=kLoop, calls=%fused_computation.4 | loop fusion | flops 3145728 | bytes 4194304 | tf_op jit(solution)/shard_map/convert_element_type | solution.py:653
  263.4 2.4 collective-permute-start.33
  265.9 5.8 %shard_map.317 = (f32[512,1024]{1,0:T(8,128)}, f32[2,1024]{1,0:T(2,128)}) custom-call(s32[6]{0:T(128)} %stack.38.refs_0_, bf16[512,1024]{1,0:T(8,128)(2,1)} %get-tuple-element.127.refs_1_, bf16[512,1024]{1,0:T(8,128)(2,1)} %collective-permute-done.27.refs_2_, bf16[512,1024]{1,0:T(8,128)(2,1)} %refs_3_.1, f32[512,1024]{1,0:T(8,128)} %get-tuple-element.129.refs_4_, ...), custom_call_target="tpu_custom_call" | custom-call | flops 4194304 | bytes 65536 | tf_op jit(solution)/shard_map/pallas_call | solution.py:110
  274.4 3.3 %collective-permute-done.29 = f32[7680]{0:T(1024)S(1)} collective-permute-done((f32[7680]{0:T(1024)S(1)}, f32[7680]{0:T(1024)S(1)}, u32[]{:S(2)}, u32[]{:S(2)}) %collective-permute-start.29) | collective-permute-done | bytes 30752 | tf_op jit(solution)/shard_map/ppermute | solution.py:23
  278.7 4.4 %shard_map.315 = bf16[512,1024]{1,0:T(8,128)(2,1)} custom-call(s32[6]{0:T(128)} %stack.38.refs_0_, f32[512,1024]{1,0:T(8,128)} %get-tuple-element.95.refs_3_.refs_1_, bf16[512,1024]{1,0:T(8,128)(2,1)} %get-tuple-element.126.refs_2_, bf16[512,1024]{1,0:T(8,128)(2,1)} %copy-done.22, f32[1,1024]{1,0:T(1,128)} %bitcast.69), custom_call_target="tpu_custom_call" | custom-call | flops 4194304 | bytes 65536 | tf_op jit(solution)/shard_map/pallas_call | solution.py:110
  283.8 1.8 convert_add_fusion
  288.4 2.6 collective-permute-done.34
  291.1 1.8 bitcast_convert_fusion
  292.9 2.2 collective-permute-start.39
  295.1 2.6 collective-permute-done.39
  (195 shorter events, 63.1 us)
Async XLA Ops:
  7.2 33.7 %all-gather.9.cloned.1.call-start = ((), (), s32[]{:S(2)}) async-start(), calls=%async_computation.8 | async-start | bytes 1310720 | tf_op jit(solution)/shard_map/all_gather | solution.py:646
  9.7 73.5 %all-gather.11.cloned.1.call-start = ((), (), s32[]{:S(2)}) async-start(), calls=%async_computation.9 | async-start | bytes 1310720 | tf_op jit(solution)/shard_map/all_gather | solution.py:646
  10.5 113.4 %all-gather.13.cloned.1.call-start = ((), (), s32[]{:S(2)}) async-start(), calls=%async_computation.10 | async-start | bytes 1310720 | tf_op jit(solution)/shard_map/all_gather | solution.py:646
  10.5 14.5 %collective-permute-start = (bf16[1024,128]{1,0:T(8,128)(2,1)}, bf16[1024,128]{1,0:T(8,128)(2,1)S(1)}, u32[]{:S(2)}, u32[]{:S(2)}) collective-permute-start(bf16[1024,128]{1,0:T(8,128)(2,1)} %param.33), channel_id=1, source_target_pairs={{0,6},{2,4},{4,2},{6,0},{1,7},{3,5},{5,3},{7,1},{8,14},{10,12},{12... | collective-permute-start | bytes 786440 | tf_op jit(solution)/shard_map/ppermute | solution.py:27
  24.9 46.4 %collective-permute-start.8 = (bf16[512,1024]{1,0:T(8,128)(2,1)}, bf16[512,1024]{1,0:T(8,128)(2,1)S(1)}, u32[]{:S(2)}, u32[]{:S(2)}) collective-permute-start(bf16[512,1024]{1,0:T(8,128)(2,1)} %get-tuple-element.86.refs_1_.refs_7_), channel_id=1, source_target_pairs={{0,1},{1,0},{2,3},{3,2},{4,5},{5,4},{6,7},{7,6},{8,9},{9,8},{10,11... | collective-permute-start | bytes 3145736 | tf_op jit(solution)/shard_map/ppermute | solution.py:23
  42.1 14.9 %collective-permute-start.5 = (bf16[4,2,128,256]{3,2,1,0:T(8,128)(2,1)S(1)}, bf16[4,2,128,256]{3,2,1,0:T(8,128)(2,1)S(1)}, u32[]{:S(2)}, u32[]{:S(2)}) collective-permute-start(bf16[4,2,128,256]{3,2,1,0:T(8,128)(2,1)S(1)} %get-tuple-element.157), channel_id=1, source_target_pairs={{0,2},{2,0},{1,3},{3,1},{4,6},{6,4},{5,7},{7,5},{8,10},{10,8},{9,1... | collective-permute-start | bytes 1572872 | tf_op jit(solution)/shard_map/ppermute | solution.py:23
  43.7 14.9 %collective-permute-start.4 = (bf16[4,2,128,256]{3,2,1,0:T(8,128)(2,1)S(1)}, bf16[4,2,128,256]{3,2,1,0:T(8,128)(2,1)S(1)}, u32[]{:S(2)}, u32[]{:S(2)}) collective-permute-start(bf16[4,2,128,256]{3,2,1,0:T(8,128)(2,1)S(1)} %get-tuple-element.157), channel_id=1, source_target_pairs={{0,4},{4,0},{1,5},{5,1},{2,6},{6,2},{3,7},{7,3},{8,12},{12,8},{9,1... | collective-permute-start | bytes 1572872 | tf_op jit(solution)/shard_map/ppermute | solution.py:23
  45.1 23.0 %collective-permute-start.3 = (bf16[4,2,128,256]{3,2,1,0:T(8,128)(2,1)S(1)}, bf16[4,2,128,256]{3,2,1,0:T(8,128)(2,1)S(1)}, u32[]{:S(2)}, u32[]{:S(2)}) collective-permute-start(bf16[4,2,128,256]{3,2,1,0:T(8,128)(2,1)S(1)} %get-tuple-element.158), channel_id=1, source_target_pairs={{0,4},{4,0},{1,5},{5,1},{2,6},{6,2},{3,7},{7,3},{8,12},{12,8},{9,1... | collective-permute-start | bytes 1572872 | tf_op jit(solution)/shard_map/ppermute | solution.py:23
  45.7 22.4 %collective-permute-start.2 = (bf16[4,2,128,256]{3,2,1,0:T(8,128)(2,1)S(1)}, bf16[4,2,128,256]{3,2,1,0:T(8,128)(2,1)S(1)}, u32[]{:S(2)}, u32[]{:S(2)}) collective-permute-start(bf16[4,2,128,256]{3,2,1,0:T(8,128)(2,1)S(1)} %get-tuple-element.158), channel_id=1, source_target_pairs={{0,2},{2,0},{1,3},{3,1},{4,6},{6,4},{5,7},{7,5},{8,10},{10,8},{9,1... | collective-permute-start | bytes 1572872 | tf_op jit(solution)/shard_map/ppermute | solution.py:23
  71.0 80.9 %all-gather.15.cloned.1.call-start = ((), (), s32[]{:S(2)}) async-start(), calls=%async_computation.11 | async-start | bytes 1310720 | tf_op jit(solution)/shard_map/all_gather | solution.py:646
  84.7 16.6 %collective-permute-start.12 = (bf16[2,128,1024]{2,1,0:T(8,128)(2,1)S(1)}, bf16[2,128,1024]{2,1,0:T(8,128)(2,1)}, u32[]{:S(2)}, u32[]{:S(2)}) collective-permute-start(bf16[2,128,1024]{2,1,0:T(8,128)(2,1)S(1)} %get-tuple-element.155), channel_id=1, source_target_pairs={{0,4},{4,0},{1,5},{5,1},{2,6},{6,2},{3,7},{7,3},{8,12},{12,8},{9,1... | collective-permute-start | bytes 1572872 | tf_op jit(solution)/shard_map/ppermute | solution.py:23
  85.3 16.0 %collective-permute-start.10 = (bf16[2,128,1024]{2,1,0:T(8,128)(2,1)S(1)}, bf16[2,128,1024]{2,1,0:T(8,128)(2,1)S(1)}, u32[]{:S(2)}, u32[]{:S(2)}) collective-permute-start(bf16[2,128,1024]{2,1,0:T(8,128)(2,1)S(1)} %get-tuple-element.155), channel_id=1, source_target_pairs={{0,2},{2,0},{1,3},{3,1},{4,6},{6,4},{5,7},{7,5},{8,10},{10,8},{9,1... | collective-permute-start | bytes 1572872 | tf_op jit(solution)/shard_map/ppermute | solution.py:23
  86.8 21.1 %collective-permute-start.11 = (bf16[2,128,1024]{2,1,0:T(8,128)(2,1)S(1)}, bf16[2,128,1024]{2,1,0:T(8,128)(2,1)S(1)}, u32[]{:S(2)}, u32[]{:S(2)}) collective-permute-start(bf16[2,128,1024]{2,1,0:T(8,128)(2,1)S(1)} %get-tuple-element.156), channel_id=1, source_target_pairs={{0,4},{4,0},{1,5},{5,1},{2,6},{6,2},{3,7},{7,3},{8,12},{12,8},{9,1... | collective-permute-start | bytes 1572872 | tf_op jit(solution)/shard_map/ppermute | solution.py:23
  88.3 19.9 %collective-permute-start.9 = (bf16[2,128,1024]{2,1,0:T(8,128)(2,1)S(1)}, bf16[2,128,1024]{2,1,0:T(8,128)(2,1)S(1)}, u32[]{:S(2)}, u32[]{:S(2)}) collective-permute-start(bf16[2,128,1024]{2,1,0:T(8,128)(2,1)S(1)} %get-tuple-element.156), channel_id=1, source_target_pairs={{0,2},{2,0},{1,3},{3,1},{4,6},{6,4},{5,7},{7,5},{8,10},{10,8},{9,1... | collective-permute-start | bytes 1572872 | tf_op jit(solution)/shard_map/ppermute | solution.py:23
  111.1 152.3 %reduce-scatter.7.cloned.1.call-start = ((), (), s32[]{:S(2)}) async-start(), calls=%async_computation.5 | async-start | bytes 1310720 | tf_op jit(solution)/shard_map/reduce_scatter | solution.py:785
  111.2 15.1 %collective-permute-start.17 = (bf16[512,1024]{1,0:T(8,128)(2,1)}, bf16[512,1024]{1,0:T(8,128)(2,1)S(1)}, u32[]{:S(2)}, u32[]{:S(2)}) collective-permute-start(bf16[512,1024]{1,0:T(8,128)(2,1)} %get-tuple-element.98.refs_7_.refs_1_), channel_id=1, source_target_pairs={{0,1},{1,0},{2,3},{3,2},{4,5},{5,4},{6,7},{7,6},{8,9},{9,8},{10,11... | collective-permute-start | bytes 3145736 | tf_op jit(solution)/shard_map/ppermute | solution.py:23
  123.9 25.8 %collective-permute-start.19 = (bf16[4,1024,128]{2,1,0:T(8,128)(2,1)}, bf16[4,1024,128]{2,1,0:T(8,128)(2,1)S(1)}, u32[]{:S(2)}, u32[]{:S(2)}) collective-permute-start(bf16[4,1024,128]{2,1,0:T(8,128)(2,1)} %bitcast.53), channel_id=1, source_target_pairs={{0,2},{2,0},{1,3},{3,1},{4,6},{6,4},{5,7},{7,5},{8,10},{10,8},{9,1... | collective-permute-start | bytes 3145736 | tf_op jit(solution)/shard_map/ppermute | solution.py:23
  125.4 25.5 %collective-permute-start.18 = (bf16[4,1024,128]{2,1,0:T(8,128)(2,1)}, bf16[4,1024,128]{2,1,0:T(8,128)(2,1)S(1)}, u32[]{:S(2)}, u32[]{:S(2)}) collective-permute-start(bf16[4,1024,128]{2,1,0:T(8,128)(2,1)} %bitcast.54), channel_id=1, source_target_pairs={{0,4},{4,0},{1,5},{5,1},{2,6},{6,2},{3,7},{7,3},{8,12},{12,8},{9,1... | collective-permute-start | bytes 3145736 | tf_op jit(solution)/shard_map/ppermute | solution.py:23
  145.2 138.6 %reduce-scatter.5.cloned.1.call-start = ((), (), s32[]{:S(2)}) async-start(), calls=%async_computation.4 | async-start | bytes 1310720 | tf_op jit(solution)/shard_map/reduce_scatter | solution.py:789
  150.9 24.8 %collective-permute-start.32 = (bf16[4,1024,128]{2,1,0:T(8,128)(2,1)}, bf16[4,1024,128]{2,1,0:T(8,128)(2,1)}, u32[]{:S(2)}, u32[]{:S(2)}) collective-permute-start(bf16[4,1024,128]{2,1,0:T(8,128)(2,1)} %get-tuple-element.142), channel_id=1, source_target_pairs={{0,2},{2,0},{1,3},{3,1},{4,6},{6,4},{5,7},{7,5},{8,10},{10,8},{9,1... | collective-permute-start | bytes 3145736 | tf_op jit(solution)/shard_map/ppermute | solution.py:23
  151.4 24.6 %collective-permute-start.31 = (bf16[4,1024,128]{2,1,0:T(8,128)(2,1)}, bf16[4,1024,128]{2,1,0:T(8,128)(2,1)}, u32[]{:S(2)}, u32[]{:S(2)}) collective-permute-start(bf16[4,1024,128]{2,1,0:T(8,128)(2,1)} %get-tuple-element.140), channel_id=1, source_target_pairs={{0,4},{4,0},{1,5},{5,1},{2,6},{6,2},{3,7},{7,3},{8,12},{12,8},{9,1... | collective-permute-start | bytes 3145736 | tf_op jit(solution)/shard_map/ppermute | solution.py:23
  172.6 14.7 %collective-permute-start.37 = (bf16[2,128,1024]{2,1,0:T(8,128)(2,1)}, bf16[2,128,1024]{2,1,0:T(8,128)(2,1)}, u32[]{:S(2)}, u32[]{:S(2)}) collective-permute-start(bf16[2,128,1024]{2,1,0:T(8,128)(2,1)} %get-tuple-element.151), channel_id=1, source_target_pairs={{0,2},{2,0},{1,3},{3,1},{4,6},{6,4},{5,7},{7,5},{8,10},{10,8},{9,1... | collective-permute-start | bytes 1572872 | tf_op jit(solution)/shard_map/ppermute | solution.py:23
  179.0 112.1 %reduce-scatter.9.cloned.1.call-start = ((), (), s32[]{:S(2)}) async-start(), calls=%async_computation.6 | async-start | bytes 1310720 | tf_op jit(solution)/shard_map/reduce_scatter | solution.py:663
  190.5 39.6 %collective-permute-start.38 = (bf16[4,128,1024]{2,1,0:T(8,128)(2,1)S(1)}, bf16[4,128,1024]{2,1,0:T(8,128)(2,1)}, u32[]{:S(2)}, u32[]{:S(2)}) collective-permute-start(bf16[4,128,1024]{2,1,0:T(8,128)(2,1)S(1)} %add_convert_fusion.1), channel_id=1, source_target_pairs={{0,4},{4,0},{1,5},{5,1},{2,6},{6,2},{3,7},{7,3},{8,12},{12,8},{9,1... | collective-permute-start | bytes 3145736 | tf_op jit(solution)/shard_map/ppermute | solution.py:23
  192.4 37.8 %collective-permute-start.36 = (bf16[4,128,1024]{2,1,0:T(8,128)(2,1)S(1)}, bf16[4,128,1024]{2,1,0:T(8,128)(2,1)}, u32[]{:S(2)}, u32[]{:S(2)}) collective-permute-start(bf16[4,128,1024]{2,1,0:T(8,128)(2,1)S(1)} %add_convert_fusion.2), channel_id=1, source_target_pairs={{0,2},{2,0},{1,3},{3,1},{4,6},{6,4},{5,7},{7,5},{8,10},{10,8},{9,1... | collective-permute-start | bytes 3145736 | tf_op jit(solution)/shard_map/ppermute | solution.py:23
  211.2 22.8 %collective-permute-start.22 = (bf16[2,4,128,256]{3,2,1,0:T(8,128)(2,1)}, bf16[2,4,128,256]{3,2,1,0:T(8,128)(2,1)}, u32[]{:S(2)}, u32[]{:S(2)}) collective-permute-start(bf16[2,4,128,256]{3,2,1,0:T(8,128)(2,1)} %get-tuple-element.119), channel_id=1, source_target_pairs={{0,4},{4,0},{1,5},{5,1},{2,6},{6,2},{3,7},{7,3},{8,12},{12,8},{9,1... | collective-permute-start | bytes 1572872 | tf_op jit(solution)/shard_map/ppermute | solution.py:23
  211.8 22.2 %collective-permute-start.24 = (bf16[2,4,128,256]{3,2,1,0:T(8,128)(2,1)}, bf16[2,4,128,256]{3,2,1,0:T(8,128)(2,1)S(1)}, u32[]{:S(2)}, u32[]{:S(2)}) collective-permute-start(bf16[2,4,128,256]{3,2,1,0:T(8,128)(2,1)} %get-tuple-element.124), channel_id=1, source_target_pairs={{0,2},{2,0},{1,3},{3,1},{4,6},{6,4},{5,7},{7,5},{8,10},{10,8},{9,1... | collective-permute-start | bytes 1572872 | tf_op jit(solution)/shard_map/ppermute | solution.py:23
  233.7 65.2 %reduce-scatter.11.cloned.1.call-start = ((), (), s32[]{:S(2)}) async-start(), calls=%async_computation.7 | async-start | bytes 1310720 | tf_op jit(solution)/shard_map/reduce_scatter | solution.py:828
  236.1 23.6 %collective-permute-start.23 = (bf16[4,4,128,256]{3,2,1,0:T(8,128)(2,1)S(1)}, bf16[4,4,128,256]{3,2,1,0:T(8,128)(2,1)}, u32[]{:S(2)}, u32[]{:S(2)}) collective-permute-start(bf16[4,4,128,256]{3,2,1,0:T(8,128)(2,1)S(1)} %add_convert_fusion.6), channel_id=1, source_target_pairs={{0,2},{2,0},{1,3},{3,1},{4,6},{6,4},{5,7},{7,5},{8,10},{10,8},{9,1... | collective-permute-start | bytes 3145736 | tf_op jit(solution)/shard_map/ppermute | solution.py:23
  236.9 23.3 %collective-permute-start.25 = (bf16[4,4,128,256]{3,2,1,0:T(8,128)(2,1)S(1)}, bf16[4,4,128,256]{3,2,1,0:T(8,128)(2,1)}, u32[]{:S(2)}, u32[]{:S(2)}) collective-permute-start(bf16[4,4,128,256]{3,2,1,0:T(8,128)(2,1)S(1)} %add_convert_fusion.5), channel_id=1, source_target_pairs={{0,4},{4,0},{1,5},{5,1},{2,6},{6,2},{3,7},{7,3},{8,12},{12,8},{9,1... | collective-permute-start | bytes 3145736 | tf_op jit(solution)/shard_map/ppermute | solution.py:23
  247.4 18.5 %collective-permute-start.27 = (bf16[512,1024]{1,0:T(8,128)(2,1)}, bf16[512,1024]{1,0:T(8,128)(2,1)}, u32[]{:S(2)}, u32[]{:S(2)}) collective-permute-start(bf16[512,1024]{1,0:T(8,128)(2,1)} %get-tuple-element.128), channel_id=1, source_target_pairs={{0,1},{1,0},{2,3},{3,2},{4,5},{5,4},{6,7},{7,6},{8,9},{9,8},{10,11... | collective-permute-start | bytes 3145736 | tf_op jit(solution)/shard_map/ppermute | solution.py:23
  263.4 20.3 %collective-permute-start.33 = (bf16[1024,128]{1,0:T(8,128)(2,1)}, bf16[1024,128]{1,0:T(8,128)(2,1)S(1)}, u32[]{:S(2)}, u32[]{:S(2)}) collective-permute-start(bf16[1024,128]{1,0:T(8,128)(2,1)} %bitcast.76), channel_id=1, source_target_pairs={{0,6},{2,4},{4,2},{6,0},{1,7},{3,5},{5,3},{7,1},{8,14},{10,12},{12... | collective-permute-start | bytes 786440 | tf_op jit(solution)/shard_map/ppermute | solution.py:27
  (53 other events, 534.9 us)
Sparse Core Ops, SparseCore 0:
  10.2 30.6 all-gather.8
  42.4 27.3 all-gather.10
  71.4 27.4 all-gather.12
  111.2 26.2 all-gather.14
  145.3 26.0 reduce-scatter.6
  179.1 26.2 reduce-scatter.4
  233.8 26.4 reduce-scatter.8
  263.4 27.2 reduce-scatter.10
